TPU v7x, 512 devices: a whole 4x8x8 slice. The times are simulated.
512 devices in a mesh: mer: 128 (over z, y, core), az: 4 (over x).
Axes of the slice: x: 4, y: 8, z: 8, core: 2. Of those that a mesh axis runs over, the one named last changes fastest.
Arguments:
- displacement: float32 [3, 5, 1024, 512], P(None, None, 'mer', 'az'), may hold values from -6 to 6
- velocity: float32 [3, 5, 1024, 512], P(None, None, 'mer', 'az'), may hold values from -1.5 to 1.5
- modulus: float32 [1, 256], P(None, 'mer'), may hold values from 0.5 to 2
- hoop_strength: float32 [1, 256], P(None, 'mer'), may hold values from 0.5 to 2
- coupling: float32 [1, 256], P(None, 'mer'), may hold values from -1 to 1
- density: float32 [1, 256], P(None, 'mer'), may hold values from 0.5 to 2
- order_count: int32 [1, 256], P(None, 'mer'), may hold values from 1 to 256
- point_element: int32 [8192, 2], P('mer'), may hold values from 0 to 255, as said below
- point_local: float32 [8192, 2], P('mer'), may hold values from -1 to 1
- azimuth_scale: float32 [8192], P('mer'), may hold values from 0.5 to 2
- point_owner: int32 [8192, 1], P('mer'), may hold values from 0 to 127; in each aligned block of 64 rows (0 to 63, 64 to 127, ...) at most 2 rows name the same one
- point_cell: int32 [8192], P('mer'), may hold values from 0 to 31
- adjoint_strain: float32 [9, 8, 512, 512], P(None, None, 'mer', 'az'), may hold values from -6 to 6
Outputs:
- final_displacement: float32 [3, 5, 1024, 512], P(None, None, 'mer', 'az')
- kernel: float32 [8, 512, 512], P(None, 'mer', 'az')
Inputs may be any that keep to these rules, and one draw needn't show every extreme that they name: `point_element`: points p with p // 64 = i lie in colatitude elements i * 2 to (i + 1) * 2 - 1; the first column is below 1. `point_owner`: among the points of one device (aligned blocks of 64 points) no owner is named more than 2 times, a bound that some block reaches.
All inputs are finite; a program needn't handle non-finite values.
Results may differ from a plain program's by a relative error of at most 0.0003.
Values sent between devices are 32-bit elements; how exact they have to be, the bound alone decides.
No kernel may reach another device: no remote copies, remote signals or barrier semaphores. Data moves between devices by JAX's collectives and lax.ppermute only.
A program may use at most 64 MiB of HBM per device.

v0:
```python
import math

import jax
import jax.numpy as jnp
import numpy as np
from jax import lax
from jax.sharding import Mesh
from jax.sharding import PartitionSpec as P

ORDERS = 256
STEPS = 3
MER = ("mer_0", "mer_1", "mer_2")


step_scale = 0.015
smooth_rate = 0.125


def from_behind(value, axis, steps):
    count = lax.axis_size(axis)
    first, last = (max(0, -steps), min(count, count - steps))
    return lax.ppermute(value, axis, [(source, source + steps) for source in range(first, last)])


def split_up(array, dim, size):
    before, after = (array.shape[:dim], array.shape[dim + 1 :])
    return jnp.moveaxis(array.reshape(*before, size, -1, *after), dim, 0)


def joined_along(blocks, dim):
    blocks = jnp.moveaxis(blocks, 0, dim)
    shape = blocks.shape
    return blocks.reshape(*shape[:dim], shape[dim] * shape[dim + 1], *shape[dim + 2 :])


def moved_by_axis(blocks, axes, turns):
    inside = blocks.shape[1:]
    result = blocks.reshape(*(lax.axis_size(a) for a in axes), *inside)
    for k in turns:
        result = lax.all_to_all(result, axes[k], k, k, tiled=True)
    return result.reshape(-1, *inside)


def exchange_by_chip(array, groups, turns, split_dim, concat_dim):
    size = lax.axis_size(groups[0]) * lax.axis_size(groups[1])
    blocks = split_up(array, split_dim, size)
    return joined_along(moved_by_axis(blocks, groups, turns), concat_dim)


def summed_on_arrival(array, axis, dim):
    blocks = split_up(array, dim, lax.axis_size(axis))
    arrived = lax.all_to_all(blocks, axis, split_axis=0, concat_axis=0, tiled=True)
    return arrived.sum(axis=0)


def with_halo(array, sides, width):
    edges = {}
    for axis, dim in sides:
        size, length = (lax.axis_size(axis), array.shape[dim])
        up = [(i, (i + 1) % size) for i in range(size)]
        last = lax.slice_in_dim(array, length - width, length, axis=dim)
        first = lax.slice_in_dim(array, 0, width, axis=dim)
        edges[dim] = (
            lax.ppermute(last, axis, up),
            lax.ppermute(first, axis, [(b, a) for a, b in up]),
        )
    done = []
    for _, dim in sides:
        low, high = edges[dim]
        around = [(width, width) if d in done else (0, 0) for d in range(array.ndim)]
        array = jnp.concatenate([jnp.pad(low, around), array, jnp.pad(high, around)], axis=dim)
        done.append(dim)
    return array


def gll_tables():
    gll_nodes = np.array([-1.0, -math.sqrt(3.0 / 7.0), 0.0, math.sqrt(3.0 / 7.0), 1.0])
    gll_weights = np.array([0.1, 49.0 / 90.0, 32.0 / 45.0, 49.0 / 90.0, 0.1])
    derivative = np.zeros((5, 5))
    for i in range(5):
        for j in range(5):
            if i == j:
                derivative[i, j] = sum(
                    (1.0 / (gll_nodes[i] - gll_nodes[l]) for l in range(5) if l != i)
                )
            else:
                scale_i = np.prod([gll_nodes[i] - gll_nodes[l] for l in range(5) if l != i])
                scale_j = np.prod([gll_nodes[j] - gll_nodes[l] for l in range(5) if l != j])
                derivative[i, j] = scale_i / (scale_j * (gll_nodes[i] - gll_nodes[j]))
    return (gll_nodes, gll_weights, derivative)


def lagrange(position):
    gll_nodes = gll_tables()[0]
    basis_values = []
    basis_slopes = []
    for j in range(5):
        others = [l for l in range(5) if l != j]
        product = jnp.ones_like(position)
        for l in others:
            product = (
                product * (position - float(gll_nodes[l])) / float(gll_nodes[j] - gll_nodes[l])
            )
        gradient_sum = jnp.zeros_like(position)
        for l in others:
            summand = jnp.ones_like(position) / float(gll_nodes[j] - gll_nodes[l])
            for i in others:
                if i != l:
                    summand = (
                        summand
                        * (position - float(gll_nodes[i]))
                        / float(gll_nodes[j] - gll_nodes[i])
                    )
            gradient_sum = gradient_sum + summand
        basis_values.append(product)
        basis_slopes.append(gradient_sum)
    return (jnp.stack(basis_values, axis=1), jnp.stack(basis_slopes, axis=1))


def to_elements(nodal):
    count_rows = (nodal.shape[1] - 1) // 4
    count_cols = (nodal.shape[2] - 1) // 4
    radial = jnp.stack([nodal[:, a : a + 4 * count_rows : 4] for a in range(5)], axis=2)
    return jnp.stack([radial[:, :, :, b : b + 4 * count_cols : 4] for b in range(5)], axis=4)


def from_elements(element_values):
    components, count_rows, _, count_cols, _, coef_width = element_values.shape
    radial = jnp.zeros(
        (components, 4 * count_rows + 1, count_cols, 5, coef_width), element_values.dtype
    )
    for a in range(5):
        radial = radial.at[:, a : a + 4 * count_rows : 4].add(element_values[:, :, a])
    assembled = jnp.zeros(
        (components, 4 * count_rows + 1, 4 * count_cols + 1, coef_width), element_values.dtype
    )
    for b in range(5):
        assembled = assembled.at[:, :, b : b + 4 * count_cols : 4].add(radial[:, :, :, b])
    return assembled


def quadrature_table():
    gll_weights = jnp.asarray(gll_tables()[1], jnp.float32)
    return gll_weights[:, None] * gll_weights[None, :]


def rotate(vector, order_ratio):
    lane_index = lax.broadcasted_iota(jnp.int32, vector.shape, vector.ndim - 1)
    is_even = lane_index % 2 == 0
    return (
        jnp.where(is_even, jnp.roll(vector, -1, axis=-1), -jnp.roll(vector, 1, axis=-1))
        * order_ratio
    )


def element_mass(density):
    quadrature = quadrature_table()
    return (density[:, None, :, None] * quadrature[None, :, None, :])[None, :, :, :, :, None]


def element_forces(
    element_values, modulus, hoop_strength, coupling, order_count, order_index, order_ratio
):
    quadrature = quadrature_table()
    derivative = jnp.asarray(gll_tables()[2], jnp.float32)
    highest = lax.Precision.HIGHEST

    def spread(per_element):
        return (per_element[:, None, :, None] * quadrature[None, :, None, :])[:, :, :, :, None]

    stiff_node = spread(modulus)[None]
    hoop_node = spread(hoop_strength)[None]
    couple_node = spread(coupling)
    grad_radial = jnp.einsum("pa,cEaFbk->cEpFbk", derivative, element_values, precision=highest)
    grad_colat = jnp.einsum("qb,cEaFbk->cEaFqk", derivative, element_values, precision=highest)
    back_radial = jnp.einsum(
        "pa,cEpFbk->cEaFbk", derivative, stiff_node * grad_radial, precision=highest
    )
    back_colat = jnp.einsum(
        "qb,cEaFqk->cEaFbk", derivative, stiff_node * grad_colat, precision=highest
    )
    forces = -(back_radial + back_colat + hoop_node * (order_ratio * order_ratio) * element_values)
    forces = jnp.stack(
        [
            forces[0] + couple_node * rotate(element_values[2], order_ratio),
            forces[1],
            forces[2] - couple_node * rotate(element_values[0], order_ratio),
        ],
        axis=0,
    )
    order_mask = order_index[None, None, None, None, :] < order_count[:, None, :, None, None]
    return jnp.where(order_mask[None], forces, 0.0)


def point_gradients(
    gathered, xi_values, xi_slopes, eta_values, eta_slopes, azimuth_scale, order_ratio
):
    highest = lax.Precision.HIGHEST
    nodal_value = jnp.einsum("pa,pb,cpabk->pck", xi_values, eta_values, gathered, precision=highest)
    along_radius = jnp.einsum(
        "pa,pb,cpabk->pck", xi_slopes, eta_values, gathered, precision=highest
    )
    along_colat = jnp.einsum("pa,pb,cpabk->pck", xi_values, eta_slopes, gathered, precision=highest)
    around_axis = azimuth_scale[:, None, None] * rotate(nodal_value, order_ratio)
    stacked = jnp.stack([along_radius, along_colat, around_axis], axis=2)
    return stacked.reshape(gathered.shape[1], 9, gathered.shape[4])


def fourier_basis(coef_start, coef_count, phi_count, total_phi):
    coef_rows = coef_start + lax.broadcasted_iota(jnp.int32, (coef_count, phi_count), 0)
    phi_cols = lax.broadcasted_iota(jnp.int32, (coef_count, phi_count), 1)
    wrapped = coef_rows // 2 * phi_cols % total_phi
    angles = wrapped.astype(jnp.float32) * (2.0 * math.pi / total_phi)
    return jnp.where(coef_rows % 2 == 0, jnp.cos(angles), jnp.sin(angles))


def on_device(
    displacement,
    velocity,
    modulus,
    hoop_strength,
    coupling,
    density,
    order_count,
    point_element,
    point_local,
    azimuth_scale,
    point_owner,
    point_cell,
    adjoint_strain,
):
    highest = lax.Precision.HIGHEST
    coef_width = displacement.shape[3]
    local_cols = displacement.shape[2]
    elem_cols = modulus.shape[1]
    coef_first = lax.axis_index("az") * coef_width
    order_index = (coef_first + jnp.arange(coef_width, dtype=jnp.int32)) // 2
    order_ratio = order_index.astype(jnp.float32) / ORDERS
    mass_parts = from_elements(element_mass(density))
    mass_edge = from_behind(mass_parts[:, :, local_cols:], MER, 1)
    nodal_mass = mass_parts[:, :, :local_cols].at[:, :, 0:1].add(mass_edge)[0]

    def right_rim(nodal):
        return from_behind(nodal[:, :, 0:1], MER, -1)

    current = displacement
    previous = displacement - velocity
    for step_index in range(STEPS):
        padded = jnp.concatenate([current, right_rim(current)], axis=2)
        assembled = from_elements(
            element_forces(
                to_elements(padded),
                modulus,
                hoop_strength,
                coupling,
                order_count,
                order_index,
                order_ratio,
            )
        )
        incoming = from_behind(assembled[:, :, local_cols:], MER, 1)
        forces = assembled[:, :, :local_cols].at[:, :, 0:1].add(incoming)
        following = 2.0 * current - previous + step_scale * forces / nodal_mass
        previous, current = (current, following)
    padded = jnp.concatenate([current, right_rim(current)], axis=2)
    xi_values, xi_slopes = lagrange(point_local[:, 0])
    eta_values, eta_slopes = lagrange(point_local[:, 1])
    offsets = jnp.arange(5, dtype=jnp.int32)[None, :]
    row_index = 4 * point_element[:, 0:1] + offsets
    col_index = 4 * (point_element[:, 1:2] % elem_cols) + offsets
    gathered = padded[:, row_index[:, :, None], col_index[:, None, :], :]
    gradients = point_gradients(
        gathered, xi_values, xi_slopes, eta_values, eta_slopes, azimuth_scale, order_ratio
    )
    point_count = gradients.shape[0]
    mer_count = lax.axis_size(MER)
    capacity = max(2, (2 * point_count + mer_count - 1) // mer_count)
    slot_total = mer_count * capacity
    owners = point_owner[:, 0]
    point_iota = jnp.arange(point_count, dtype=jnp.int32)
    earlier = (owners[None, :] == owners[:, None]) & (point_iota[None, :] < point_iota[:, None])
    slot_index = owners * capacity + jnp.sum(earlier.astype(jnp.int32), axis=1)
    placing = (slot_index[None, :] == jnp.arange(slot_total, dtype=jnp.int32)[:, None]).astype(
        jnp.float32
    )
    cell_code = jnp.dot(placing, (point_cell + 1).astype(jnp.float32), precision=highest) - 1.0
    outgoing = jnp.einsum("sp,pgk->sgk", placing, gradients, precision=highest)
    layer_count = adjoint_strain.shape[1]
    row_count_lat = adjoint_strain.shape[2]
    phi_width = adjoint_strain.shape[3]
    cell_total = layer_count * row_count_lat
    total_phi = 2 * ORDERS
    fourier_norm = 1.0 / math.sqrt(ORDERS)
    adjoint_cells = adjoint_strain.reshape(9, cell_total, phi_width)
    cell_iota = jnp.arange(cell_total, dtype=jnp.float32)
    arriving, arriving_cells = (
        exchange_by_chip(outgoing, (("mer_0", "mer_1"), "mer_2"), (1, 0), 0, 0),
        exchange_by_chip(cell_code, (("mer_0", "mer_1"), "mer_2"), (1, 0), 0, 0),
    )
    sorting = (arriving_cells[None, :] == cell_iota[:, None]).astype(jnp.float32)
    voxel_coefs = jnp.einsum("cs,sgk->cgk", sorting, arriving, precision=highest)
    basis = fourier_basis(coef_first, coef_width, phi_width * lax.axis_size("az"), total_phi)
    samples = (
        summed_on_arrival(jnp.einsum("kj,cgk->jgc", basis, voxel_coefs, precision=highest), "az", 0)
        * fourier_norm
    )
    kernel_raw = jnp.einsum("jgc,gcj->cj", samples, adjoint_cells, precision=highest)
    kernel_block = kernel_raw.reshape(layer_count, row_count_lat, phi_width)
    framed = with_halo(kernel_block, ((MER, 1), ("az", 2)), 1)
    mer_index = lax.axis_index(MER)
    lower_keep = (mer_index > 0).astype(jnp.float32)
    upper_keep = (mer_index < mer_count - 1).astype(jnp.float32)
    lateral = jnp.concatenate(
        [framed[:, 0:1, 1:-1] * lower_keep, kernel_block, framed[:, -1:, 1:-1] * upper_keep], axis=1
    )
    neighbours = lateral[:, :-2] + lateral[:, 2:]
    neighbours = neighbours + framed[:, 1:-1, :-2] + framed[:, 1:-1, 2:]
    deeper = jnp.pad(kernel_block, ((1, 1), (0, 0), (0, 0)))
    neighbours = neighbours + deeper[2:] + deeper[:-2]
    kernel = kernel_block + smooth_rate * (neighbours - 6.0 * kernel_block)
    return (current, kernel)


def solution(mesh):
    torus = Mesh(mesh.devices.reshape(8, 8, 2, mesh.shape["az"]), ("mer_0", "mer_1", "mer_2", "az"))
    return jax.shard_map(
        on_device,
        mesh=torus,
        in_specs=(
            P(None, None, MER, "az"),
            P(None, None, MER, "az"),
            P(None, MER),
            P(None, MER),
            P(None, MER),
            P(None, MER),
            P(None, MER),
            P(MER, None),
            P(MER, None),
            P(MER),
            P(MER, None),
            P(MER),
            P(None, None, MER, "az"),
        ),
        out_specs=(P(None, None, MER, "az"), P(None, MER, "az")),
        check_vma=False,
    )
```

profile of v0, /device:TPU:1, one launch (start us, length us, event | category | flops | bytes accessed | tf_op | source)
XLA Modules:
  0.0 200.4 jit_solution(8474695924827684429)
XLA Ops:
  0.6 0.8 slice.1341
  1.5 8.7 %collective-permute-start = (f32[3,5,1,128]{3,1,2,0:T(8,128)S(1)}, f32[3,5,1,128]{3,1,2,0:T(8,128)S(1)}, u32[]{:S(2)}, u32[]{:S(2)}) collective-permute-start(f32[3,5,1,128]{3,1,2,0:T(8,128)S(1)} %copy.767), channel_id=1, source_target_pairs={{4,0},{8,4},{12,8},{16,12},{20,16},{24,20},{28,24},{32,28},{36,32}... | collective-permute-start | bytes 23048 | tf_op jit(solution)/shard_map/ppermute | solution.py:22
  10.3 0.8 broadcast_multiply_fusion.7
  11.1 0.7 broadcast_multiply_fusion.4
  15.7 1.9 collective-permute-start.2
  17.6 0.9 convert_reduce_fusion
  18.5 0.7 multiply_add_fusion.3
  19.2 0.8 fusion.50
  20.9 3.7 %all-to-all-start = ((f32[2,1,128]{2,1,0:T(1,128)}), f32[2,1,128]{2,1,0:T(1,128)S(1)}, u32[]{:S(2)}, u32[]{:S(2)}) async-start(f32[2,1,128]{2,1,0:T(1,128)} %reshape.2540), calls=%async_computation | async-start | bytes 2048 | tf_op jit(solution)/shard_map/all_to_all | solution.py:40
  24.7 0.8 constant_dynamic-update-slice_fusion.1
  25.6 0.8 multiply_add_fusion.1
  26.4 0.7 fusion.148
  27.1 0.8 broadcast_multiply_fusion.1
  28.0 0.7 broadcast_compare_fusion
  36.5 1.9 collective-permute-start.1
  38.7 0.9 collective-permute-done.1
  39.7 2.1 %collective-permute-start.3 = (f32[3,5,1,128]{3,1,2,0:T(8,128)S(1)}, f32[3,5,1,128]{3,1,2,0:T(8,128)S(1)}, u32[]{:S(2)}, u32[]{:S(2)}) collective-permute-start(f32[3,5,1,128]{3,1,2,0:T(8,128)S(1)} %slice.1389), channel_id=1, source_target_pairs={{4,0},{8,4},{12,8},{16,12},{20,16},{24,20},{28,24},{32,28},{36,32}... | collective-permute-start | bytes 23048 | tf_op jit(solution)/shard_map/ppermute | solution.py:22
  42.0 2.9 %collective-permute-done.3 = f32[3,5,1,128]{3,1,2,0:T(8,128)S(1)} collective-permute-done((f32[3,5,1,128]{3,1,2,0:T(8,128)S(1)}, f32[3,5,1,128]{3,1,2,0:T(8,128)S(1)}, u32[]{:S(2)}, u32[]{:S(2)}) %collective-permute-start.3) | collective-permute-done | bytes 7712 | tf_op jit(solution)/shard_map/ppermute | solution.py:22
  52.2 1.9 collective-permute-start.4
  54.3 1.0 collective-permute-done.4
  55.4 2.1 %collective-permute-start.5 = (f32[3,5,1,128]{3,1,2,0:T(8,128)S(1)}, f32[3,5,1,128]{3,1,2,0:T(8,128)S(1)}, u32[]{:S(2)}, u32[]{:S(2)}) collective-permute-start(f32[3,5,1,128]{3,1,2,0:T(8,128)S(1)} %slice.1419), channel_id=1, source_target_pairs={{4,0},{8,4},{12,8},{16,12},{20,16},{24,20},{28,24},{32,28},{36,32}... | collective-permute-start | bytes 23048 | tf_op jit(solution)/shard_map/ppermute | solution.py:22
  57.6 3.1 %collective-permute-done.5 = f32[3,5,1,128]{3,1,2,0:T(8,128)S(1)} collective-permute-done((f32[3,5,1,128]{3,1,2,0:T(8,128)S(1)}, f32[3,5,1,128]{3,1,2,0:T(8,128)S(1)}, u32[]{:S(2)}, u32[]{:S(2)}) %collective-permute-start.5) | collective-permute-done | bytes 7712 | tf_op jit(solution)/shard_map/ppermute | solution.py:22
  68.0 1.9 collective-permute-start.6
  70.1 0.9 collective-permute-done.6
  71.1 2.3 %collective-permute-start.7 = (f32[3,5,1,128]{3,1,2,0:T(8,128)S(1)}, f32[3,5,1,128]{3,1,2,0:T(8,128)S(1)}, u32[]{:S(2)}, u32[]{:S(2)}) collective-permute-start(f32[3,5,1,128]{3,1,2,0:T(8,128)S(1)} %slice.1449), channel_id=1, source_target_pairs={{4,0},{8,4},{12,8},{16,12},{20,16},{24,20},{28,24},{32,28},{36,32}... | collective-permute-start | bytes 23048 | tf_op jit(solution)/shard_map/ppermute | solution.py:22
  73.6 1.2 copy.719
  74.8 1.2 copy.720
  76.0 1.2 copy.721
  78.4 0.7 copy.629
  79.2 10.8 %gather_fusion = f32[1600,3,128]{2,1,0:T(4,128)S(1)} fusion(f32[3,5,9,128]{3,0,2,1:T(4,128)S(1)} %copy.630, s32[1600]{0:T(1024)S(1)} %reshape.2323), kind=kCustom, calls=%fused_computation | custom fusion | bytes 4928000 | tf_op jit(solution)/shard_map/gather | solution.py:271
  90.1 4.4 %fusion = (f32[64,3,128]{2,0,1:T(8,128)}, f32[64,3,128]{2,0,1:T(8,128)}, f32[64,3,128]{2,0,1:T(8,128)S(1)}) fusion(f32[64,5,5,3,128]{4,3,2,1,0:T(4,128)S(1)} %bitcast.561, f32[64,5,5]{2,1,0:T(8,128)} %copy.719, f32[64,5,5]{2,1,0:T(8,128)} %copy.720, f32[64,5,5]{2,1,0:T(8,128)} %copy.721), kind=kLoop, calls=%fused_computation.24 | loop fusion | flops 3612672 | bytes 2771712
  96.0 0.7 fusion.47
  96.7 4.3 %all_to_all.25 = f32[64,2,2,9,128]{4,0,3,2,1:T(8,128)S(1)} all-to-all(f32[64,2,2,9,128]{4,0,3,2,1:T(8,128)S(1)} %fusion.47), channel_id=1, replica_groups=mesh['mer_0'=8,'mer_1'=8,'mer_2'=2,'az'=4] {'mer_2'}, dimensions={1} | all-to-all | bytes 2359296 | tf_op jit(solution)/shard_map/all_to_all | solution.py:40
  101.0 19.0 %all-to-all-start.1 = ((f32[64,2,2]{2,1,0:T(2,128)}), f32[64,2,2]{2,1,0:T(2,128)S(1)}, u32[]{:S(2)}, u32[]{:S(2)}) async-start(f32[64,2,2]{2,1,0:T(2,128)} %copy.629), calls=%async_computation.1 | async-start | bytes 131072 | tf_op jit(solution)/shard_map/all_to_all | solution.py:40
  120.0 1.9 copy.639
  121.9 9.2 %all-to-all-done.1 = f32[64,2,2]{2,1,0:T(2,128)S(1)} async-done(((f32[64,2,2]{2,1,0:T(2,128)}), f32[64,2,2]{2,1,0:T(2,128)S(1)}, u32[]{:S(2)}, u32[]{:S(2)}) %all-to-all-start.1) | async-done | bytes 1056 | tf_op jit(solution)/shard_map/all_to_all | solution.py:40
  131.1 4.7 %all-to-all-start.3 = ((f32[64,2,2,9,128]{4,2,3,1,0:T(2,128)}), f32[64,2,2,9,128]{4,2,3,1,0:T(2,128)S(1)}, u32[]{:S(2)}, u32[]{:S(2)}) async-start(f32[64,2,2,9,128]{4,2,3,1,0:T(2,128)} %copy.639), calls=%async_computation.3 | async-start | bytes 2359296 | tf_op jit(solution)/shard_map/all_to_all | solution.py:40
  135.9 28.9 %all-to-all-done.3 = f32[64,2,2,9,128]{4,2,3,1,0:T(2,128)S(1)} async-done(((f32[64,2,2,9,128]{4,2,3,1,0:T(2,128)}), f32[64,2,2,9,128]{4,2,3,1,0:T(2,128)S(1)}, u32[]{:S(2)}, u32[]{:S(2)}) %all-to-all-start.3) | async-done | bytes 1179680 | tf_op jit(solution)/shard_map/all_to_all | solution.py:40
  165.8 1.7 convolution_bitcast_fusion
  167.6 0.9 copy.768
  168.5 4.1 %all-to-all-start.4 = ((f32[4,128,9,32]{1,3,2,0:T(8,128)}), f32[4,128,9,32]{1,3,2,0:T(8,128)S(1)}, u32[]{:S(2)}, u32[]{:S(2)}) async-start(f32[4,128,9,32]{1,3,2,0:T(8,128)} %bitcast.556), calls=%async_computation.4 | async-start | bytes 1179648 | tf_op jit(solution)/shard_map/all_to_all | solution.py:52
  173.3 6.6 %all-to-all-done.4 = f32[4,128,9,32]{1,3,2,0:T(8,128)S(1)} async-done(((f32[4,128,9,32]{1,3,2,0:T(8,128)}), f32[4,128,9,32]{1,3,2,0:T(8,128)S(1)}, u32[]{:S(2)}, u32[]{:S(2)}) %all-to-all-start.4) | async-done | bytes 589856 | tf_op jit(solution)/shard_map/all_to_all | solution.py:52
  180.0 7.8 %collective-permute-start.9 = (f32[8,1,128]{2,1,0:T(1,128)S(1)}, f32[8,1,128]{2,1,0:T(1,128)S(1)}, u32[]{:S(2)}, u32[]{:S(2)}) collective-permute-start(f32[8,1,128]{2,1,0:T(1,128)S(1)} %get-tuple-element.392), channel_id=1, source_target_pairs={{4,0},{8,4},{12,8},{16,12},{20,16},{24,20},{28,24},{32,28},{36,32}... | collective-permute-start | bytes 12296 | tf_op jit(solution)/shard_map/ppermute | solution.py:65
  187.9 2.8 %collective-permute-start.11 = (f32[8,4,1]{2,1,0:T(4,128)S(1)}, f32[8,4,1]{2,1,0:T(4,128)S(1)}, u32[]{:S(2)}, u32[]{:S(2)}) collective-permute-start(f32[8,4,1]{2,1,0:T(4,128)S(1)} %get-tuple-element.390), channel_id=1, source_target_pairs={{1,0},{2,1},{3,2},{0,3},{5,4},{6,5},{7,6},{4,7},{9,8},{10,9},{11,1... | collective-permute-start | bytes 392 | tf_op jit(solution)/shard_map/ppermute | solution.py:65
  190.7 3.0 %collective-permute-start.8 = (f32[8,1,128]{2,1,0:T(1,128)S(1)}, f32[8,1,128]{2,1,0:T(1,128)S(1)}, u32[]{:S(2)}, u32[]{:S(2)}) collective-permute-start(f32[8,1,128]{2,1,0:T(1,128)S(1)} %get-tuple-element.391), channel_id=1, source_target_pairs={{0,4},{4,8},{8,12},{12,16},{16,20},{20,24},{24,28},{28,32},{32,36}... | collective-permute-start | bytes 12296 | tf_op jit(solution)/shard_map/ppermute | solution.py:64
  193.6 2.5 %collective-permute-start.10 = (f32[8,4,1]{2,1,0:T(4,128)S(1)}, f32[8,4,1]{2,1,0:T(4,128)S(1)}, u32[]{:S(2)}, u32[]{:S(2)}) collective-permute-start(f32[8,4,1]{2,1,0:T(4,128)S(1)} %get-tuple-element.389), channel_id=1, source_target_pairs={{0,1},{1,2},{2,3},{3,0},{4,5},{5,6},{6,7},{7,4},{8,9},{9,10},{10,1... | collective-permute-start | bytes 392 | tf_op jit(solution)/shard_map/ppermute | solution.py:64
  196.2 3.4 %collective-permute-done.10 = f32[8,4,1]{2,1,0:T(4,128)S(1)} collective-permute-done((f32[8,4,1]{2,1,0:T(4,128)S(1)}, f32[8,4,1]{2,1,0:T(4,128)S(1)}, u32[]{:S(2)}, u32[]{:S(2)}) %collective-permute-start.10) | collective-permute-done | bytes 160 | tf_op jit(solution)/shard_map/ppermute | solution.py:64
  199.6 0.7 fusion.83
  (273 shorter events, 32.6 us)
Async XLA Ops:
  0.6 29.2 %copy-start.3 = (f32[5,5,1,1,1]{1,0,4,3,2:T(8,128)S(1)}, f32[5,5,1,1,1]{1,0,4,3,2:T(8,128)}, u32[]{:S(2)}) copy-start(f32[5,5,1,1,1]{1,0,4,3,2:T(8,128)} %constant.949) | copy-start | bytes 304
  1.5 27.8 %collective-permute-start = (f32[3,5,1,128]{3,1,2,0:T(8,128)S(1)}, f32[3,5,1,128]{3,1,2,0:T(8,128)S(1)}, u32[]{:S(2)}, u32[]{:S(2)}) collective-permute-start(f32[3,5,1,128]{3,1,2,0:T(8,128)S(1)} %copy.767), channel_id=1, source_target_pairs={{4,0},{8,4},{12,8},{16,12},{20,16},{24,20},{28,24},{32,28},{36,32}... | collective-permute-start | bytes 23048 | tf_op jit(solution)/shard_map/ppermute | solution.py:22
  15.7 22.8 %collective-permute-start.2 = (f32[1,5,1,1]{2,1,3,0:T(8,128)S(1)}, f32[1,5,1,1]{2,1,3,0:T(8,128)S(1)}, u32[]{:S(2)}, u32[]{:S(2)}) collective-permute-start(f32[1,5,1,1]{2,1,3,0:T(8,128)S(1)} %slice.1239), channel_id=1, source_target_pairs={{0,4},{4,8},{8,12},{12,16},{16,20},{20,24},{24,28},{28,32},{32,36}... | collective-permute-start | bytes 68 | tf_op jit(solution)/shard_map/ppermute | solution.py:22
  20.9 56.2 %all-to-all-start = ((f32[2,1,128]{2,1,0:T(1,128)}), f32[2,1,128]{2,1,0:T(1,128)S(1)}, u32[]{:S(2)}, u32[]{:S(2)}) async-start(f32[2,1,128]{2,1,0:T(1,128)} %reshape.2540), calls=%async_computation | async-start | bytes 2048 | tf_op jit(solution)/shard_map/all_to_all | solution.py:40
  32.3 7.3 %copy-start = (f32[3,5,8,128]{3,2,1,0:T(8,128)S(1)}, f32[3,5,8,128]{3,2,1,0:T(8,128)}, u32[]{:S(2)}) copy-start(f32[3,5,8,128]{3,2,1,0:T(8,128)} %param.68) | copy-start | bytes 184324
  32.3 7.3 %copy-start.5 = (f32[3,5,8,128]{3,2,1,0:T(8,128)S(1)}, f32[3,5,8,128]{3,2,1,0:T(8,128)}, u32[]{:S(2)}) copy-start(f32[3,5,8,128]{3,2,1,0:T(8,128)} %param.69) | copy-start | bytes 184324
  36.5 3.1 %collective-permute-start.1 = (f32[3,5,1,128]{3,1,2,0:T(8,128)S(1)}, f32[3,5,1,128]{3,1,2,0:T(8,128)S(1)}, u32[]{:S(2)}, u32[]{:S(2)}) collective-permute-start(f32[3,5,1,128]{3,1,2,0:T(8,128)S(1)} %copy.700), channel_id=1, source_target_pairs={{0,4},{4,8},{8,12},{12,16},{16,20},{20,24},{24,28},{28,32},{32,36}... | collective-permute-start | bytes 23048 | tf_op jit(solution)/shard_map/ppermute | solution.py:22
  39.7 5.2 %collective-permute-start.3 = (f32[3,5,1,128]{3,1,2,0:T(8,128)S(1)}, f32[3,5,1,128]{3,1,2,0:T(8,128)S(1)}, u32[]{:S(2)}, u32[]{:S(2)}) collective-permute-start(f32[3,5,1,128]{3,1,2,0:T(8,128)S(1)} %slice.1389), channel_id=1, source_target_pairs={{4,0},{8,4},{12,8},{16,12},{20,16},{24,20},{28,24},{32,28},{36,32}... | collective-permute-start | bytes 23048 | tf_op jit(solution)/shard_map/ppermute | solution.py:22
  47.7 6.5 %copy-start.6 = (s32[64,2]{0,1:T(2,128)S(1)}, s32[64,2]{0,1:T(2,128)}, u32[]{:S(2)}) copy-start(s32[64,2]{0,1:T(2,128)} %param.75) | copy-start | bytes 1540
  52.2 3.1 %collective-permute-start.4 = (f32[3,5,1,128]{3,1,2,0:T(8,128)S(1)}, f32[3,5,1,128]{3,1,2,0:T(8,128)S(1)}, u32[]{:S(2)}, u32[]{:S(2)}) collective-permute-start(f32[3,5,1,128]{3,1,2,0:T(8,128)S(1)} %copy.707), channel_id=1, source_target_pairs={{0,4},{4,8},{8,12},{12,16},{16,20},{20,24},{24,28},{28,32},{32,36}... | collective-permute-start | bytes 23048 | tf_op jit(solution)/shard_map/ppermute | solution.py:22
  55.4 5.3 %collective-permute-start.5 = (f32[3,5,1,128]{3,1,2,0:T(8,128)S(1)}, f32[3,5,1,128]{3,1,2,0:T(8,128)S(1)}, u32[]{:S(2)}, u32[]{:S(2)}) collective-permute-start(f32[3,5,1,128]{3,1,2,0:T(8,128)S(1)} %slice.1419), channel_id=1, source_target_pairs={{4,0},{8,4},{12,8},{16,12},{20,16},{24,20},{28,24},{32,28},{36,32}... | collective-permute-start | bytes 23048 | tf_op jit(solution)/shard_map/ppermute | solution.py:22
  68.0 3.1 %collective-permute-start.6 = (f32[3,5,1,128]{3,1,2,0:T(8,128)S(1)}, f32[3,5,1,128]{3,1,2,0:T(8,128)S(1)}, u32[]{:S(2)}, u32[]{:S(2)}) collective-permute-start(f32[3,5,1,128]{3,1,2,0:T(8,128)S(1)} %copy.714), channel_id=1, source_target_pairs={{0,4},{4,8},{8,12},{12,16},{16,20},{20,24},{24,28},{28,32},{32,36}... | collective-permute-start | bytes 23048 | tf_op jit(solution)/shard_map/ppermute | solution.py:22
  71.1 8.0 %collective-permute-start.7 = (f32[3,5,1,128]{3,1,2,0:T(8,128)S(1)}, f32[3,5,1,128]{3,1,2,0:T(8,128)S(1)}, u32[]{:S(2)}, u32[]{:S(2)}) collective-permute-start(f32[3,5,1,128]{3,1,2,0:T(8,128)S(1)} %slice.1449), channel_id=1, source_target_pairs={{4,0},{8,4},{12,8},{16,12},{20,16},{24,20},{28,24},{32,28},{36,32}... | collective-permute-start | bytes 23048 | tf_op jit(solution)/shard_map/ppermute | solution.py:22
  94.4 0.9 copy-start.2
  94.4 1.0 copy-start.1
  94.4 1.2 copy-start.7
  101.0 30.1 %all-to-all-start.1 = ((f32[64,2,2]{2,1,0:T(2,128)}), f32[64,2,2]{2,1,0:T(2,128)S(1)}, u32[]{:S(2)}, u32[]{:S(2)}) async-start(f32[64,2,2]{2,1,0:T(2,128)} %copy.629), calls=%async_computation.1 | async-start | bytes 131072 | tf_op jit(solution)/shard_map/all_to_all | solution.py:40
  131.1 33.8 %all-to-all-start.3 = ((f32[64,2,2,9,128]{4,2,3,1,0:T(2,128)}), f32[64,2,2,9,128]{4,2,3,1,0:T(2,128)S(1)}, u32[]{:S(2)}, u32[]{:S(2)}) async-start(f32[64,2,2,9,128]{4,2,3,1,0:T(2,128)} %copy.639), calls=%async_computation.3 | async-start | bytes 2359296 | tf_op jit(solution)/shard_map/all_to_all | solution.py:40
  168.5 11.5 %copy-start.4 = (f32[9,8,4,128]{3,2,1,0:T(4,128)S(1)}, f32[9,8,4,128]{3,2,1,0:T(4,128)}, u32[]{:S(2)}) copy-start(f32[9,8,4,128]{3,2,1,0:T(4,128)} %param.80) | copy-start | bytes 442372
  168.5 11.4 %all-to-all-start.4 = ((f32[4,128,9,32]{1,3,2,0:T(8,128)}), f32[4,128,9,32]{1,3,2,0:T(8,128)S(1)}, u32[]{:S(2)}, u32[]{:S(2)}) async-start(f32[4,128,9,32]{1,3,2,0:T(8,128)} %bitcast.556), calls=%async_computation.4 | async-start | bytes 1179648 | tf_op jit(solution)/shard_map/all_to_all | solution.py:52
  180.0 16.1 %collective-permute-start.9 = (f32[8,1,128]{2,1,0:T(1,128)S(1)}, f32[8,1,128]{2,1,0:T(1,128)S(1)}, u32[]{:S(2)}, u32[]{:S(2)}) collective-permute-start(f32[8,1,128]{2,1,0:T(1,128)S(1)} %get-tuple-element.392), channel_id=1, source_target_pairs={{4,0},{8,4},{12,8},{16,12},{20,16},{24,20},{28,24},{32,28},{36,32}... | collective-permute-start | bytes 12296 | tf_op jit(solution)/shard_map/ppermute | solution.py:65
  187.9 8.3 %collective-permute-start.11 = (f32[8,4,1]{2,1,0:T(4,128)S(1)}, f32[8,4,1]{2,1,0:T(4,128)S(1)}, u32[]{:S(2)}, u32[]{:S(2)}) collective-permute-start(f32[8,4,1]{2,1,0:T(4,128)S(1)} %get-tuple-element.390), channel_id=1, source_target_pairs={{1,0},{2,1},{3,2},{0,3},{5,4},{6,5},{7,6},{4,7},{9,8},{10,9},{11,1... | collective-permute-start | bytes 392 | tf_op jit(solution)/shard_map/ppermute | solution.py:65
  190.7 5.5 %collective-permute-start.8 = (f32[8,1,128]{2,1,0:T(1,128)S(1)}, f32[8,1,128]{2,1,0:T(1,128)S(1)}, u32[]{:S(2)}, u32[]{:S(2)}) collective-permute-start(f32[8,1,128]{2,1,0:T(1,128)S(1)} %get-tuple-element.391), channel_id=1, source_target_pairs={{0,4},{4,8},{8,12},{12,16},{16,20},{20,24},{24,28},{28,32},{32,36}... | collective-permute-start | bytes 12296 | tf_op jit(solution)/shard_map/ppermute | solution.py:64
  193.6 6.0 %collective-permute-start.10 = (f32[8,4,1]{2,1,0:T(4,128)S(1)}, f32[8,4,1]{2,1,0:T(4,128)S(1)}, u32[]{:S(2)}, u32[]{:S(2)}) collective-permute-start(f32[8,4,1]{2,1,0:T(4,128)S(1)} %get-tuple-element.389), channel_id=1, source_target_pairs={{0,1},{1,2},{2,3},{3,0},{4,5},{5,6},{6,7},{7,4},{8,9},{9,10},{10,1... | collective-permute-start | bytes 392 | tf_op jit(solution)/shard_map/ppermute | solution.py:64
where the time goes:
time: 201 us; the launch traced here: 200 us
  starting transfers between devices  70.3 us (35%)
  waiting for transfers between devices  57 us (28%)
  local copies, waits for them, and re-layouts  32.7 us (16%)
  other arithmetic  26.8 us (13%)
  matrix products  7.07 us (4%)
  blocking collectives  4.32 us (2%)
  between operations  2.15 us (1%)
    all_to_all x3, waiting for transfers between devices, moved_by_axis(): result = lax.all_to_all(result, axes[k], k, k, tiled=True)  38.1 us
    all_to_all x3, starting transfers between devices, moved_by_axis(): result = lax.all_to_all(result, axes[k], k, k, tiled=True)  27.3 us
    ppermute x8, starting transfers between devices, from_behind(): lax.ppermute(value, axis, [(source, source + steps) for source in range(f...  22.8 us
    scatter-add x20, other arithmetic, from_elements(): assembled.at[:, :, b:b + 4 * count_cols:4].add(radial[:, :, :, b])  12.9 us
    gather x1, local copies, waits for them, and re-layouts, on_device(): gathered = padded[:, row_index[:, :, None], col_index[:, None, :], :]  10.8 us
    ppermute x2, starting transfers between devices, with_halo(): lax.ppermute(first, axis, [(b, a) for a, b in up])  10.6 us
    ppermute x8, waiting for transfers between devices, from_behind(): lax.ppermute(value, axis, [(source, source + steps) for source in range(f...  8.86 us
    unnamed x46, local copies, waits for them, and re-layouts  6.7 us
  transfers between devices with their start and end apart: 16, of which 9 were waited for; matrix products, arithmetic and copies ran while one was open for 22% of the time, Pallas kernels for 0%

commit v1 on v0

v1 whole, which is shorter than its diff:
```python
import math

import jax
import jax.numpy as jnp
import numpy as np
from jax import lax
from jax.experimental import pallas as pl
from jax.experimental.pallas import tpu as pltpu
from jax.sharding import Mesh
from jax.sharding import PartitionSpec as P

ORDERS = 256
STEPS = 3
MER = ("mer_0", "mer_1", "mer_2")
SIDES = ("mer_0", "mer_1")

step_scale = 0.015
smooth_rate = 0.125


def gll_tables():
    nodes = np.array([-1.0, -math.sqrt(3.0 / 7.0), 0.0, math.sqrt(3.0 / 7.0), 1.0])
    weights = np.array([0.1, 49.0 / 90.0, 32.0 / 45.0, 49.0 / 90.0, 0.1])
    derivative = np.zeros((5, 5))
    for i in range(5):
        for j in range(5):
            if i == j:
                derivative[i, j] = sum(1.0 / (nodes[i] - nodes[l]) for l in range(5) if l != i)
            else:
                scale_i = np.prod([nodes[i] - nodes[l] for l in range(5) if l != i])
                scale_j = np.prod([nodes[j] - nodes[l] for l in range(5) if l != j])
                derivative[i, j] = scale_i / (scale_j * (nodes[i] - nodes[j]))
    return nodes, weights, derivative


def stiffness_rows():
    _, weights, derivative = gll_tables()
    return (derivative.T @ np.diag(weights) @ derivative) / weights[:, None]


def basis_tables(blocks):
    k = np.arange(2 * ORDERS)
    order = k // 2
    width = 2 * ORDERS // blocks
    j = np.arange(2 * ORDERS)
    angle = (order[:, None] * j[None, :] % (2 * ORDERS)) * (2.0 * math.pi / (2 * ORDERS))
    even = (k % 2 == 0)[:, None]
    value = np.where(even, np.cos(angle), np.sin(angle)) / math.sqrt(ORDERS)
    slope = np.where(even, -np.sin(angle), np.cos(angle)) * (order[:, None] / ORDERS) / math.sqrt(ORDERS)
    table = np.stack([
        np.concatenate([value[:, b * width:(b + 1) * width], slope[:, b * width:(b + 1) * width]], axis=1)
        for b in range(blocks)
    ]).astype(np.float32)
    high = table.astype(jnp.bfloat16)
    low = (table - high.astype(np.float32)).astype(jnp.bfloat16)
    return np.stack([high, low], axis=1)


def lane_tables():
    nodes = gll_tables()[0]
    rows = np.zeros((16, 256), np.float32)
    for r in range(135):
        if r < 120:
            s, a, c = r // 40, r // 8 % 5, r % 8
        else:
            s, a, c = (r - 120) // 5, (r - 120) % 5, 8

        def place(first, n):
            others = [l for l in range(5) if l != n]
            for i, l in enumerate(others):
                rows[first + i, r] = nodes[l]
            rows[first + 4, r] = 1.0 / np.prod([nodes[n] - nodes[l] for l in others])

        place(0, a)
        if c <= 4:
            place(5, c)
        if c >= 4:
            place(10, c - 4)
        rows[15, r] = s + 1
    return rows


def split(x):
    high = x.astype(jnp.bfloat16)
    low = (x - high.astype(jnp.float32)).astype(jnp.bfloat16)
    return high, low


def dot(a, b):
    return jnp.dot(a, b, preferred_element_type=jnp.float32)


def pack_kernel(u_ref, v_ref, mod_ref, hoop_ref, coup_ref, dens_ref, count_ref, own_ref, up_ref, down_ref):
    own_ref[30:32] = jnp.zeros((2, 8, 128), jnp.float32)
    up_ref[7] = jnp.zeros((8, 128), jnp.float32)
    up_ref[8] = jnp.zeros((8, 128), jnp.float32)
    down_ref[15] = jnp.zeros((8, 128), jnp.float32)
    for i in range(15):
        u, v = u_ref[i], v_ref[i]
        own_ref[i] = u
        own_ref[15 + i] = v
        up_ref[i // 2, 4 * (i % 2):4 * (i % 2) + 4, :] = u_ref[i, 4:8, :]
        down_ref[i] = u
        down_ref[i, 5:6, :] = v_ref[i, 0:1, :]
    for i, ref in enumerate((mod_ref, hoop_ref, coup_ref, dens_ref, count_ref)):
        both = ref[...].astype(jnp.float32)
        first = jnp.broadcast_to(both[:, 0:1], (1, 128))
        second = jnp.broadcast_to(both[:, 1:2], (1, 128))
        own_ref[30, i:i + 1, :] = first
        own_ref[31, i:i + 1, :] = second
        down_ref[15, i:i + 1, :] = first
        up_ref[8, i:i + 1, :] = second


def pack(u, v, *coefs):
    f32 = jnp.float32
    return pl.pallas_call(
        pack_kernel,
        out_shape=(
            jax.ShapeDtypeStruct((32, 8, 128), f32),
            jax.ShapeDtypeStruct((9, 8, 128), f32),
            jax.ShapeDtypeStruct((16, 8, 128), f32),
        ),
        name="pack",
    )(u, v, *coefs)


def step_kernel(place_ref, own_ref, sib_ref, cross_ref, low_ref, high_ref, u_ref, gather_ref,
                ucol, vcol, coef, state, field):
    core, az = place_ref[0], place_ref[1]
    is_low = core == 0

    def left(i):
        return jnp.where(is_low, cross_ref[i], sib_ref[i])

    def right(i):
        return jnp.where(is_low, sib_ref[i], cross_ref[i])

    zero4 = jnp.zeros((4, 128), jnp.float32)
    zero8 = jnp.zeros((8, 128), jnp.float32)
    for i in range(15):
        ucol[i, 0:8, :] = zero8
        ucol[i, 4:8, :] = low_ref[i // 2, 4 * (i % 2):4 * (i % 2) + 4, :]
        ucol[i, 8:16, :] = left(i)
        ucol[i, 16:24, :] = own_ref[i]
        ucol[i, 24:32, :] = right(i)
        ucol[i, 32:40, :] = high_ref[i]
        vcol[i, 0:8, :] = zero8
        vcol[i, 8:16, :] = left(15 + i)
        vcol[i, 16:24, :] = own_ref[15 + i]
        vcol[i, 24:32, :] = right(15 + i)
        vcol[i, 32:40, :] = zero8
        vcol[i, 32:33, :] = high_ref[i, 5:6, :]
    l0, l1, r0, r1 = left(30), left(31), right(30), right(31)
    sources = (low_ref[8], l0, l1, own_ref[30], own_ref[31], r0, r1, high_ref[15])
    for i in range(5):
        for e, tile in enumerate(sources):
            coef[i, e:e + 1, :] = tile[i:i + 1, :]

    lane = lax.broadcasted_iota(jnp.int32, (8, 128), 1)
    order = ((az * 128 + lane) // 2).astype(jnp.float32)
    ratio = order * (1.0 / ORDERS)
    mask = jnp.where(order < coef[4], 1.0, 0.0)
    is_even = lane % 2 == 0
    stiff = coef[0] * mask
    hoop = coef[1] * mask * ratio * ratio
    couple = coef[2] * mask * ratio
    couple_even = jnp.where(is_even, couple, 0.0)
    couple_odd = jnp.where(is_even, 0.0, -couple)
    density = coef[3]
    present = density > 0.0
    inner = jnp.where(present, step_scale / jnp.where(present, density, 1.0), 0.0)
    shared_density = density + pltpu.roll(density, 1, 0)
    edge = jnp.where(present, step_scale / jnp.where(present, shared_density, 1.0), 0.0)
    field[0], field[1], field[2], field[3], field[4], field[5] = (
        stiff, hoop, couple_even, couple_odd, inner, edge)

    for i in range(15):
        for b in range(5):
            u = ucol[i, pl.ds(4 + b, 8, stride=4), :]
            state[0, i, b] = u
            if b < 4:
                state[1, i, b] = u - vcol[i, pl.ds(4 + b, 8, stride=4), :]

    rows = stiffness_rows()

    def one_step(n, carry):
        now = lax.rem(n, 2)
        other = 1 - now
        stiff, hoop = field[0], field[1]
        couple_even, couple_odd = field[2], field[3]
        inner, edge = field[4], field[5]

        def coupled(x):
            return pltpu.roll(x, 127, 1) * couple_even + pltpu.roll(x, 1, 1) * couple_odd

        for s in range(3):
            u = [[state[now, 5 * s + a, b] for b in range(5)] for a in range(5)]
            for a in range(5):
                forces = []
                for b in range(5):
                    total = u[a][b] * float(rows[a, a] + rows[b, b])
                    for other_a in range(5):
                        if other_a != a:
                            total = total + u[other_a][b] * float(rows[a, other_a])
                    for other_b in range(5):
                        if other_b != b:
                            total = total + u[a][other_b] * float(rows[b, other_b])
                    force = -(stiff * total + hoop * u[a][b])
                    if s == 0:
                        force = force + coupled(state[now, 10 + a, b])
                    if s == 2:
                        force = force - coupled(state[now, a, b])
                    forces.append(force)
                forces[0] = forces[0] + pltpu.roll(forces[4], 1, 0)
                for b in range(4):
                    following = (
                        2.0 * u[a][b] - state[other, 5 * s + a, b]
                        + (edge if b == 0 else inner) * forces[b]
                    )
                    state[other, 5 * s + a, b] = following
                    if b == 0:
                        state[other, 5 * s + a, 4] = pltpu.roll(following, 7, 0)
        return carry

    lax.fori_loop(0, STEPS, one_step, 0)
    last = STEPS % 2
    for i in range(15):
        for b in range(4):
            ucol[i, pl.ds(4 + b, 8, stride=4), :] = state[last, i, b]
    for q in range(4):
        gather_ref[q, 15:17] = jnp.zeros((2, 8, 128), jnp.float32)
    for i in range(15):
        own = ucol[i, 16:24, :]
        rim = ucol[i, 24:25, :]
        u_ref[i] = own
        for q in range(4):
            gather_ref[q, i] = own
            gather_ref[q, 15 + i // 8, i % 8:i % 8 + 1, :] = rim


def march(place, own, sib, cross, low, high):
    f32 = jnp.float32
    vmem = pl.BlockSpec(memory_space=pltpu.VMEM)
    return pl.pallas_call(
        step_kernel,
        in_specs=[pl.BlockSpec(memory_space=pltpu.SMEM)] + [vmem] * 5,
        out_specs=(vmem, vmem),
        out_shape=(
            jax.ShapeDtypeStruct((15, 8, 128), f32),
            jax.ShapeDtypeStruct((4, 17, 8, 128), f32),
        ),
        scratch_shapes=[
            pltpu.VMEM((15, 40, 128), f32),
            pltpu.VMEM((15, 40, 128), f32),
            pltpu.VMEM((5, 8, 128), f32),
            pltpu.VMEM((2, 15, 5, 8, 128), f32),
            pltpu.VMEM((6, 8, 128), f32),
        ],
        name="march",
    )(place, own, sib, cross, low, high)


def weight_kernel(table_ref, owners_ref, lanes_ref, value_ref, pair_ref, last_ref, extra_ref):
    table = table_ref[...]
    xi, eta, second, scale = table[:, 0:1], table[:, 1:2], table[:, 2:3], table[:, 3:4]
    owner, code = table[:, 4:5], table[:, 5:6]

    def basis(x, rows):
        d1, d2, d3, d4 = x - rows[0], x - rows[1], x - rows[2], x - rows[3]
        d12, d34 = d1 * d2, d3 * d4
        return d12 * d34 * rows[4], ((d1 + d2) * d34 + d12 * (d3 + d4)) * rows[4]

    lanes = [lanes_ref[i:i + 1, :] for i in range(16)]
    value_a, slope_a = basis(xi, lanes[0:5])
    first_b = basis(eta, lanes[5:10])
    second_b = basis(eta, lanes[10:15])
    value_b = jnp.where(second > 0.5, second_b[0], first_b[0])
    slope_b = jnp.where(second > 0.5, second_b[1], first_b[1])
    along = split(jnp.concatenate([slope_a * value_b, value_a * slope_b], axis=0))
    around = split(value_a * value_b * scale)

    owners = owners_ref[0:1, :]
    lane = lax.broadcasted_iota(jnp.int32, (64, 128), 1)
    earlier = lax.broadcasted_iota(jnp.int32, (64, 128), 0) < lane % 64
    rank = jnp.sum(jnp.where((owner == owners) & earlier, 1.0, 0.0), axis=0, keepdims=True)
    slot = owners * 2.0 + rank

    row = lax.broadcasted_iota(jnp.int32, (512, 128), 0)
    column = lax.broadcasted_iota(jnp.int32, (512, 128), 1)
    half = (row // 4) % 2
    row_slot = (row // 8) * 4 + row % 4
    hit = slot == row_slot.astype(jnp.float32)
    in_half = (column // 64) == half
    value_place = jnp.where(hit & in_half, 1.0, 0.0).astype(jnp.bfloat16)
    around_place = jnp.where(hit & (column < 64), 1.0, 0.0).astype(jnp.bfloat16)
    for n in range(2):
        value_ref[n] = dot(value_place, along[n]).astype(jnp.bfloat16)
    row2 = lax.broadcasted_iota(jnp.int32, (512, 256), 0)
    half2 = ((row2 // 4) % 2).astype(jnp.float32)
    component = lanes[15]
    pad = jnp.zeros((64, 256), jnp.bfloat16)
    for n in range(2):
        weights = dot(around_place, jnp.concatenate([around[n], pad], axis=0))
        pair_ref[n] = jnp.where(component == half2 + 1.0, weights, 0.0).astype(jnp.bfloat16)
        last_ref[n] = jnp.where((component == 3.0) & (half2 == 0.0), weights, 0.0).astype(jnp.bfloat16)
    codes = jnp.concatenate(
        [jnp.broadcast_to(code, (64, 128)), jnp.zeros((64, 128), jnp.float32)], axis=0
    ).astype(jnp.bfloat16)
    extra_ref[...] = jnp.where(half == 1, dot(around_place, codes), 0.0)


def point_weights(table, owners, lanes):
    bf16 = jnp.bfloat16
    return pl.pallas_call(
        weight_kernel,
        out_shape=(
            jax.ShapeDtypeStruct((2, 512, 256), bf16),
            jax.ShapeDtypeStruct((2, 512, 256), bf16),
            jax.ShapeDtypeStruct((2, 512, 256), bf16),
            jax.ShapeDtypeStruct((512, 128), jnp.float32),
        ),
        name="weights",
    )(table, owners, lanes)


def message_kernel(nodes_ref, basis_ref, value_ref, pair_ref, last_ref, extra_ref, out_ref):
    coefs = jnp.concatenate([nodes_ref[q].reshape(136, 128) for q in range(4)], axis=1)
    high, low = split(coefs)
    samples = dot(high, basis_ref[0]) + (dot(low, basis_ref[0]) + dot(high, basis_ref[1]))
    row = lax.broadcasted_iota(jnp.int32, (136, 128), 0)
    component = jnp.where(row < 120, row // 40, (row - 120) // 5)
    values, slopes = samples[:, :128], samples[:, 128:]
    pad = jnp.zeros((120, 384), jnp.float32)
    spread = jnp.concatenate([jnp.where(component == s, values, 0.0) for s in range(3)], axis=1)
    high, low = split(jnp.concatenate([spread, pad], axis=0))
    along = dot(value_ref[0], high) + (dot(value_ref[1], high) + dot(value_ref[0], low))
    for s in range(3):
        out_ref[:, s] = along[:, 128 * s:128 * s + 128].reshape(64, 8, 128)
    high, low = split(jnp.concatenate([slopes, pad[:, :128]], axis=0))
    pair = dot(pair_ref[0], high) + (dot(pair_ref[1], high) + dot(pair_ref[0], low))
    out_ref[:, 3] = pair.reshape(64, 8, 128)
    last = dot(last_ref[0], high) + (dot(last_ref[1], high) + dot(last_ref[0], low))
    out_ref[:, 4] = (last + extra_ref[...]).reshape(64, 8, 128)


def messages(nodes, basis, value, pair, last, extra):
    return pl.pallas_call(
        message_kernel,
        out_shape=jax.ShapeDtypeStruct((64, 5, 8, 128), jnp.float32),
        name="messages",
    )(nodes, basis, value, pair, last, extra)


def voxel_kernel(place_ref, arrived_ref, own_ref, sib_ref, out_ref):
    is_low = place_ref[0] == 0
    tail = arrived_ref[:, 4]
    sub = lax.broadcasted_iota(jnp.int32, (64, 8, 128), 1)
    codes = jnp.where(sub >= 4, tail, pltpu.roll(tail, 4, 1)).reshape(512, 128)
    row = lax.broadcasted_iota(jnp.int32, (512, 128), 0)
    lane = lax.broadcasted_iota(jnp.int32, (512, 128), 1)
    match = ((row // 2) % 4 == lane // 32) & (codes == (lane % 32 + 1).astype(jnp.float32))
    sorting = jnp.where(match, 1.0, 0.0).astype(jnp.bfloat16)
    which = ((0, 1), (3, 4), (6, 7), (2, 5), (8, None))
    totals = [jnp.zeros((32, 128), jnp.float32) for _ in range(2)]
    for t in range(5):
        high, low = split(arrived_ref[:, t].reshape(512, 128))
        both = lax.dot_general(
            sorting, jnp.concatenate([high, low], axis=1), (((0,), (0,)), ((), ())),
            preferred_element_type=jnp.float32,
        )
        summed = both[:, :128] + both[:, 128:]
        for half in range(2):
            g = which[t][half]
            if g is None:
                continue
            for core in range(2):
                mine, theirs = own_ref[g], sib_ref[g]
                adjoint = jnp.where(is_low, mine, theirs) if core == 0 else jnp.where(is_low, theirs, mine)
                first = half * 64 + core * 32
                totals[core] = totals[core] + summed[first:first + 32] * adjoint
    out_ref[0] = totals[0]
    out_ref[1] = totals[1]


def voxels(place, arrived, own, sib):
    vmem = pl.BlockSpec(memory_space=pltpu.VMEM)
    return pl.pallas_call(
        voxel_kernel,
        in_specs=[pl.BlockSpec(memory_space=pltpu.SMEM), vmem, vmem, vmem],
        out_specs=vmem,
        out_shape=jax.ShapeDtypeStruct((2, 32, 128), jnp.float32),
        name="voxels",
    )(place, arrived, own, sib)


def total_kernel(place_ref, mine_ref, theirs_ref, own_ref, inner_ref, edge_ref, full):
    is_low = place_ref[0] == 0
    low = mine_ref[0] + theirs_ref[0]
    high = mine_ref[1] + theirs_ref[1]
    own_ref[...] = jnp.where(is_low, low, high)
    full[0] = low
    full[1] = high
    low_first, low_last = full[0, pl.ds(0, 8, stride=4), :], full[0, pl.ds(3, 8, stride=4), :]
    high_first, high_last = full[1, pl.ds(0, 8, stride=4), :], full[1, pl.ds(3, 8, stride=4), :]
    edge_ref[...] = jnp.where(is_low, low_first, high_last)
    inner_ref[...] = jnp.where(is_low, high_first, low_last)


def total(place, mine, theirs):
    vmem = pl.BlockSpec(memory_space=pltpu.VMEM)
    f32 = jnp.float32
    return pl.pallas_call(
        total_kernel,
        in_specs=[pl.BlockSpec(memory_space=pltpu.SMEM), vmem, vmem],
        out_specs=(vmem, vmem, vmem),
        out_shape=(
            jax.ShapeDtypeStruct((32, 128), f32),
            jax.ShapeDtypeStruct((8, 128), f32),
            jax.ShapeDtypeStruct((8, 128), f32),
        ),
        scratch_shapes=[pltpu.VMEM((2, 32, 128), f32)],
        name="total",
    )(place, mine, theirs)


def smooth_kernel(place_ref, raw_ref, inner_ref, outer_ref, before_ref, after_ref, out_ref, framed):
    is_low = place_ref[0] == 0
    raw = raw_ref[...]
    inner, outer = inner_ref[...], outer_ref[...]
    below = jnp.where(is_low, outer, inner)
    above = jnp.where(is_low, inner, outer)
    framed[0:8] = jnp.zeros((8, 128), jnp.float32)
    framed[8:40] = raw
    framed[40:48] = jnp.zeros((8, 128), jnp.float32)
    lane = lax.broadcasted_iota(jnp.int32, (32, 128), 1)
    row = lax.broadcasted_iota(jnp.int32, (32, 128), 0)
    west = pltpu.roll(jnp.where(lane == 127, before_ref[...], raw), 1, 1)
    east = pltpu.roll(jnp.where(lane == 0, after_ref[...], raw), 127, 1)
    neighbours = framed[4:36] + framed[12:44] + west + east
    down = jnp.where(row % 4 == 0, 0.0, framed[7:39])
    up = jnp.where(row % 4 == 3, 0.0, framed[9:41])
    neighbours = neighbours + down + up
    out_ref[...] = raw + smooth_rate * (neighbours - 6.0 * raw)
    out_ref[pl.ds(0, 8, stride=4), :] += smooth_rate * below
    out_ref[pl.ds(3, 8, stride=4), :] += smooth_rate * above


def smooth(place, raw, inner, outer, before, after):
    vmem = pl.BlockSpec(memory_space=pltpu.VMEM)
    return pl.pallas_call(
        smooth_kernel,
        in_specs=[pl.BlockSpec(memory_space=pltpu.SMEM)] + [vmem] * 5,
        out_specs=vmem,
        out_shape=jax.ShapeDtypeStruct((32, 128), jnp.float32),
        scratch_shapes=[pltpu.VMEM((48, 128), jnp.float32)],
        name="smooth",
    )(place, raw, inner, outer, before, after)


def on_device(
    displacement,
    velocity,
    modulus,
    hoop_strength,
    coupling,
    density,
    order_count,
    point_element,
    point_local,
    azimuth_scale,
    point_owner,
    point_cell,
    adjoint_strain,
):
    f32 = jnp.float32
    count = lax.axis_size(MER)
    az_count = lax.axis_size("az")
    core, az = lax.axis_index("mer_2"), lax.axis_index("az")
    place = jnp.stack([core, az]).astype(jnp.int32)
    swap = [(0, 1), (1, 0)]
    cross = [(c, c + 1) for c in range(1, count - 1, 2)] + [(c + 1, c) for c in range(1, count - 1, 2)]

    own, up, down = pack(
        displacement.reshape(15, 8, 128), velocity.reshape(15, 8, 128),
        modulus, hoop_strength, coupling, density, order_count,
    )
    sib = lax.ppermute(own, "mer_2", swap)
    outer = lax.ppermute(own, MER, cross)
    low = lax.ppermute(up, MER, [(i, i + 2) for i in range(count - 2)])
    high = lax.ppermute(down, MER, [(i + 2, i) for i in range(count - 2)])
    final, spread = march(place, own, sib, outer, low, high)

    owner = point_owner.astype(f32)
    table = jnp.concatenate(
        [
            point_local,
            (point_element[:, 1:2] % 2).astype(f32),
            azimuth_scale[:, None],
            owner,
            (point_cell[:, None] + 1).astype(f32),
            jnp.zeros((64, 2), f32),
        ],
        axis=1,
    )
    owners = jnp.concatenate([owner, owner], axis=0).reshape(1, 128)
    weights = point_weights(table, owners, jnp.asarray(lane_tables()))
    basis = lax.dynamic_index_in_dim(jnp.asarray(basis_tables(az_count)), az, 0, keepdims=False)

    nodes = lax.all_to_all(spread, "az", 0, 0, tiled=True)
    outgoing = messages(nodes, basis, *weights)
    arrived = lax.all_to_all(outgoing, SIDES, 0, 0, tiled=True)

    adjoint = adjoint_strain.reshape(9, 32, 128)
    adjoint_sib = lax.ppermute(adjoint, "mer_2", swap)
    part = voxels(place, arrived, adjoint, adjoint_sib)
    raw, inner, edge = total(place, part, lax.ppermute(part, "mer_2", swap))
    beyond = lax.ppermute(edge, MER, cross)
    ahead = [(i, (i + 1) % az_count) for i in range(az_count)]
    before = lax.ppermute(raw, "az", ahead)
    after = lax.ppermute(raw, "az", [(b, a) for a, b in ahead])
    kernel = smooth(place, raw, inner, beyond, before, after)
    return final.reshape(3, 5, 8, 128), kernel.reshape(8, 4, 128)


def solution(mesh):
    torus = Mesh(mesh.devices.reshape(8, 8, 2, mesh.shape["az"]), ("mer_0", "mer_1", "mer_2", "az"))
    return jax.shard_map(
        on_device,
        mesh=torus,
        in_specs=(
            P(None, None, MER, "az"),
            P(None, None, MER, "az"),
            P(None, MER),
            P(None, MER),
            P(None, MER),
            P(None, MER),
            P(None, MER),
            P(MER, None),
            P(MER, None),
            P(MER),
            P(MER, None),
            P(MER),
            P(None, None, MER, "az"),
        ),
        out_specs=(P(None, None, MER, "az"), P(None, MER, "az")),
        check_vma=False,
    )
```

time: 201 us -> 113 us (0.56)
  waiting for transfers between devices: 57 us -> 28.6 us
  local copies, waits for them, and re-layouts: 32.7 us -> 7.59 us
  other arithmetic: 26.8 us -> 3.24 us
  Pallas kernels: 0 us -> 16.6 us
  starting transfers between devices: 70.3 us -> 55.5 us
  matrix products: 7.07 us -> 0 us
  blocking collectives: 4.32 us -> 0 us
    all_to_all x4 -> x2, waiting for transfers between devices: 44.7 us -> 25.1 us  [the longest x1 24.5 us: on_device(): arrived = lax.all_to_all(outgoing, SIDES, 0, 0, tiled=True)]
    pallas_call x0 -> x7, Pallas kernels: none -> 16.6 us  [the longest x1 4.21 us: messages(): pl.pallas_call(message_kernel, out_shape=jax.ShapeDtypeStruct((64, 5, 8,...]
    scatter-add x26 -> x0, other arithmetic: 12.9 us -> none  [the longest x20 12.9 us: from_elements(): assembled.at[:, :, b:b + 4 * count_cols:4].add(radial[:, :, :, b])]
    all_to_all x4 -> x2, starting transfers between devices: 31.4 us -> 19.3 us  [the longest x1 15.9 us: on_device(): arrived = lax.all_to_all(outgoing, SIDES, 0, 0, tiled=True)]
    gather x1 -> x0, local copies, waits for them, and re-layouts: 10.8 us -> none  [on_device(): gathered = padded[:, row_index[:, :, None], col_index[:, None, :], :]]
    ppermute x12 -> x9, waiting for transfers between devices: 12.3 us -> 3.54 us  [the longest x1 1.49 us: on_device(): beyond = lax.ppermute(edge, MER, cross)]
    dot_general x16 -> x0, matrix products: 7.07 us -> none  [the longest x1 1.75 us: on_device(): jnp.einsum('kj,cgk->jgc', basis, voxel_coefs, precision=highest)]
    unnamed x6 -> x0, other arithmetic: 4.67 us -> none
  transfers between devices with their start and end apart: 16 -> 11, of which waited for: 9 -> 5; matrix products, arithmetic and copies ran while one was open for 22% -> 6% of each run, Pallas kernels for 0% -> 2%
where the time goes in v1:
time: 113 us; the launch traced here: 112 us
  starting transfers between devices  55.5 us (49%)
  waiting for transfers between devices  28.6 us (25%)
  Pallas kernels  16.6 us (15%)
  local copies, waits for them, and re-layouts  7.59 us (7%)
  other arithmetic  3.24 us (3%)
    all_to_all x1, waiting for transfers between devices, on_device(): arrived = lax.all_to_all(outgoing, SIDES, 0, 0, tiled=True)  24.5 us
    all_to_all x1, starting transfers between devices, on_device(): arrived = lax.all_to_all(outgoing, SIDES, 0, 0, tiled=True)  15.9 us
    ppermute x1, starting transfers between devices, on_device(): sib = lax.ppermute(own, 'mer_2', swap)  8.73 us
    ppermute x1, starting transfers between devices, on_device(): raw, inner, edge = total(place, part, lax.ppermute(part, 'mer_2', swap))  7.71 us
    ppermute x1, starting transfers between devices, on_device(): adjoint_sib = lax.ppermute(adjoint, 'mer_2', swap)  5 us
    unnamed x24, local copies, waits for them, and re-layouts  4.3 us
    pallas_call x1, Pallas kernels, messages(): pl.pallas_call(message_kernel, out_shape=jax.ShapeDtypeStruct((64, 5, 8,...  4.21 us
    ppermute x1, starting transfers between devices, on_device(): beyond = lax.ppermute(edge, MER, cross)  3.69 us
  transfers between devices with their start and end apart: 11, of which 5 were waited for; matrix products, arithmetic and copies ran while one was open for 6% of the time, Pallas kernels for 2%

profile of v1, /device:TPU:1, one launch (start us, length us, event | category | flops | bytes accessed | tf_op | source)
XLA Modules:
  0.0 112.3 jit_solution(13661449401008554852)
XLA Ops:
  0.6 1.7 %pack.1 = (f32[32,8,128]{2,1,0:T(8,128)}, f32[9,8,128]{2,1,0:T(8,128)}, f32[16,8,128]{2,1,0:T(8,128)}) custom-call(f32[15,8,128]{2,1,0:T(8,128)} %bitcast.16, f32[15,8,128]{2,1,0:T(8,128)} %bitcast.17, f32[1,2]{1,0:T(1,128)} %mod_ref.1, f32[1,2]{1,0:T(1,128)} %hoop_ref.1, f32[1,2]{1,0:T(1,128)} %coup_ref.1, f32[1,2]{1,0:T(1,128)} %dens_ref.1, s32[1,2]{1,0:T(1,128)} %count_ref.1), custom_call_target="tpu_custom_call" | custom-call | tf_op jit(solution)/shard_map/pack/pallas_call | solution.py:117
  2.3 8.7 %collective-permute-start = (f32[32,8,128]{2,1,0:T(8,128)}, f32[32,8,128]{2,1,0:T(8,128)S(1)}, u32[]{:S(2)}, u32[]{:S(2)}) collective-permute-start(f32[32,8,128]{2,1,0:T(8,128)} %get-tuple-element.14.own_ref), channel_id=1, source_target_pairs={{0,4},{4,0},{1,5},{5,1},{2,6},{6,2},{3,7},{7,3},{8,12},{12,8},{9,1... | collective-permute-start | bytes 393224 | tf_op jit(solution)/shard_map/ppermute | solution.py:488
  11.0 1.9 %collective-permute-start.1 = (f32[32,8,128]{2,1,0:T(8,128)}, f32[32,8,128]{2,1,0:T(8,128)S(1)}, u32[]{:S(2)}, u32[]{:S(2)}) collective-permute-start(f32[32,8,128]{2,1,0:T(8,128)} %get-tuple-element.14.own_ref), channel_id=1, source_target_pairs={{4,8},{12,16},{20,24},{28,32},{36,40},{44,48},{52,56},{60,64},{68,... | collective-permute-start | bytes 393224 | tf_op jit(solution)/shard_map/ppermute | solution.py:489
  13.0 1.3 %collective-permute-start.2 = (f32[9,8,128]{2,1,0:T(8,128)}, f32[9,8,128]{2,1,0:T(8,128)S(1)}, u32[]{:S(2)}, u32[]{:S(2)}) collective-permute-start(f32[9,8,128]{2,1,0:T(8,128)} %get-tuple-element.15), channel_id=1, source_target_pairs={{0,8},{4,12},{8,16},{12,20},{16,24},{20,28},{24,32},{28,36},{32,40... | collective-permute-start | bytes 110600 | tf_op jit(solution)/shard_map/ppermute | solution.py:490
  14.3 1.3 %collective-permute-start.3 = (f32[16,8,128]{2,1,0:T(8,128)}, f32[16,8,128]{2,1,0:T(8,128)S(1)}, u32[]{:S(2)}, u32[]{:S(2)}) collective-permute-start(f32[16,8,128]{2,1,0:T(8,128)} %get-tuple-element.16), channel_id=1, source_target_pairs={{8,0},{12,4},{16,8},{20,12},{24,16},{28,20},{32,24},{36,28},{40,32... | collective-permute-start | bytes 196616 | tf_op jit(solution)/shard_map/ppermute | solution.py:491
  15.6 0.7 fusion
  16.2 0.7 convert_bitcast_fusion
  16.9 0.7 pad_add_fusion.place_ref
  17.6 0.7 convert_element_type.13
  18.2 0.7 concatenate.6
  18.9 0.7 copy.35.table_ref
  19.6 0.0 collective-permute-done.2.low_ref
  19.6 0.0 collective-permute-done.3.high_ref
  19.6 0.0 copy-start.6
  19.6 0.0 collective-permute-done.sib_ref
  19.7 0.0 collective-permute-done.1.cross_ref
  19.7 0.6 copy-done.7
  20.2 0.0 copy-done.6
  20.3 0.0 copy-done.4
  20.3 0.7 copy-done.5
  21.0 2.9 %march.1 = (f32[15,8,128]{2,1,0:T(8,128)}, f32[4,17,8,128]{3,2,1,0:T(8,128)}) custom-call(s32[2]{0:T(128)} %pad_add_fusion.place_ref, f32[32,8,128]{2,1,0:T(8,128)} %get-tuple-element.14.own_ref, f32[32,8,128]{2,1,0:T(8,128)} %copy-done.4, f32[32,8,128]{2,1,0:T(8,128)} %copy-done.5, f32[9,8,128]{2,1,0:T(8,128)} %copy-done.7, f32[16,8,128]{2,1,0:T(8,128)} %copy-done.6), custom_call_target="tpu_custom_call" | custom-call | tf_op jit(solution)/shard_map/march/pallas_call | solution.py:245
  23.8 3.4 %all-to-all-start = ((f32[4,17,8,128]{3,2,1,0:T(8,128)}), f32[4,17,8,128]{3,2,1,0:T(8,128)S(1)}, u32[]{:S(2)}, u32[]{:S(2)}) async-start(f32[4,17,8,128]{3,2,1,0:T(8,128)} %get-tuple-element.18), calls=%async_computation | async-start | bytes 557056 | tf_op jit(solution)/shard_map/all_to_all | solution.py:510
  27.3 0.6 maximum_bitcast_fusion.owners_ref
  27.9 2.5 %weights.1 = (bf16[2,512,256]{2,1,0:T(8,128)(2,1)}, bf16[2,512,256]{2,1,0:T(8,128)(2,1)}, bf16[2,512,256]{2,1,0:T(8,128)(2,1)}, f32[512,128]{1,0:T(8,128)}) custom-call(f32[64,8]{1,0:T(8,128)} %copy.35.table_ref, f32[1,128]{1,0:T(1,128)} %maximum_bitcast_fusion.owners_ref, f32[16,256]{1,0:T(8,128)} %constant.36.clone.lanes_ref), custom_call_target="tpu_custom_call" | custom-call | tf_op jit(solution)/shard_map/weights/pallas_call | solution.py:315
  30.4 1.9 %dynamic-slice_bitcast_fusion.basis_ref = bf16[2,512,256]{2,1,0:T(8,128)(2,1)} fusion(bf16[4,2,512,256]{3,2,1,0:T(8,128)(2,1)} %constant.37.clone, s32[]{:T(128)S(6)} %select_n.11), kind=kLoop, calls=%fused_computation | loop fusion | bytes 1048580 | tf_op jit(solution)/shard_map/jit(dynamic_index_in_dim)/squeeze | solution.py:508
  32.3 0.6 all-to-all-done.nodes_ref
  32.9 0.7 copy-done.1
  33.6 4.2 %messages.1 = f32[64,5,8,128]{3,2,1,0:T(8,128)} custom-call(f32[4,17,8,128]{3,2,1,0:T(8,128)} %copy-done.1, bf16[2,512,256]{2,1,0:T(8,128)(2,1)} %dynamic-slice_bitcast_fusion.basis_ref, bf16[2,512,256]{2,1,0:T(8,128)(2,1)} %get-tuple-element.19.value_ref, bf16[2,512,256]{2,1,0:T(8,128)(2,1)} %get-tuple-element.20.pair_ref, ...), custom_call_target="tpu_custom_call" | custom-call | tf_op jit(solution)/shard_map/messages/pallas_call | solution.py:348
  37.8 15.9 %all-to-all-start.1 = ((f32[64,5,8,128]{3,2,1,0:T(8,128)}), f32[64,5,8,128]{3,2,1,0:T(8,128)S(1)}, u32[]{:S(2)}, u32[]{:S(2)}) async-start(f32[64,5,8,128]{3,2,1,0:T(8,128)} %messages.1), calls=%async_computation.1 | async-start | bytes 2621440 | tf_op jit(solution)/shard_map/all_to_all | solution.py:512
  53.7 5.0 %collective-permute-start.4 = (f32[9,32,128]{2,1,0:T(8,128)S(1)}, f32[9,32,128]{2,1,0:T(8,128)S(1)}, u32[]{:S(2)}, u32[]{:S(2)}) collective-permute-start(f32[9,32,128]{2,1,0:T(8,128)S(1)} %bitcast.15), channel_id=1, source_target_pairs={{0,4},{4,0},{1,5},{5,1},{2,6},{6,2},{3,7},{7,3},{8,12},{12,8},{9,1... | collective-permute-start | bytes 442376 | tf_op jit(solution)/shard_map/ppermute | solution.py:515
  58.7 1.0 collective-permute-done.4.sib_ref
  59.7 24.5 %all-to-all-done.1.arrived_ref = f32[64,5,8,128]{3,2,1,0:T(8,128)S(1)} async-done(((f32[64,5,8,128]{3,2,1,0:T(8,128)}), f32[64,5,8,128]{3,2,1,0:T(8,128)S(1)}, u32[]{:S(2)}, u32[]{:S(2)}) %all-to-all-start.1) | async-done | bytes 1310752 | tf_op jit(solution)/shard_map/all_to_all | solution.py:512
  84.2 1.1 copy-done
  85.3 2.4 %voxels.1.mine_ref = f32[2,32,128]{2,1,0:T(8,128)} custom-call(s32[2]{0:T(128)} %pad_add_fusion.place_ref, f32[64,5,8,128]{3,2,1,0:T(8,128)} %copy-done, f32[9,32,128]{2,1,0:T(8,128)} %bitcast.14, f32[9,32,128]{2,1,0:T(8,128)} %copy-done.3), custom_call_target="tpu_custom_call" | custom-call | tf_op jit(solution)/shard_map/voxels/pallas_call | solution.py:388
  87.7 7.7 %collective-permute-start.5 = (f32[2,32,128]{2,1,0:T(8,128)}, f32[2,32,128]{2,1,0:T(8,128)S(1)}, u32[]{:S(2)}, u32[]{:S(2)}) collective-permute-start(f32[2,32,128]{2,1,0:T(8,128)} %voxels.1.mine_ref), channel_id=1, source_target_pairs={{0,4},{4,0},{1,5},{5,1},{2,6},{6,2},{3,7},{7,3},{8,12},{12,8},{9,1... | collective-permute-start | bytes 98312 | tf_op jit(solution)/shard_map/ppermute | solution.py:517
  95.4 1.0 collective-permute-done.5.theirs_ref
  96.5 0.6 copy-done.8
  97.1 1.4 %total.1 = (f32[32,128]{1,0:T(8,128)}, f32[8,128]{1,0:T(8,128)}, f32[8,128]{1,0:T(8,128)}) custom-call(s32[2]{0:T(128)} %pad_add_fusion.place_ref, f32[2,32,128]{2,1,0:T(8,128)} %voxels.1.mine_ref, f32[2,32,128]{2,1,0:T(8,128)} %copy-done.8), custom_call_target="tpu_custom_call" | custom-call | tf_op jit(solution)/shard_map/total/pallas_call | solution.py:413
  98.5 2.8 %collective-permute-start.7 = (f32[32,128]{1,0:T(8,128)}, f32[32,128]{1,0:T(8,128)S(1)}, u32[]{:S(2)}, u32[]{:S(2)}) collective-permute-start(f32[32,128]{1,0:T(8,128)} %get-tuple-element.23.raw_ref), channel_id=1, source_target_pairs={{0,1},{1,2},{2,3},{3,0},{4,5},{5,6},{6,7},{7,4},{8,9},{9,10},{10,1... | collective-permute-start | bytes 49160 | tf_op jit(solution)/shard_map/ppermute | solution.py:520
  101.3 3.7 %collective-permute-start.8 = (f32[32,128]{1,0:T(8,128)}, f32[32,128]{1,0:T(8,128)S(1)}, u32[]{:S(2)}, u32[]{:S(2)}) collective-permute-start(f32[32,128]{1,0:T(8,128)} %get-tuple-element.23.raw_ref), channel_id=1, source_target_pairs={{1,0},{2,1},{3,2},{0,3},{5,4},{6,5},{7,6},{4,7},{9,8},{10,9},{11,1... | collective-permute-start | bytes 49160 | tf_op jit(solution)/shard_map/ppermute | solution.py:521
  105.0 3.7 %collective-permute-start.6 = (f32[8,128]{1,0:T(8,128)}, f32[8,128]{1,0:T(8,128)S(1)}, u32[]{:S(2)}, u32[]{:S(2)}) collective-permute-start(f32[8,128]{1,0:T(8,128)} %get-tuple-element.25), channel_id=1, source_target_pairs={{4,8},{12,16},{20,24},{28,32},{36,40},{44,48},{52,56},{60,64},{68,... | collective-permute-start | bytes 12296 | tf_op jit(solution)/shard_map/ppermute | solution.py:518
  108.7 1.5 %collective-permute-done.6.outer_ref = f32[8,128]{1,0:T(8,128)S(1)} collective-permute-done((f32[8,128]{1,0:T(8,128)}, f32[8,128]{1,0:T(8,128)S(1)}, u32[]{:S(2)}, u32[]{:S(2)}) %collective-permute-start.6) | collective-permute-done | bytes 4128 | tf_op jit(solution)/shard_map/ppermute | solution.py:518
  110.2 0.0 collective-permute-done.7.before_ref
  110.2 0.0 collective-permute-done.8.after_ref
  110.2 0.6 copy-done.11
  110.8 0.0 copy-done.9
  110.8 0.0 copy-done.10
  110.8 1.5 %smooth.1 = f32[32,128]{1,0:T(8,128)} custom-call(s32[2]{0:T(128)} %pad_add_fusion.place_ref, f32[32,128]{1,0:T(8,128)} %get-tuple-element.23.raw_ref, f32[8,128]{1,0:T(8,128)} %get-tuple-element.24.inner_ref, f32[8,128]{1,0:T(8,128)} %copy-done.11, f32[32,128]{1,0:T(8,128)} %copy-done.9, f32[32,128]{1,0:T(8,128)} %copy-done.10), custom_call_target="tpu_custom_call" | custom-call | tf_op jit(solution)/shard_map/smooth/pallas_call | solution.py:451
  (14 shorter events, 0.0 us)
Async XLA Ops:
  2.3 17.4 %collective-permute-start = (f32[32,8,128]{2,1,0:T(8,128)}, f32[32,8,128]{2,1,0:T(8,128)S(1)}, u32[]{:S(2)}, u32[]{:S(2)}) collective-permute-start(f32[32,8,128]{2,1,0:T(8,128)} %get-tuple-element.14.own_ref), channel_id=1, source_target_pairs={{0,4},{4,0},{1,5},{5,1},{2,6},{6,2},{3,7},{7,3},{8,12},{12,8},{9,1... | collective-permute-start | bytes 393224 | tf_op jit(solution)/shard_map/ppermute | solution.py:488
  11.0 8.6 %collective-permute-start.1 = (f32[32,8,128]{2,1,0:T(8,128)}, f32[32,8,128]{2,1,0:T(8,128)S(1)}, u32[]{:S(2)}, u32[]{:S(2)}) collective-permute-start(f32[32,8,128]{2,1,0:T(8,128)} %get-tuple-element.14.own_ref), channel_id=1, source_target_pairs={{4,8},{12,16},{20,24},{28,32},{36,40},{44,48},{52,56},{60,64},{68,... | collective-permute-start | bytes 393224 | tf_op jit(solution)/shard_map/ppermute | solution.py:489
  13.0 6.7 %collective-permute-start.2 = (f32[9,8,128]{2,1,0:T(8,128)}, f32[9,8,128]{2,1,0:T(8,128)S(1)}, u32[]{:S(2)}, u32[]{:S(2)}) collective-permute-start(f32[9,8,128]{2,1,0:T(8,128)} %get-tuple-element.15), channel_id=1, source_target_pairs={{0,8},{4,12},{8,16},{12,20},{16,24},{20,28},{24,32},{28,36},{32,40... | collective-permute-start | bytes 110600 | tf_op jit(solution)/shard_map/ppermute | solution.py:490
  14.3 5.4 %collective-permute-start.3 = (f32[16,8,128]{2,1,0:T(8,128)}, f32[16,8,128]{2,1,0:T(8,128)S(1)}, u32[]{:S(2)}, u32[]{:S(2)}) collective-permute-start(f32[16,8,128]{2,1,0:T(8,128)} %get-tuple-element.16), channel_id=1, source_target_pairs={{8,0},{12,4},{16,8},{20,12},{24,16},{28,20},{32,24},{36,28},{40,32... | collective-permute-start | bytes 196616 | tf_op jit(solution)/shard_map/ppermute | solution.py:491
  19.6 0.6 copy-start.7
  19.6 0.6 copy-start.6
  19.6 0.7 copy-start.4
  20.3 0.7 copy-start.5
  23.8 9.0 %all-to-all-start = ((f32[4,17,8,128]{3,2,1,0:T(8,128)}), f32[4,17,8,128]{3,2,1,0:T(8,128)S(1)}, u32[]{:S(2)}, u32[]{:S(2)}) async-start(f32[4,17,8,128]{3,2,1,0:T(8,128)} %get-tuple-element.18), calls=%async_computation | async-start | bytes 557056 | tf_op jit(solution)/shard_map/all_to_all | solution.py:510
  32.9 0.7 copy-start.1
  37.8 15.9 %copy-start.2 = (f32[9,8,4,128]{3,2,1,0:T(4,128)S(1)}, f32[9,8,4,128]{3,2,1,0:T(4,128)}, u32[]{:S(2)}) copy-start(f32[9,8,4,128]{3,2,1,0:T(4,128)} %param.27) | copy-start | bytes 442372
  37.8 46.4 %all-to-all-start.1 = ((f32[64,5,8,128]{3,2,1,0:T(8,128)}), f32[64,5,8,128]{3,2,1,0:T(8,128)S(1)}, u32[]{:S(2)}, u32[]{:S(2)}) async-start(f32[64,5,8,128]{3,2,1,0:T(8,128)} %messages.1), calls=%async_computation.1 | async-start | bytes 2621440 | tf_op jit(solution)/shard_map/all_to_all | solution.py:512
  53.7 6.0 %collective-permute-start.4 = (f32[9,32,128]{2,1,0:T(8,128)S(1)}, f32[9,32,128]{2,1,0:T(8,128)S(1)}, u32[]{:S(2)}, u32[]{:S(2)}) collective-permute-start(f32[9,32,128]{2,1,0:T(8,128)S(1)} %bitcast.15), channel_id=1, source_target_pairs={{0,4},{4,0},{1,5},{5,1},{2,6},{6,2},{3,7},{7,3},{8,12},{12,8},{9,1... | collective-permute-start | bytes 442376 | tf_op jit(solution)/shard_map/ppermute | solution.py:515
  59.7 24.5 %copy-start.3 = (f32[9,32,128]{2,1,0:T(8,128)}, f32[9,32,128]{2,1,0:T(8,128)S(1)}, u32[]{:S(2)}) copy-start(f32[9,32,128]{2,1,0:T(8,128)S(1)} %collective-permute-done.4.sib_ref) | copy-start | bytes 442372
  84.2 1.1 copy-start
  87.7 8.8 %collective-permute-start.5 = (f32[2,32,128]{2,1,0:T(8,128)}, f32[2,32,128]{2,1,0:T(8,128)S(1)}, u32[]{:S(2)}, u32[]{:S(2)}) collective-permute-start(f32[2,32,128]{2,1,0:T(8,128)} %voxels.1.mine_ref), channel_id=1, source_target_pairs={{0,4},{4,0},{1,5},{5,1},{2,6},{6,2},{3,7},{7,3},{8,12},{12,8},{9,1... | collective-permute-start | bytes 98312 | tf_op jit(solution)/shard_map/ppermute | solution.py:517
  96.5 0.6 copy-start.8
  98.5 11.7 %collective-permute-start.7 = (f32[32,128]{1,0:T(8,128)}, f32[32,128]{1,0:T(8,128)S(1)}, u32[]{:S(2)}, u32[]{:S(2)}) collective-permute-start(f32[32,128]{1,0:T(8,128)} %get-tuple-element.23.raw_ref), channel_id=1, source_target_pairs={{0,1},{1,2},{2,3},{3,0},{4,5},{5,6},{6,7},{7,4},{8,9},{9,10},{10,1... | collective-permute-start | bytes 49160 | tf_op jit(solution)/shard_map/ppermute | solution.py:520
  101.3 8.9 %collective-permute-start.8 = (f32[32,128]{1,0:T(8,128)}, f32[32,128]{1,0:T(8,128)S(1)}, u32[]{:S(2)}, u32[]{:S(2)}) collective-permute-start(f32[32,128]{1,0:T(8,128)} %get-tuple-element.23.raw_ref), channel_id=1, source_target_pairs={{1,0},{2,1},{3,2},{0,3},{5,4},{6,5},{7,6},{4,7},{9,8},{10,9},{11,1... | collective-permute-start | bytes 49160 | tf_op jit(solution)/shard_map/ppermute | solution.py:521
  105.0 5.2 %collective-permute-start.6 = (f32[8,128]{1,0:T(8,128)}, f32[8,128]{1,0:T(8,128)S(1)}, u32[]{:S(2)}, u32[]{:S(2)}) collective-permute-start(f32[8,128]{1,0:T(8,128)} %get-tuple-element.25), channel_id=1, source_target_pairs={{4,8},{12,16},{20,24},{28,32},{36,40},{44,48},{52,56},{60,64},{68,... | collective-permute-start | bytes 12296 | tf_op jit(solution)/shard_map/ppermute | solution.py:518
  110.2 0.6 copy-start.11
  110.2 0.6 copy-start.9
  110.2 0.6 copy-start.10

commit v2 on v1

v2 whole, which is shorter than its diff:
```python
import math

import jax
import jax.numpy as jnp
import numpy as np
from jax import lax
from jax.experimental import pallas as pl
from jax.experimental.pallas import tpu as pltpu
from jax.sharding import Mesh
from jax.sharding import PartitionSpec as P

ORDERS = 256
STEPS = 3
MER = ("mer_0", "mer_1", "mer_2")
SIDES = ("mer_0", "mer_1")

GRANT = pltpu.CompilerParams(vmem_limit_bytes=16 << 20)

step_scale = 0.015
smooth_rate = 0.125


def gll_tables():
    nodes = np.array([-1.0, -math.sqrt(3.0 / 7.0), 0.0, math.sqrt(3.0 / 7.0), 1.0])
    weights = np.array([0.1, 49.0 / 90.0, 32.0 / 45.0, 49.0 / 90.0, 0.1])
    derivative = np.zeros((5, 5))
    for i in range(5):
        for j in range(5):
            if i == j:
                derivative[i, j] = sum(1.0 / (nodes[i] - nodes[l]) for l in range(5) if l != i)
            else:
                scale_i = np.prod([nodes[i] - nodes[l] for l in range(5) if l != i])
                scale_j = np.prod([nodes[j] - nodes[l] for l in range(5) if l != j])
                derivative[i, j] = scale_i / (scale_j * (nodes[i] - nodes[j]))
    return nodes, weights, derivative


def stiffness_rows():
    _, weights, derivative = gll_tables()
    return (derivative.T @ np.diag(weights) @ derivative) / weights[:, None]


ROWS = 37


def basis_tables():
    k = np.arange(2 * ORDERS)
    order = k // 2
    j = np.zeros(256, np.int64)
    j[:128] = np.arange(128)
    edge = np.arange(128) % 32
    j[128:] = np.where(edge < 9, -1, np.where(edge < 18, 128, 0))
    angle = (order[:, None] * j[None, :] % (2 * ORDERS)) * (2.0 * math.pi / (2 * ORDERS))
    even = (k % 2 == 0)[:, None]
    value = np.where(even, np.cos(angle), np.sin(angle))
    slope = np.where(even, -np.sin(angle), np.cos(angle))
    return (np.stack([value, slope]) / math.sqrt(ORDERS)).astype(np.float32)


def lane_tables():
    nodes = gll_tables()[0]
    rows = np.zeros((16, 256), np.float32)
    for r in range(135):
        if r < 120:
            s, a, c = r // 40, r // 8 % 5, r % 8
        else:
            s, a, c = (r - 120) // 5, (r - 120) % 5, 8

        def place(first, n):
            others = [l for l in range(5) if l != n]
            for i, l in enumerate(others):
                rows[first + i, r] = nodes[l]
            rows[first + 4, r] = 1.0 / np.prod([nodes[n] - nodes[l] for l in others])

        place(0, a)
        if c <= 4:
            place(5, c)
        if c >= 4:
            place(10, c - 4)
        rows[15, r] = s + 1
    return rows


def constant_table():
    return np.concatenate([basis_tables().reshape(1024, 256), lane_tables()], axis=0)


def split(x):
    high = x.astype(jnp.bfloat16)
    low = (x - high.astype(jnp.float32)).astype(jnp.bfloat16)
    return high, low


def dot(a, b):
    return jnp.dot(a, b, preferred_element_type=jnp.float32)


def fetch(pairs, arrived):
    copies = [pltpu.make_async_copy(a, b, arrived.at[i]) for i, (a, b) in enumerate(pairs)]
    for copy in copies:
        copy.start()
    return copies


def pack_kernel(*refs):
    sources, (own_ref, up_ref, down_ref, points_ref) = refs[:12], refs[12:16]
    scratch, arrived = refs[16:28], refs[28]
    copies = fetch(list(zip(sources, scratch)), arrived)
    u_ref, v_ref = scratch[:2]
    element_ref, local_ref, scale_ref, owner_ref, cell_ref = scratch[7:]
    f32 = jnp.float32
    own_ref[30:32] = jnp.zeros((2, 8, 128), f32)
    up_ref[7] = jnp.zeros((8, 128), f32)
    up_ref[8] = jnp.zeros((8, 128), f32)
    down_ref[15] = jnp.zeros((8, 128), f32)
    points_ref[...] = jnp.zeros((8, 128), f32)
    for copy in copies:
        copy.wait()
    for i in range(15):
        u, v = u_ref[i], v_ref[i]
        own_ref[i] = u
        own_ref[15 + i] = v
        up_ref[i // 2, 4 * (i % 2):4 * (i % 2) + 4, :] = u_ref[i, 4:8, :]
        down_ref[i] = u
        down_ref[i, 5:6, :] = v_ref[i, 0:1, :]
    for i, ref in enumerate(scratch[2:7]):
        both = ref[...].astype(f32)
        first = jnp.broadcast_to(both[:, 0:1], (1, 128))
        second = jnp.broadcast_to(both[:, 1:2], (1, 128))
        own_ref[30, i:i + 1, :] = first
        own_ref[31, i:i + 1, :] = second
        down_ref[15, i:i + 1, :] = first
        up_ref[8, i:i + 1, :] = second
    points_ref[0:2, 0:64] = local_ref[...]
    points_ref[2:3, 0:64] = (element_ref[1:2, :] % 2).astype(f32)
    points_ref[3:4, 0:64] = scale_ref[...]
    points_ref[4:5, 0:64] = owner_ref[...].astype(f32)
    points_ref[5:6, 0:64] = (cell_ref[...] + 1).astype(f32)


def pack(*arrays):
    f32 = jnp.float32
    hbm, vmem = pl.BlockSpec(memory_space=pltpu.HBM), pl.BlockSpec(memory_space=pltpu.VMEM)
    return pl.pallas_call(
        pack_kernel,
        in_specs=[hbm] * 12,
        out_specs=(vmem, vmem, vmem, vmem),
        scratch_shapes=[pltpu.VMEM(a.shape, a.dtype) for a in arrays] + [pltpu.SemaphoreType.DMA((12,))],
        out_shape=(
            jax.ShapeDtypeStruct((32, 8, 128), f32),
            jax.ShapeDtypeStruct((9, 8, 128), f32),
            jax.ShapeDtypeStruct((16, 8, 128), f32),
            jax.ShapeDtypeStruct((8, 128), f32),
        ),
        name="pack",
    )(*arrays)


def step_kernel(own_ref, sib_ref, cross_ref, low_ref, high_ref, u_ref, gather_ref,
                ucol, vcol, coef, state, field):
    core, az = lax.axis_index("mer_2"), lax.axis_index("az")
    is_low = core == 0

    def left(i):
        return jnp.where(is_low, cross_ref[i], sib_ref[i])

    def right(i):
        return jnp.where(is_low, sib_ref[i], cross_ref[i])

    zero4 = jnp.zeros((4, 128), jnp.float32)
    zero8 = jnp.zeros((8, 128), jnp.float32)
    for i in range(15):
        ucol[i, 0:8, :] = zero8
        ucol[i, 4:8, :] = low_ref[i // 2, 4 * (i % 2):4 * (i % 2) + 4, :]
        ucol[i, 8:16, :] = left(i)
        ucol[i, 16:24, :] = own_ref[i]
        ucol[i, 24:32, :] = right(i)
        ucol[i, 32:40, :] = high_ref[i]
        vcol[i, 0:8, :] = zero8
        vcol[i, 8:16, :] = left(15 + i)
        vcol[i, 16:24, :] = own_ref[15 + i]
        vcol[i, 24:32, :] = right(15 + i)
        vcol[i, 32:40, :] = zero8
        vcol[i, 32:33, :] = high_ref[i, 5:6, :]
    l0, l1, r0, r1 = left(30), left(31), right(30), right(31)
    sources = (low_ref[8], l0, l1, own_ref[30], own_ref[31], r0, r1, high_ref[15])
    for i in range(5):
        for e, tile in enumerate(sources):
            coef[i, e:e + 1, :] = tile[i:i + 1, :]

    lane = lax.broadcasted_iota(jnp.int32, (8, 128), 1)
    order = ((az * 128 + lane) // 2).astype(jnp.float32)
    ratio = order * (1.0 / ORDERS)
    mask = jnp.where(order < coef[4], 1.0, 0.0)
    is_even = lane % 2 == 0
    stiff = coef[0] * mask
    hoop = coef[1] * mask * ratio * ratio
    couple = coef[2] * mask * ratio
    couple_even = jnp.where(is_even, couple, 0.0)
    couple_odd = jnp.where(is_even, 0.0, -couple)
    density = coef[3]
    present = density > 0.0
    inner = jnp.where(present, step_scale / jnp.where(present, density, 1.0), 0.0)
    shared_density = density + pltpu.roll(density, 1, 0)
    edge = jnp.where(present, step_scale / jnp.where(present, shared_density, 1.0), 0.0)
    field[0], field[1], field[2], field[3], field[4], field[5] = (
        stiff, hoop, couple_even, couple_odd, inner, edge)

    for i in range(15):
        for b in range(5):
            u = ucol[i, pl.ds(4 + b, 8, stride=4), :]
            state[0, i, b] = u
            if b < 4:
                state[1, i, b] = u - vcol[i, pl.ds(4 + b, 8, stride=4), :]

    rows = stiffness_rows()

    def one_step(n, carry):
        now = lax.rem(n, 2)
        other = 1 - now
        stiff, hoop = field[0], field[1]
        couple_even, couple_odd = field[2], field[3]
        inner, edge = field[4], field[5]

        def coupled(x):
            return pltpu.roll(x, 127, 1) * couple_even + pltpu.roll(x, 1, 1) * couple_odd

        for s in range(3):
            u = [[state[now, 5 * s + a, b] for b in range(5)] for a in range(5)]
            for a in range(5):
                forces = []
                for b in range(5):
                    total = u[a][b] * float(rows[a, a] + rows[b, b])
                    for other_a in range(5):
                        if other_a != a:
                            total = total + u[other_a][b] * float(rows[a, other_a])
                    for other_b in range(5):
                        if other_b != b:
                            total = total + u[a][other_b] * float(rows[b, other_b])
                    force = -(stiff * total + hoop * u[a][b])
                    if s == 0:
                        force = force + coupled(state[now, 10 + a, b])
                    if s == 2:
                        force = force - coupled(state[now, a, b])
                    forces.append(force)
                forces[0] = forces[0] + pltpu.roll(forces[4], 1, 0)
                for b in range(4):
                    following = (
                        2.0 * u[a][b] - state[other, 5 * s + a, b]
                        + (edge if b == 0 else inner) * forces[b]
                    )
                    state[other, 5 * s + a, b] = following
                    if b == 0:
                        state[other, 5 * s + a, 4] = pltpu.roll(following, 7, 0)
        return carry

    lax.fori_loop(0, STEPS, one_step, 0)
    last = STEPS % 2
    for i in range(15):
        for b in range(4):
            ucol[i, pl.ds(4 + b, 8, stride=4), :] = state[last, i, b]
    for q in range(4):
        gather_ref[q, 15:17] = jnp.zeros((2, 8, 128), jnp.float32)
    for i in range(15):
        own = ucol[i, 16:24, :]
        rim = ucol[i, 24:25, :]
        u_ref[i] = own
        for q in range(4):
            gather_ref[q, i] = own
            gather_ref[q, 15 + i // 8, i % 8:i % 8 + 1, :] = rim


def march(own, sib, cross, low, high):
    f32 = jnp.float32
    vmem = pl.BlockSpec(memory_space=pltpu.VMEM)
    return pl.pallas_call(
        step_kernel,
        in_specs=[vmem] * 5,
        out_specs=(vmem, vmem),
        out_shape=(
            jax.ShapeDtypeStruct((15, 8, 128), f32),
            jax.ShapeDtypeStruct((4, 17, 8, 128), f32),
        ),
        scratch_shapes=[
            pltpu.VMEM((15, 40, 128), f32),
            pltpu.VMEM((15, 40, 128), f32),
            pltpu.VMEM((5, 8, 128), f32),
            pltpu.VMEM((2, 15, 5, 8, 128), f32),
            pltpu.VMEM((6, 8, 128), f32),
        ],
        compiler_params=GRANT,
        name="march",
    )(own, sib, cross, low, high)


def weight_kernel(points_ref, table_ref, weight_ref, point_ref, basis_ref):
    f32, bf16 = jnp.float32, jnp.bfloat16
    az = lax.axis_index("az")
    diagonal = (lax.broadcasted_iota(jnp.int32, (64, 128), 0)
                == lax.broadcasted_iota(jnp.int32, (64, 128), 1))

    def upright(line):
        return jnp.sum(jnp.where(diagonal, line, 0.0), axis=1, keepdims=True)

    xi, eta, second, scale, owner, code = (upright(points_ref[i:i + 1, :]) for i in range(6))

    def basis(x, rows):
        d1, d2, d3, d4 = x - rows[0], x - rows[1], x - rows[2], x - rows[3]
        d12, d34 = d1 * d2, d3 * d4
        return d12 * d34 * rows[4], ((d1 + d2) * d34 + d12 * (d3 + d4)) * rows[4]

    lanes = [table_ref[1024 + i:1025 + i, :] for i in range(16)]
    value_a, slope_a = basis(xi, lanes[0:5])
    first_b = basis(eta, lanes[5:10])
    second_b = basis(eta, lanes[10:15])
    value_b = jnp.where(second > 0.5, second_b[0], first_b[0])
    slope_b = jnp.where(second > 0.5, second_b[1], first_b[1])
    around = value_a * value_b * scale
    point = split(jnp.concatenate([slope_a * value_b, value_a * slope_b, around], axis=0))
    point_ref[0, 0:192] = point[0]
    point_ref[1, 0:192] = point[1]

    lane = lax.broadcasted_iota(jnp.int32, (64, 128), 1)
    sub = lax.broadcasted_iota(jnp.int32, (64, 128), 0)
    owners = points_ref[4:5, :]
    rank = jnp.sum(jnp.where((owner == owners) & (sub < lane), 1.0, 0.0), axis=0, keepdims=True)
    slot = owners * 2.0 + rank
    row = lax.broadcasted_iota(jnp.int32, (256, 128), 0)
    column = lax.broadcasted_iota(jnp.int32, (256, 128), 1)
    row_slot = (row % 64) * 4 + row // 64
    place = jnp.where((slot == row_slot.astype(f32)) & (column < 64), 1.0, 0.0).astype(bf16)[:, :64]
    for n in range(2):
        for d in range(3):
            weight_ref[2 * d + n] = dot(place, point[n][64 * d:64 * d + 64]).astype(bf16)

    upright_slot = upright(slot)
    group = (lane // 32).astype(f32)
    mine = upright_slot - 4.0 * jnp.floor(upright_slot * 0.25) == group
    point_ref[0, 192:256, 0:128] = jnp.where(mine & (lane % 32 == 31), code, 0.0).astype(bf16)
    point_ref[0, 192:256, 128:256] = jnp.where(mine & (lane % 32 < 18), 1.0, 0.0).astype(bf16)
    chip = jnp.where((jnp.floor(slot * 0.25) == sub.astype(f32)) & (lane < 64), 1.0, 0.0).astype(bf16)
    point_ref[1, 192:256, 0:128] = chip
    point_ref[1, 192:256, 128:256] = chip

    order = lax.broadcasted_iota(jnp.int32, (512, 128), 0) // 2
    turns = (order * az) % 4
    along = jnp.where(turns == 0, 1.0, jnp.where(turns == 2, -1.0, 0.0))
    across = jnp.where(turns == 1, 1.0, jnp.where(turns == 3, -1.0, 0.0))
    ratio = order.astype(f32) * (1.0 / ORDERS)
    first, other = slice(0, 512), slice(512, 1024)
    low_lanes, edge_lanes = slice(0, 128), slice(128, 256)
    value = along * table_ref[first, low_lanes] + across * table_ref[other, low_lanes]
    slope = ratio * (along * table_ref[other, low_lanes] - across * table_ref[first, low_lanes])
    edge_value = along * table_ref[first, edge_lanes] + across * table_ref[other, edge_lanes]
    edge_slope = ratio * (along * table_ref[other, edge_lanes] - across * table_ref[first, edge_lanes])
    kind = ((lax.broadcasted_iota(jnp.int32, (512, 128), 1) % 32) % 9) % 3
    edge = jnp.where(kind == 2, edge_slope, edge_value)
    for i, block in enumerate((value, slope, edge)):
        high, low = split(block)
        basis_ref[0, :, 128 * i:128 * i + 128] = high
        basis_ref[1, :, 128 * i:128 * i + 128] = low


def point_weights(points):
    bf16 = jnp.bfloat16
    return pl.pallas_call(
        weight_kernel,
        out_shape=(
            jax.ShapeDtypeStruct((6, 256, 256), bf16),
            jax.ShapeDtypeStruct((2, 256, 256), bf16),
            jax.ShapeDtypeStruct((2, 512, 384), bf16),
        ),
        compiler_params=GRANT,
        name="weights",
    )(points, jnp.asarray(constant_table()))


def thrice(a, b):
    return dot(a[0], b[0]) + (dot(a[1], b[0]) + dot(a[0], b[1]))


def message_kernel(nodes_ref, weight_ref, point_ref, basis_ref, out_ref):
    f32 = jnp.float32
    coefs = jnp.concatenate([nodes_ref[q].reshape(136, 128) for q in range(4)], axis=1)
    samples = thrice(split(coefs), (basis_ref[0], basis_ref[1]))
    row = lax.broadcasted_iota(jnp.int32, (136, 128), 0)
    component = jnp.where(row < 120, row // 40, (row - 120) // 5)
    pad = jnp.zeros((120, 384), f32)
    values, slopes, edges = samples[:, :128], samples[:, 128:256], samples[:, 256:]

    def spread(block):
        parts = jnp.concatenate([jnp.where(component == s, block, 0.0) for s in range(3)], axis=1)
        return split(jnp.concatenate([parts, pad], axis=0))

    by_kind = (spread(values), None, spread(slopes))
    for d in range(3):
        field = by_kind[0] if d < 2 else by_kind[2]
        rows = thrice((weight_ref[2 * d], weight_ref[2 * d + 1]), field)
        for s in range(3):
            for c in range(4):
                out_ref[pl.ds(4 * (3 * s + d) + c, 64, stride=ROWS), :] = (
                    rows[64 * c:64 * c + 64, 128 * s:128 * s + 128])

    lane = lax.broadcasted_iota(jnp.int32, (136, 128), 1)
    edges = jnp.where(((lane % 32) % 9) // 3 == component, edges, 0.0)
    edges = split(jnp.concatenate([edges, pad[:, :128]], axis=0))
    rows = thrice((point_ref[0, 0:192], point_ref[1, 0:192]), edges)
    lane = lax.broadcasted_iota(jnp.int32, (64, 128), 1)
    kind = ((lane % 32) % 9) % 3
    extra = jnp.where(kind == 0, rows[:64], jnp.where(kind == 1, rows[64:128], rows[128:]))
    extra = (extra * point_ref[0, 192:256, 128:256].astype(f32)
             + point_ref[0, 192:256, 0:128].astype(f32))
    chip = point_ref[1, 192:256, 0:64]
    high, low = split(extra)
    out_ref[pl.ds(36, 64, stride=ROWS), :] = dot(chip, high) + dot(chip, low)


def messages(nodes, *weights):
    return pl.pallas_call(
        message_kernel,
        out_shape=jax.ShapeDtypeStruct((64 * ROWS, 128), jnp.float32),
        compiler_params=GRANT,
        name="messages",
    )(nodes, *weights)


def rims_kernel(own_ref, sib_ref, first_ref, last_ref):
    lane = lax.broadcasted_iota(jnp.int32, (32, 128), 1)
    for n, ref in enumerate((own_ref, sib_ref)):
        first = jnp.zeros((32, 128), jnp.float32)
        last = jnp.zeros((32, 128), jnp.float32)
        for g in range(9):
            first = jnp.where(lane == 9 + g, ref[g, :, 0:1], first)
            last = jnp.where(lane == g, ref[g, :, 127:128], last)
        first_ref[n] = first
        last_ref[n] = last


def rims(own, sib):
    shape = jax.ShapeDtypeStruct((2, 32, 128), jnp.float32)
    return pl.pallas_call(
        rims_kernel, out_shape=(shape, shape), compiler_params=GRANT, name="rims",
    )(own, sib)


def voxel_kernel(arrived_ref, own_ref, sib_ref, before_ref, after_ref, out_ref, cross_ref, diag_ref):
    is_low = lax.axis_index("mer_2") == 0
    f32 = jnp.float32
    tail = arrived_ref[pl.ds(36, 64, stride=ROWS), :]
    lane = lax.broadcasted_iota(jnp.int32, (64, 128), 1)
    wanted = (lane % 32 + 1).astype(f32)
    sorting = jnp.concatenate(
        [
            jnp.where((lane // 32 == c // 2) & (tail[:, 32 * c + 31:32 * c + 32] == wanted), 1.0, 0.0)
            for c in range(4)
        ],
        axis=0,
    ).astype(jnp.bfloat16)

    def sorted_sum(rows):
        high, low = split(rows)
        both = lax.dot_general(
            sorting, jnp.concatenate([high, low], axis=1), (((0,), (0,)), ((), ())),
            preferred_element_type=f32,
        )
        return both[:64, :128] + both[:64, 128:]

    totals = [jnp.zeros((32, 128), f32) for _ in range(2)]
    for g in range(9):
        summed = sorted_sum(jnp.concatenate(
            [arrived_ref[pl.ds(4 * g + c, 64, stride=ROWS), :] for c in range(4)], axis=0))
        mine, theirs = own_ref[g], sib_ref[g]
        totals[0] = totals[0] + summed[:32] * jnp.where(is_low, mine, theirs)
        totals[1] = totals[1] + summed[32:] * jnp.where(is_low, theirs, mine)
    shifted = [tail] + [pltpu.roll(tail, 128 - 32 * c, 1) for c in range(1, 4)]
    ends = sorted_sum(jnp.concatenate([jnp.where(lane < 18, x, 0.0) for x in shifted], axis=0))
    own_edge, sib_edge = before_ref[0] + after_ref[0], before_ref[1] + after_ref[1]
    side = (ends[:32] * jnp.where(is_low, own_edge, sib_edge), ends[32:] * jnp.where(is_low, sib_edge, own_edge))
    out_ref[0] = totals[0]
    out_ref[1] = totals[1]
    for core in range(2):
        product = side[core]
        small = lax.broadcasted_iota(jnp.int32, (32, 128), 1)
        west = jnp.sum(jnp.where(small < 9, product, 0.0), axis=1, keepdims=True)
        east = jnp.sum(jnp.where((small >= 9) & (small < 18), product, 0.0), axis=1, keepdims=True)
        out_ref[2 + core] = jnp.where(small == 127, west, jnp.where(small == 0, east, 0.0))
    bottom = out_ref[0, pl.ds(0, 8, stride=4), :]
    top = out_ref[1, pl.ds(3, 8, stride=4), :]
    cross_ref[...] = jnp.where(is_low, bottom, top)
    diag_ref[...] = jnp.where(is_low, top, bottom)


def voxels(arrived, own, sib, before, after):
    f32 = jnp.float32
    return pl.pallas_call(
        voxel_kernel,
        out_shape=(
            jax.ShapeDtypeStruct((4, 32, 128), f32),
            jax.ShapeDtypeStruct((8, 128), f32),
            jax.ShapeDtypeStruct((8, 128), f32),
        ),
        compiler_params=GRANT,
        name="voxels",
    )(arrived, own, sib, before, after)


def smooth_kernel(mine_ref, theirs_ref, cross_ref, diag_ref, out_ref, full, framed):
    is_low = lax.axis_index("mer_2") == 0
    low = mine_ref[0] + theirs_ref[0]
    high = mine_ref[1] + theirs_ref[1]
    raw = jnp.where(is_low, low, high)
    ends = jnp.where(is_low, mine_ref[2] + theirs_ref[2], mine_ref[3] + theirs_ref[3])
    full[0] = low
    full[1] = high
    outer = cross_ref[...] + diag_ref[...]
    below = jnp.where(is_low, outer, full[0, pl.ds(3, 8, stride=4), :])
    above = jnp.where(is_low, full[1, pl.ds(0, 8, stride=4), :], outer)
    framed[0:8] = jnp.zeros((8, 128), jnp.float32)
    framed[8:40] = raw
    framed[40:48] = jnp.zeros((8, 128), jnp.float32)
    lane = lax.broadcasted_iota(jnp.int32, (32, 128), 1)
    row = lax.broadcasted_iota(jnp.int32, (32, 128), 0)
    west = pltpu.roll(jnp.where(lane == 127, ends, raw), 1, 1)
    east = pltpu.roll(jnp.where(lane == 0, ends, raw), 127, 1)
    neighbours = framed[4:36] + framed[12:44] + west + east
    down = jnp.where(row % 4 == 0, 0.0, framed[7:39])
    up = jnp.where(row % 4 == 3, 0.0, framed[9:41])
    neighbours = neighbours + down + up
    out_ref[...] = raw + smooth_rate * (neighbours - 6.0 * raw)
    out_ref[pl.ds(0, 8, stride=4), :] += smooth_rate * below
    out_ref[pl.ds(3, 8, stride=4), :] += smooth_rate * above


def smooth(mine, theirs, cross, diag):
    return pl.pallas_call(
        smooth_kernel,
        out_shape=jax.ShapeDtypeStruct((32, 128), jnp.float32),
        scratch_shapes=[pltpu.VMEM((2, 32, 128), jnp.float32), pltpu.VMEM((48, 128), jnp.float32)],
        compiler_params=GRANT,
        name="smooth",
    )(mine, theirs, cross, diag)


def on_device(
    displacement,
    velocity,
    modulus,
    hoop_strength,
    coupling,
    density,
    order_count,
    point_element,
    point_local,
    azimuth_scale,
    point_owner,
    point_cell,
    adjoint_strain,
):
    count = lax.axis_size(MER)
    az_count = lax.axis_size("az")
    swap = [(0, 1), (1, 0)]
    cross = [(c, c + 1) for c in range(1, count - 1, 2)] + [(c + 1, c) for c in range(1, count - 1, 2)]
    diagonal = [(c, c + 2) for c in range(0, count - 2, 2)] + [(c + 2, c) for c in range(1, count - 2, 2)]
    ahead = [(i, (i + 1) % az_count) for i in range(az_count)]

    own, up, down, points = pack(
        displacement.reshape(15, 8, 128), velocity.reshape(15, 8, 128),
        modulus, hoop_strength, coupling, density, order_count,
        point_element.T, point_local.T, azimuth_scale.reshape(1, 64), point_owner.reshape(1, 64),
        point_cell.reshape(1, 64),
    )
    sib = lax.ppermute(own, "mer_2", swap)
    outer = lax.ppermute(own, MER, cross)
    low = lax.ppermute(up, MER, [(i, i + 2) for i in range(count - 2)])
    high = lax.ppermute(down, MER, [(i + 2, i) for i in range(count - 2)])
    final, spread = march(own, sib, outer, low, high)

    weights = point_weights(points)
    nodes = lax.all_to_all(spread, "az", 0, 0, tiled=True)
    outgoing = messages(nodes, *weights)
    arrived = lax.all_to_all(outgoing.reshape(64, ROWS, 1, 128), SIDES, 0, 0, tiled=True)
    arrived = arrived.reshape(64 * ROWS, 128)

    adjoint = adjoint_strain.reshape(9, 32, 128)
    adjoint_sib = lax.ppermute(adjoint, "mer_2", swap)
    first, last = rims(adjoint, adjoint_sib)
    before = lax.ppermute(last, "az", ahead)
    after = lax.ppermute(first, "az", [(b, a) for a, b in ahead])
    part, near, far = voxels(arrived, adjoint, adjoint_sib, before, after)
    kernel = smooth(
        part, lax.ppermute(part, "mer_2", swap), lax.ppermute(near, MER, cross), lax.ppermute(far, MER, diagonal)
    )
    return final.reshape(3, 5, 8, 128), kernel.reshape(8, 4, 128)


def solution(mesh):
    torus = Mesh(mesh.devices.reshape(8, 8, 2, mesh.shape["az"]), ("mer_0", "mer_1", "mer_2", "az"))
    return jax.shard_map(
        on_device,
        mesh=torus,
        in_specs=(
            P(None, None, MER, "az"),
            P(None, None, MER, "az"),
            P(None, MER),
            P(None, MER),
            P(None, MER),
            P(None, MER),
            P(None, MER),
            P(MER, None),
            P(MER, None),
            P(MER),
            P(MER, None),
            P(MER),
            P(None, None, MER, "az"),
        ),
        out_specs=(P(None, None, MER, "az"), P(None, MER, "az")),
        check_vma=False,
    )
```

time: 113 us -> 98.1 us (0.87)
  the two profiles are of different devices: /device:TPU:1 before, /device:TPU:64 now
where the time goes in v2:
time: 98.1 us; the launch traced here: 97.5 us
  starting transfers between devices  47.1 us (48%)
  waiting for transfers between devices  39.4 us (40%)
  Pallas kernels  8.63 us (9%)
  local copies, waits for them, and re-layouts  1.59 us (2%)
    all_to_all x1, waiting for transfers between devices, on_device(): lax.all_to_all(outgoing.reshape(64, ROWS, 1, 128), SIDES, 0, 0, tiled=True)  20.2 us
    all_to_all x1, starting transfers between devices, on_device(): lax.all_to_all(outgoing.reshape(64, ROWS, 1, 128), SIDES, 0, 0, tiled=True)  13.2 us
    ppermute x1, waiting for transfers between devices, on_device(): low = lax.ppermute(up, MER, [(i, i + 2) for i in range(count - 2)])  5.58 us
    ppermute x1, waiting for transfers between devices, on_device(): lax.ppermute(far, MER, diagonal)  5.08 us
    all_to_all x1, waiting for transfers between devices, on_device(): nodes = lax.all_to_all(spread, 'az', 0, 0, tiled=True)  5 us
    ppermute x1, starting transfers between devices, on_device(): after = lax.ppermute(first, 'az', [(b, a) for a, b in ahead])  4.58 us
    ppermute x1, starting transfers between devices, on_device(): outer = lax.ppermute(own, MER, cross)  4.57 us
    ppermute x1, starting transfers between devices, on_device(): lax.ppermute(near, MER, cross)  4.49 us
  transfers between devices with their start and end apart: 12, of which 7 were waited for; matrix products, arithmetic and copies ran while one was open for 0% of the time, Pallas kernels for 1%

profile of v2, /device:TPU:64, one launch (start us, length us, event | category | flops | bytes accessed | tf_op | source)
XLA Modules:
  0.0 97.5 jit_solution(5358129854122792254)
XLA Ops:
  0.6 0.0 copy-start
  0.6 1.8 %pack.1 = (f32[32,8,128]{2,1,0:T(8,128)}, f32[9,8,128]{2,1,0:T(8,128)}, f32[16,8,128]{2,1,0:T(8,128)}, f32[8,128]{1,0:T(8,128)}) custom-call(f32[15,8,128]{2,1,0:T(8,128)} %bitcast.16, f32[15,8,128]{2,1,0:T(8,128)} %bitcast.17, f32[1,2]{1,0:T(1,128)} %refs_2_.1, f32[1,2]{1,0:T(1,128)} %refs_3_.1, f32[1,2]{1,0:T(1,128)} %refs_4_.1, f32[1,2]{1,0:T(1,128)} %refs_5_.1, ...), custom_call_target="tpu_custom_call" | custom-call | tf_op jit(solution)/shard_map/pack/pallas_call | solution.py:144
  2.5 1.9 %collective-permute-start = (f32[32,8,128]{2,1,0:T(8,128)}, f32[32,8,128]{2,1,0:T(8,128)S(1)}, u32[]{:S(2)}, u32[]{:S(2)}) collective-permute-start(f32[32,8,128]{2,1,0:T(8,128)} %get-tuple-element.16.own_ref), channel_id=1, source_target_pairs={{0,4},{4,0},{1,5},{5,1},{2,6},{6,2},{3,7},{7,3},{8,12},{12,8},{9,1... | collective-permute-start | bytes 393224 | tf_op jit(solution)/shard_map/ppermute | solution.py:572
  4.4 4.6 %collective-permute-start.1 = (f32[32,8,128]{2,1,0:T(8,128)}, f32[32,8,128]{2,1,0:T(8,128)S(1)}, u32[]{:S(2)}, u32[]{:S(2)}) collective-permute-start(f32[32,8,128]{2,1,0:T(8,128)} %get-tuple-element.16.own_ref), channel_id=1, source_target_pairs={{4,8},{12,16},{20,24},{28,32},{36,40},{44,48},{52,56},{60,64},{68,... | collective-permute-start | bytes 393224 | tf_op jit(solution)/shard_map/ppermute | solution.py:573
  9.0 3.3 %collective-permute-start.3 = (f32[16,8,128]{2,1,0:T(8,128)}, f32[16,8,128]{2,1,0:T(8,128)S(1)}, u32[]{:S(2)}, u32[]{:S(2)}) collective-permute-start(f32[16,8,128]{2,1,0:T(8,128)} %get-tuple-element.18), channel_id=1, source_target_pairs={{8,0},{12,4},{16,8},{20,12},{24,16},{28,20},{32,24},{36,28},{40,32... | collective-permute-start | bytes 196616 | tf_op jit(solution)/shard_map/ppermute | solution.py:575
  12.2 2.6 %collective-permute-start.2 = (f32[9,8,128]{2,1,0:T(8,128)}, f32[9,8,128]{2,1,0:T(8,128)S(1)}, u32[]{:S(2)}, u32[]{:S(2)}) collective-permute-start(f32[9,8,128]{2,1,0:T(8,128)} %get-tuple-element.17), channel_id=1, source_target_pairs={{0,8},{4,12},{8,16},{12,20},{16,24},{20,28},{24,32},{28,36},{32,40... | collective-permute-start | bytes 110600 | tf_op jit(solution)/shard_map/ppermute | solution.py:574
  14.8 5.6 %collective-permute-done.2.low_ref = f32[9,8,128]{2,1,0:T(8,128)S(1)} collective-permute-done((f32[9,8,128]{2,1,0:T(8,128)}, f32[9,8,128]{2,1,0:T(8,128)S(1)}, u32[]{:S(2)}, u32[]{:S(2)}) %collective-permute-start.2) | collective-permute-done | bytes 36896 | tf_op jit(solution)/shard_map/ppermute | solution.py:574
  20.4 0.0 collective-permute-done.3.high_ref
  20.4 0.0 collective-permute-done.sib_ref
  20.4 0.0 collective-permute-done.1.cross_ref
  20.4 0.0 copy-start.2
  20.4 0.9 copy-done.2
  21.3 1.8 %march.1 = (f32[15,8,128]{2,1,0:T(8,128)}, f32[4,17,8,128]{3,2,1,0:T(8,128)}) custom-call(f32[32,8,128]{2,1,0:T(8,128)S(1)} %copy-done.2, f32[32,8,128]{2,1,0:T(8,128)S(1)} %collective-permute-done.sib_ref, f32[32,8,128]{2,1,0:T(8,128)S(1)} %collective-permute-done.1.cross_ref, f32[9,8,128]{2,1,0:T(8,128)S(1)} %collective-permute-done.2.low_ref, ...), custom_call_target="tpu_custom_call" | custom-call | tf_op jit(solution)/shard_map/march/pallas_call | solution.py:276
  23.2 4.3 %all-to-all-start = ((f32[4,17,8,128]{3,2,1,0:T(8,128)}), f32[4,17,8,128]{3,2,1,0:T(8,128)S(1)}, u32[]{:S(2)}, u32[]{:S(2)}) async-start(f32[4,17,8,128]{3,2,1,0:T(8,128)} %get-tuple-element.20), calls=%async_computation | async-start | bytes 557056 | tf_op jit(solution)/shard_map/all_to_all | solution.py:579
  27.4 0.0 copy-done
  27.4 0.0 copy-start.3
  27.4 0.7 copy-done.3
  28.1 1.1 %weights.1 = (bf16[6,256,256]{2,1,0:T(8,128)(2,1)S(1)}, bf16[2,256,256]{2,1,0:T(8,128)(2,1)S(1)}, bf16[2,512,384]{2,1,0:T(8,128)(2,1)S(1)}) custom-call(f32[8,128]{1,0:T(8,128)S(1)} %copy-done.3, f32[1040,256]{1,0:T(8,128)S(1)} %copy-done), custom_call_target="tpu_custom_call" | custom-call | tf_op jit(solution)/shard_map/weights/pallas_call | solution.py:366
  29.2 5.0 %all-to-all-done.nodes_ref = f32[4,17,8,128]{3,2,1,0:T(8,128)S(1)} async-done(((f32[4,17,8,128]{3,2,1,0:T(8,128)}), f32[4,17,8,128]{3,2,1,0:T(8,128)S(1)}, u32[]{:S(2)}, u32[]{:S(2)}) %all-to-all-start) | async-done | bytes 278560 | tf_op jit(solution)/shard_map/all_to_all | solution.py:579
  34.2 2.4 %messages.1 = f32[2368,128]{1,0:T(8,128)} custom-call(f32[4,17,8,128]{3,2,1,0:T(8,128)S(1)} %all-to-all-done.nodes_ref, bf16[6,256,256]{2,1,0:T(8,128)(2,1)S(1)} %get-tuple-element.22.weight_ref, bf16[2,256,256]{2,1,0:T(8,128)(2,1)S(1)} %get-tuple-element.23.point_ref, bf16[2,512,384]{2,1,0:T(8,128)(2,1)S(1)} %get-tuple-element.24.basis_ref), custom_call_target="tpu_custom_call" | custom-call | tf_op jit(solution)/shard_map/messages/pallas_call | solution.py:419
  36.6 0.0 copy-start.1
  36.6 13.2 %all-to-all-start.1 = ((f32[64,37,1,128]{3,2,1,0:T(1,128)}), f32[64,37,1,128]{3,2,1,0:T(1,128)S(1)}, u32[]{:S(2)}, u32[]{:S(2)}) async-start(f32[64,37,1,128]{3,2,1,0:T(1,128)} %bitcast.8), calls=%async_computation.1 | async-start | bytes 2424832 | tf_op jit(solution)/shard_map/all_to_all | solution.py:581
  49.8 0.0 copy-done.1
  49.8 1.9 %collective-permute-start.4 = (f32[9,32,128]{2,1,0:T(8,128)S(1)}, f32[9,32,128]{2,1,0:T(8,128)S(1)}, u32[]{:S(2)}, u32[]{:S(2)}) collective-permute-start(f32[9,32,128]{2,1,0:T(8,128)S(1)} %bitcast.13), channel_id=1, source_target_pairs={{0,4},{4,0},{1,5},{5,1},{2,6},{6,2},{3,7},{7,3},{8,12},{12,8},{9,1... | collective-permute-start | bytes 442376 | tf_op jit(solution)/shard_map/ppermute | solution.py:585
  51.8 1.3 %collective-permute-done.4.sib_ref = f32[9,32,128]{2,1,0:T(8,128)S(1)} collective-permute-done((f32[9,32,128]{2,1,0:T(8,128)S(1)}, f32[9,32,128]{2,1,0:T(8,128)S(1)}, u32[]{:S(2)}, u32[]{:S(2)}) %collective-permute-start.4) | collective-permute-done | bytes 147488 | tf_op jit(solution)/shard_map/ppermute | solution.py:585
  53.1 0.3 rims.1
  53.4 2.5 %collective-permute-start.5 = (f32[2,32,128]{2,1,0:T(8,128)S(1)}, f32[2,32,128]{2,1,0:T(8,128)S(1)}, u32[]{:S(2)}, u32[]{:S(2)}) collective-permute-start(f32[2,32,128]{2,1,0:T(8,128)S(1)} %get-tuple-element.25), channel_id=1, source_target_pairs={{0,1},{1,2},{2,3},{3,0},{4,5},{5,6},{6,7},{7,4},{8,9},{9,10},{10,1... | collective-permute-start | bytes 98312 | tf_op jit(solution)/shard_map/ppermute | solution.py:587
  55.8 4.6 %collective-permute-start.6 = (f32[2,32,128]{2,1,0:T(8,128)S(1)}, f32[2,32,128]{2,1,0:T(8,128)S(1)}, u32[]{:S(2)}, u32[]{:S(2)}) collective-permute-start(f32[2,32,128]{2,1,0:T(8,128)S(1)} %get-tuple-element.26), channel_id=1, source_target_pairs={{1,0},{2,1},{3,2},{0,3},{5,4},{6,5},{7,6},{4,7},{9,8},{10,9},{11,1... | collective-permute-start | bytes 98312 | tf_op jit(solution)/shard_map/ppermute | solution.py:588
  60.4 0.0 collective-permute-done.5.before_ref
  60.4 1.6 %collective-permute-done.6.after_ref = f32[2,32,128]{2,1,0:T(8,128)S(1)} collective-permute-done((f32[2,32,128]{2,1,0:T(8,128)S(1)}, f32[2,32,128]{2,1,0:T(8,128)S(1)}, u32[]{:S(2)}, u32[]{:S(2)}) %collective-permute-start.6) | collective-permute-done | bytes 32800 | tf_op jit(solution)/shard_map/ppermute | solution.py:588
  62.0 20.2 %all-to-all-done.1 = f32[64,37,1,128]{3,2,1,0:T(1,128)S(1)} async-done(((f32[64,37,1,128]{3,2,1,0:T(1,128)}), f32[64,37,1,128]{3,2,1,0:T(1,128)S(1)}, u32[]{:S(2)}, u32[]{:S(2)}) %all-to-all-start.1) | async-done | bytes 1212448 | tf_op jit(solution)/shard_map/all_to_all | solution.py:581
  82.2 0.5 voxels.1
  82.7 1.9 %collective-permute-start.7 = (f32[4,32,128]{2,1,0:T(8,128)S(1)}, f32[4,32,128]{2,1,0:T(8,128)S(1)}, u32[]{:S(2)}, u32[]{:S(2)}) collective-permute-start(f32[4,32,128]{2,1,0:T(8,128)S(1)} %get-tuple-element.27.mine_ref), channel_id=1, source_target_pairs={{0,4},{4,0},{1,5},{5,1},{2,6},{6,2},{3,7},{7,3},{8,12},{12,8},{9,1... | collective-permute-start | bytes 196616 | tf_op jit(solution)/shard_map/ppermute | solution.py:591
  84.7 4.5 %collective-permute-start.8 = (f32[8,128]{1,0:T(8,128)S(1)}, f32[8,128]{1,0:T(8,128)S(1)}, u32[]{:S(2)}, u32[]{:S(2)}) collective-permute-start(f32[8,128]{1,0:T(8,128)S(1)} %get-tuple-element.28), channel_id=1, source_target_pairs={{4,8},{12,16},{20,24},{28,32},{36,40},{44,48},{52,56},{60,64},{68,... | collective-permute-start | bytes 12296 | tf_op jit(solution)/shard_map/ppermute | solution.py:591
  89.2 1.9 %collective-permute-start.9 = (f32[8,128]{1,0:T(8,128)S(1)}, f32[8,128]{1,0:T(8,128)S(1)}, u32[]{:S(2)}, u32[]{:S(2)}) collective-permute-start(f32[8,128]{1,0:T(8,128)S(1)} %get-tuple-element.29), channel_id=1, source_target_pairs={{0,8},{8,16},{16,24},{24,32},{32,40},{40,48},{48,56},{56,64},{64,7... | collective-permute-start | bytes 12296 | tf_op jit(solution)/shard_map/ppermute | solution.py:591
  91.1 0.6 collective-permute-done.8.cross_ref
  91.7 5.1 %collective-permute-done.9.diag_ref = f32[8,128]{1,0:T(8,128)S(1)} collective-permute-done((f32[8,128]{1,0:T(8,128)S(1)}, f32[8,128]{1,0:T(8,128)S(1)}, u32[]{:S(2)}, u32[]{:S(2)}) %collective-permute-start.9) | collective-permute-done | bytes 4128 | tf_op jit(solution)/shard_map/ppermute | solution.py:591
  96.8 0.0 collective-permute-done.7.theirs_ref
  96.8 0.7 smooth.1
Async XLA Ops:
  0.6 26.8 %copy-start = (f32[1040,256]{1,0:T(8,128)S(1)}, f32[1040,256]{1,0:T(8,128)}, u32[]{:S(2)}) copy-start(f32[1040,256]{1,0:T(8,128)} %constant.2.clone.table_ref) | copy-start | bytes 3194884
  2.5 17.9 %collective-permute-start = (f32[32,8,128]{2,1,0:T(8,128)}, f32[32,8,128]{2,1,0:T(8,128)S(1)}, u32[]{:S(2)}, u32[]{:S(2)}) collective-permute-start(f32[32,8,128]{2,1,0:T(8,128)} %get-tuple-element.16.own_ref), channel_id=1, source_target_pairs={{0,4},{4,0},{1,5},{5,1},{2,6},{6,2},{3,7},{7,3},{8,12},{12,8},{9,1... | collective-permute-start | bytes 393224 | tf_op jit(solution)/shard_map/ppermute | solution.py:572
  4.4 16.0 %collective-permute-start.1 = (f32[32,8,128]{2,1,0:T(8,128)}, f32[32,8,128]{2,1,0:T(8,128)S(1)}, u32[]{:S(2)}, u32[]{:S(2)}) collective-permute-start(f32[32,8,128]{2,1,0:T(8,128)} %get-tuple-element.16.own_ref), channel_id=1, source_target_pairs={{4,8},{12,16},{20,24},{28,32},{36,40},{44,48},{52,56},{60,64},{68,... | collective-permute-start | bytes 393224 | tf_op jit(solution)/shard_map/ppermute | solution.py:573
  9.0 11.4 %collective-permute-start.3 = (f32[16,8,128]{2,1,0:T(8,128)}, f32[16,8,128]{2,1,0:T(8,128)S(1)}, u32[]{:S(2)}, u32[]{:S(2)}) collective-permute-start(f32[16,8,128]{2,1,0:T(8,128)} %get-tuple-element.18), channel_id=1, source_target_pairs={{8,0},{12,4},{16,8},{20,12},{24,16},{28,20},{32,24},{36,28},{40,32... | collective-permute-start | bytes 196616 | tf_op jit(solution)/shard_map/ppermute | solution.py:575
  12.2 8.2 %collective-permute-start.2 = (f32[9,8,128]{2,1,0:T(8,128)}, f32[9,8,128]{2,1,0:T(8,128)S(1)}, u32[]{:S(2)}, u32[]{:S(2)}) collective-permute-start(f32[9,8,128]{2,1,0:T(8,128)} %get-tuple-element.17), channel_id=1, source_target_pairs={{0,8},{4,12},{8,16},{12,20},{16,24},{20,28},{24,32},{28,36},{32,40... | collective-permute-start | bytes 110600 | tf_op jit(solution)/shard_map/ppermute | solution.py:574
  20.4 0.9 copy-start.2
  23.2 11.1 %all-to-all-start = ((f32[4,17,8,128]{3,2,1,0:T(8,128)}), f32[4,17,8,128]{3,2,1,0:T(8,128)S(1)}, u32[]{:S(2)}, u32[]{:S(2)}) async-start(f32[4,17,8,128]{3,2,1,0:T(8,128)} %get-tuple-element.20), calls=%async_computation | async-start | bytes 557056 | tf_op jit(solution)/shard_map/all_to_all | solution.py:579
  27.4 0.7 copy-start.3
  36.6 13.2 %copy-start.1 = (f32[9,8,4,128]{3,2,1,0:T(4,128)S(1)}, f32[9,8,4,128]{3,2,1,0:T(4,128)}, u32[]{:S(2)}) copy-start(f32[9,8,4,128]{3,2,1,0:T(4,128)} %param.26) | copy-start | bytes 442372
  36.6 45.6 %all-to-all-start.1 = ((f32[64,37,1,128]{3,2,1,0:T(1,128)}), f32[64,37,1,128]{3,2,1,0:T(1,128)S(1)}, u32[]{:S(2)}, u32[]{:S(2)}) async-start(f32[64,37,1,128]{3,2,1,0:T(1,128)} %bitcast.8), calls=%async_computation.1 | async-start | bytes 2424832 | tf_op jit(solution)/shard_map/all_to_all | solution.py:581
  49.8 3.3 %collective-permute-start.4 = (f32[9,32,128]{2,1,0:T(8,128)S(1)}, f32[9,32,128]{2,1,0:T(8,128)S(1)}, u32[]{:S(2)}, u32[]{:S(2)}) collective-permute-start(f32[9,32,128]{2,1,0:T(8,128)S(1)} %bitcast.13), channel_id=1, source_target_pairs={{0,4},{4,0},{1,5},{5,1},{2,6},{6,2},{3,7},{7,3},{8,12},{12,8},{9,1... | collective-permute-start | bytes 442376 | tf_op jit(solution)/shard_map/ppermute | solution.py:585
  53.4 7.1 %collective-permute-start.5 = (f32[2,32,128]{2,1,0:T(8,128)S(1)}, f32[2,32,128]{2,1,0:T(8,128)S(1)}, u32[]{:S(2)}, u32[]{:S(2)}) collective-permute-start(f32[2,32,128]{2,1,0:T(8,128)S(1)} %get-tuple-element.25), channel_id=1, source_target_pairs={{0,1},{1,2},{2,3},{3,0},{4,5},{5,6},{6,7},{7,4},{8,9},{9,10},{10,1... | collective-permute-start | bytes 98312 | tf_op jit(solution)/shard_map/ppermute | solution.py:587
  55.8 6.2 %collective-permute-start.6 = (f32[2,32,128]{2,1,0:T(8,128)S(1)}, f32[2,32,128]{2,1,0:T(8,128)S(1)}, u32[]{:S(2)}, u32[]{:S(2)}) collective-permute-start(f32[2,32,128]{2,1,0:T(8,128)S(1)} %get-tuple-element.26), channel_id=1, source_target_pairs={{1,0},{2,1},{3,2},{0,3},{5,4},{6,5},{7,6},{4,7},{9,8},{10,9},{11,1... | collective-permute-start | bytes 98312 | tf_op jit(solution)/shard_map/ppermute | solution.py:588
  82.7 14.0 %collective-permute-start.7 = (f32[4,32,128]{2,1,0:T(8,128)S(1)}, f32[4,32,128]{2,1,0:T(8,128)S(1)}, u32[]{:S(2)}, u32[]{:S(2)}) collective-permute-start(f32[4,32,128]{2,1,0:T(8,128)S(1)} %get-tuple-element.27.mine_ref), channel_id=1, source_target_pairs={{0,4},{4,0},{1,5},{5,1},{2,6},{6,2},{3,7},{7,3},{8,12},{12,8},{9,1... | collective-permute-start | bytes 196616 | tf_op jit(solution)/shard_map/ppermute | solution.py:591
  84.7 7.0 %collective-permute-start.8 = (f32[8,128]{1,0:T(8,128)S(1)}, f32[8,128]{1,0:T(8,128)S(1)}, u32[]{:S(2)}, u32[]{:S(2)}) collective-permute-start(f32[8,128]{1,0:T(8,128)S(1)} %get-tuple-element.28), channel_id=1, source_target_pairs={{4,8},{12,16},{20,24},{28,32},{36,40},{44,48},{52,56},{60,64},{68,... | collective-permute-start | bytes 12296 | tf_op jit(solution)/shard_map/ppermute | solution.py:591
  89.2 7.6 %collective-permute-start.9 = (f32[8,128]{1,0:T(8,128)S(1)}, f32[8,128]{1,0:T(8,128)S(1)}, u32[]{:S(2)}, u32[]{:S(2)}) collective-permute-start(f32[8,128]{1,0:T(8,128)S(1)} %get-tuple-element.29), channel_id=1, source_target_pairs={{0,8},{8,16},{16,24},{24,32},{32,40},{40,48},{48,56},{56,64},{64,7... | collective-permute-start | bytes 12296 | tf_op jit(solution)/shard_map/ppermute | solution.py:591

commit v3 on v2

--- a/solution.py
+++ b/solution.py
@@ -103,34 +103,23 @@
 
 
 def pack_kernel(*refs):
-    sources, (own_ref, up_ref, down_ref, points_ref) = refs[:12], refs[12:16]
-    scratch, arrived = refs[16:28], refs[28]
+    sources, (own_ref, points_ref) = refs[:12], refs[12:14]
+    scratch, arrived = refs[14:26], refs[26]
     copies = fetch(list(zip(sources, scratch)), arrived)
     u_ref, v_ref = scratch[:2]
     element_ref, local_ref, scale_ref, owner_ref, cell_ref = scratch[7:]
     f32 = jnp.float32
     own_ref[30:32] = jnp.zeros((2, 8, 128), f32)
-    up_ref[7] = jnp.zeros((8, 128), f32)
-    up_ref[8] = jnp.zeros((8, 128), f32)
-    down_ref[15] = jnp.zeros((8, 128), f32)
     points_ref[...] = jnp.zeros((8, 128), f32)
     for copy in copies:
         copy.wait()
     for i in range(15):
-        u, v = u_ref[i], v_ref[i]
-        own_ref[i] = u
-        own_ref[15 + i] = v
-        up_ref[i // 2, 4 * (i % 2):4 * (i % 2) + 4, :] = u_ref[i, 4:8, :]
-        down_ref[i] = u
-        down_ref[i, 5:6, :] = v_ref[i, 0:1, :]
+        own_ref[i] = u_ref[i]
+        own_ref[15 + i] = v_ref[i]
     for i, ref in enumerate(scratch[2:7]):
         both = ref[...].astype(f32)
-        first = jnp.broadcast_to(both[:, 0:1], (1, 128))
-        second = jnp.broadcast_to(both[:, 1:2], (1, 128))
-        own_ref[30, i:i + 1, :] = first
-        own_ref[31, i:i + 1, :] = second
-        down_ref[15, i:i + 1, :] = first
-        up_ref[8, i:i + 1, :] = second
+        own_ref[30, i:i + 1, :] = jnp.broadcast_to(both[:, 0:1], (1, 128))
+        own_ref[31, i:i + 1, :] = jnp.broadcast_to(both[:, 1:2], (1, 128))
     points_ref[0:2, 0:64] = local_ref[...]
     points_ref[2:3, 0:64] = (element_ref[1:2, :] % 2).astype(f32)
     points_ref[3:4, 0:64] = scale_ref[...]
@@ -144,19 +133,49 @@
     return pl.pallas_call(
         pack_kernel,
         in_specs=[hbm] * 12,
-        out_specs=(vmem, vmem, vmem, vmem),
+        out_specs=(vmem, vmem),
         scratch_shapes=[pltpu.VMEM(a.shape, a.dtype) for a in arrays] + [pltpu.SemaphoreType.DMA((12,))],
         out_shape=(
             jax.ShapeDtypeStruct((32, 8, 128), f32),
-            jax.ShapeDtypeStruct((9, 8, 128), f32),
-            jax.ShapeDtypeStruct((16, 8, 128), f32),
             jax.ShapeDtypeStruct((8, 128), f32),
         ),
         name="pack",
     )(*arrays)
 
 
-def step_kernel(own_ref, sib_ref, cross_ref, low_ref, high_ref, u_ref, gather_ref,
+def near_columns(target, first, source, upward):
+    row = lax.broadcasted_iota(jnp.int32, (8, 128), 0)
+    for i in range(15):
+        u, v = source[i], source[15 + i]
+        start = jnp.broadcast_to(v[0:1, :], (8, 128))
+        target[first + i] = jnp.where((row == 5) & jnp.logical_not(upward), start, u)
+    target[first + 15] = jnp.where(upward, source[31], source[30])
+
+
+def chip_kernel(own_ref, sib_ref, out_ref):
+    out_ref[0:32] = own_ref[...]
+    near_columns(out_ref, 32, sib_ref, lax.axis_index("mer_2") == 1)
+
+
+def forward_kernel(cross_ref, out_ref):
+    near_columns(out_ref, 0, cross_ref, lax.axis_index("mer_2") == 0)
+
+
+def chip_message(own, sib):
+    return pl.pallas_call(
+        chip_kernel, out_shape=jax.ShapeDtypeStruct((48, 8, 128), jnp.float32),
+        compiler_params=GRANT, name="chip",
+    )(own, sib)
+
+
+def forward_message(cross):
+    return pl.pallas_call(
+        forward_kernel, out_shape=jax.ShapeDtypeStruct((16, 8, 128), jnp.float32),
+        compiler_params=GRANT, name="forward",
+    )(cross)
+
+
+def step_kernel(own_ref, sib_ref, cross_ref, forward_ref, u_ref, gather_ref,
                 ucol, vcol, coef, state, field):
     core, az = lax.axis_index("mer_2"), lax.axis_index("az")
     is_low = core == 0
@@ -167,23 +186,28 @@
     def right(i):
         return jnp.where(is_low, sib_ref[i], cross_ref[i])
 
-    zero4 = jnp.zeros((4, 128), jnp.float32)
+    def far_left(i):
+        return jnp.where(is_low, cross_ref[32 + i], forward_ref[i])
+
+    def far_right(i):
+        return jnp.where(is_low, forward_ref[i], cross_ref[32 + i])
+
     zero8 = jnp.zeros((8, 128), jnp.float32)
     for i in range(15):
-        ucol[i, 0:8, :] = zero8
-        ucol[i, 4:8, :] = low_ref[i // 2, 4 * (i % 2):4 * (i % 2) + 4, :]
+        ucol[i, 0:8, :] = far_left(i)
         ucol[i, 8:16, :] = left(i)
         ucol[i, 16:24, :] = own_ref[i]
         ucol[i, 24:32, :] = right(i)
-        ucol[i, 32:40, :] = high_ref[i]
+        high = far_right(i)
+        ucol[i, 32:40, :] = high
         vcol[i, 0:8, :] = zero8
         vcol[i, 8:16, :] = left(15 + i)
         vcol[i, 16:24, :] = own_ref[15 + i]
         vcol[i, 24:32, :] = right(15 + i)
         vcol[i, 32:40, :] = zero8
-        vcol[i, 32:33, :] = high_ref[i, 5:6, :]
+        vcol[i, 32:33, :] = high[5:6, :]
     l0, l1, r0, r1 = left(30), left(31), right(30), right(31)
-    sources = (low_ref[8], l0, l1, own_ref[30], own_ref[31], r0, r1, high_ref[15])
+    sources = (far_left(15), l0, l1, own_ref[30], own_ref[31], r0, r1, far_right(15))
     for i in range(5):
         for e, tile in enumerate(sources):
             coef[i, e:e + 1, :] = tile[i:i + 1, :]
@@ -270,12 +294,12 @@
             gather_ref[q, 15 + i // 8, i % 8:i % 8 + 1, :] = rim
 
 
-def march(own, sib, cross, low, high):
+def march(own, sib, cross, forward):
     f32 = jnp.float32
     vmem = pl.BlockSpec(memory_space=pltpu.VMEM)
     return pl.pallas_call(
         step_kernel,
-        in_specs=[vmem] * 5,
+        in_specs=[vmem] * 4,
         out_specs=(vmem, vmem),
         out_shape=(
             jax.ShapeDtypeStruct((15, 8, 128), f32),
@@ -290,7 +314,7 @@
         ],
         compiler_params=GRANT,
         name="march",
-    )(own, sib, cross, low, high)
+    )(own, sib, cross, forward)
 
 
 def weight_kernel(points_ref, table_ref, weight_ref, point_ref, basis_ref):
@@ -443,7 +467,7 @@
     )(own, sib)
 
 
-def voxel_kernel(arrived_ref, own_ref, sib_ref, before_ref, after_ref, out_ref, cross_ref, diag_ref):
+def voxel_kernel(arrived_ref, own_ref, sib_ref, before_ref, after_ref, out_ref):
     is_low = lax.axis_index("mer_2") == 0
     f32 = jnp.float32
     tail = arrived_ref[pl.ds(36, 64, stride=ROWS), :]
@@ -484,27 +508,19 @@
         west = jnp.sum(jnp.where(small < 9, product, 0.0), axis=1, keepdims=True)
         east = jnp.sum(jnp.where((small >= 9) & (small < 18), product, 0.0), axis=1, keepdims=True)
         out_ref[2 + core] = jnp.where(small == 127, west, jnp.where(small == 0, east, 0.0))
-    bottom = out_ref[0, pl.ds(0, 8, stride=4), :]
-    top = out_ref[1, pl.ds(3, 8, stride=4), :]
-    cross_ref[...] = jnp.where(is_low, bottom, top)
-    diag_ref[...] = jnp.where(is_low, top, bottom)
 
 
 def voxels(arrived, own, sib, before, after):
     f32 = jnp.float32
     return pl.pallas_call(
         voxel_kernel,
-        out_shape=(
-            jax.ShapeDtypeStruct((4, 32, 128), f32),
-            jax.ShapeDtypeStruct((8, 128), f32),
-            jax.ShapeDtypeStruct((8, 128), f32),
-        ),
+        out_shape=jax.ShapeDtypeStruct((4, 32, 128), f32),
         compiler_params=GRANT,
         name="voxels",
     )(arrived, own, sib, before, after)
 
 
-def smooth_kernel(mine_ref, theirs_ref, cross_ref, diag_ref, out_ref, full, framed):
+def total_kernel(mine_ref, theirs_ref, base_ref, edge_ref, full, framed):
     is_low = lax.axis_index("mer_2") == 0
     low = mine_ref[0] + theirs_ref[0]
     high = mine_ref[1] + theirs_ref[1]
@@ -512,9 +528,9 @@
     ends = jnp.where(is_low, mine_ref[2] + theirs_ref[2], mine_ref[3] + theirs_ref[3])
     full[0] = low
     full[1] = high
-    outer = cross_ref[...] + diag_ref[...]
-    below = jnp.where(is_low, outer, full[0, pl.ds(3, 8, stride=4), :])
-    above = jnp.where(is_low, full[1, pl.ds(0, 8, stride=4), :], outer)
+    low_first, low_last = full[0, pl.ds(0, 8, stride=4), :], full[0, pl.ds(3, 8, stride=4), :]
+    high_first, high_last = full[1, pl.ds(0, 8, stride=4), :], full[1, pl.ds(3, 8, stride=4), :]
+    edge_ref[...] = jnp.where(is_low, low_first, high_last)
     framed[0:8] = jnp.zeros((8, 128), jnp.float32)
     framed[8:40] = raw
     framed[40:48] = jnp.zeros((8, 128), jnp.float32)
@@ -526,19 +542,37 @@
     down = jnp.where(row % 4 == 0, 0.0, framed[7:39])
     up = jnp.where(row % 4 == 3, 0.0, framed[9:41])
     neighbours = neighbours + down + up
-    out_ref[...] = raw + smooth_rate * (neighbours - 6.0 * raw)
-    out_ref[pl.ds(0, 8, stride=4), :] += smooth_rate * below
-    out_ref[pl.ds(3, 8, stride=4), :] += smooth_rate * above
-
-
-def smooth(mine, theirs, cross, diag):
+    base_ref[...] = raw + smooth_rate * (neighbours - 6.0 * raw)
+    base_ref[pl.ds(0, 8, stride=4), :] += jnp.where(is_low, 0.0, smooth_rate * low_last)
+    base_ref[pl.ds(3, 8, stride=4), :] += jnp.where(is_low, smooth_rate * high_first, 0.0)
+
+
+def total(mine, theirs):
+    f32 = jnp.float32
+    return pl.pallas_call(
+        total_kernel,
+        out_shape=(jax.ShapeDtypeStruct((32, 128), f32), jax.ShapeDtypeStruct((8, 128), f32)),
+        scratch_shapes=[pltpu.VMEM((2, 32, 128), f32), pltpu.VMEM((48, 128), f32)],
+        compiler_params=GRANT,
+        name="total",
+    )(mine, theirs)
+
+
+def smooth_kernel(base_ref, outer_ref, out_ref):
+    is_low = lax.axis_index("mer_2") == 0
+    outer = smooth_rate * outer_ref[...]
+    out_ref[...] = base_ref[...]
+    out_ref[pl.ds(0, 8, stride=4), :] += jnp.where(is_low, outer, 0.0)
+    out_ref[pl.ds(3, 8, stride=4), :] += jnp.where(is_low, 0.0, outer)
+
+
+def smooth(base, outer):
     return pl.pallas_call(
         smooth_kernel,
         out_shape=jax.ShapeDtypeStruct((32, 128), jnp.float32),
-        scratch_shapes=[pltpu.VMEM((2, 32, 128), jnp.float32), pltpu.VMEM((48, 128), jnp.float32)],
         compiler_params=GRANT,
         name="smooth",
-    )(mine, theirs, cross, diag)
+    )(base, outer)
 
 
 def on_device(
@@ -560,20 +594,18 @@
     az_count = lax.axis_size("az")
     swap = [(0, 1), (1, 0)]
     cross = [(c, c + 1) for c in range(1, count - 1, 2)] + [(c + 1, c) for c in range(1, count - 1, 2)]
-    diagonal = [(c, c + 2) for c in range(0, count - 2, 2)] + [(c + 2, c) for c in range(1, count - 2, 2)]
     ahead = [(i, (i + 1) % az_count) for i in range(az_count)]
 
-    own, up, down, points = pack(
+    own, points = pack(
         displacement.reshape(15, 8, 128), velocity.reshape(15, 8, 128),
         modulus, hoop_strength, coupling, density, order_count,
         point_element.T, point_local.T, azimuth_scale.reshape(1, 64), point_owner.reshape(1, 64),
         point_cell.reshape(1, 64),
     )
     sib = lax.ppermute(own, "mer_2", swap)
-    outer = lax.ppermute(own, MER, cross)
-    low = lax.ppermute(up, MER, [(i, i + 2) for i in range(count - 2)])
-    high = lax.ppermute(down, MER, [(i + 2, i) for i in range(count - 2)])
-    final, spread = march(own, sib, outer, low, high)
+    outer = lax.ppermute(chip_message(own, sib), MER, cross)
+    forward = lax.ppermute(forward_message(outer), "mer_2", swap)
+    final, spread = march(own, sib, outer, forward)
 
     weights = point_weights(points)
     nodes = lax.all_to_all(spread, "az", 0, 0, tiled=True)
@@ -586,10 +618,9 @@
     first, last = rims(adjoint, adjoint_sib)
     before = lax.ppermute(last, "az", ahead)
     after = lax.ppermute(first, "az", [(b, a) for a, b in ahead])
-    part, near, far = voxels(arrived, adjoint, adjoint_sib, before, after)
-    kernel = smooth(
-        part, lax.ppermute(part, "mer_2", swap), lax.ppermute(near, MER, cross), lax.ppermute(far, MER, diagonal)
-    )
+    part = voxels(arrived, adjoint, adjoint_sib, before, after)
+    base, edge = total(part, lax.ppermute(part, "mer_2", swap))
+    kernel = smooth(base, lax.ppermute(edge, MER, cross))
     return final.reshape(3, 5, 8, 128), kernel.reshape(8, 4, 128)
 
 

time: 98.1 us -> 93.9 us (0.957)
  the two profiles are of different devices: /device:TPU:64 before, /device:TPU:1 now
where the time goes in v3:
time: 93.9 us; the launch traced here: 93.4 us
  starting transfers between devices  48.5 us (52%)
  waiting for transfers between devices  34.5 us (37%)
  Pallas kernels  8.65 us (9%)
    all_to_all x1, waiting for transfers between devices, on_device(): lax.all_to_all(outgoing.reshape(64, ROWS, 1, 128), SIDES, 0, 0, tiled=True)  16.5 us
    all_to_all x1, starting transfers between devices, on_device(): lax.all_to_all(outgoing.reshape(64, ROWS, 1, 128), SIDES, 0, 0, tiled=True)  12.1 us
    ppermute x1, starting transfers between devices, on_device(): sib = lax.ppermute(own, 'mer_2', swap)  8.75 us
    ppermute x1, starting transfers between devices, on_device(): base, edge = total(part, lax.ppermute(part, 'mer_2', swap))  6.98 us
    all_to_all x1, waiting for transfers between devices, on_device(): nodes = lax.all_to_all(spread, 'az', 0, 0, tiled=True)  5.64 us
    ppermute x1, waiting for transfers between devices, on_device(): outer = lax.ppermute(chip_message(own, sib), MER, cross)  5.06 us
    ppermute x1, starting transfers between devices, on_device(): after = lax.ppermute(first, 'az', [(b, a) for a, b in ahead])  4.31 us
    ppermute x1, starting transfers between devices, on_device(): adjoint_sib = lax.ppermute(adjoint, 'mer_2', swap)  3.98 us
  transfers between devices with their start and end apart: 10, of which 9 were waited for; matrix products, arithmetic and copies ran while one was open for 0% of the time, Pallas kernels for 1%

profile of v3, /device:TPU:1, one launch (start us, length us, event | category | flops | bytes accessed | tf_op | source)
XLA Modules:
  0.0 93.4 jit_solution(7412212325298954756)
XLA Ops:
  0.6 0.0 copy-start
  0.6 1.8 %pack.1 = (f32[32,8,128]{2,1,0:T(8,128)}, f32[8,128]{1,0:T(8,128)}) custom-call(f32[15,8,128]{2,1,0:T(8,128)} %bitcast.16, f32[15,8,128]{2,1,0:T(8,128)} %bitcast.17, f32[1,2]{1,0:T(1,128)} %refs_2_.1, f32[1,2]{1,0:T(1,128)} %refs_3_.1, f32[1,2]{1,0:T(1,128)} %refs_4_.1, f32[1,2]{1,0:T(1,128)} %refs_5_.1, s32[1,2]{1,0:T(1,128)} %refs_6_.1, ...), custom_call_target="tpu_custom_call" | custom-call | tf_op jit(solution)/shard_map/pack/pallas_call | solution.py:133
  2.5 8.7 %collective-permute-start = (f32[32,8,128]{2,1,0:T(8,128)}, f32[32,8,128]{2,1,0:T(8,128)S(1)}, u32[]{:S(2)}, u32[]{:S(2)}) collective-permute-start(f32[32,8,128]{2,1,0:T(8,128)} %get-tuple-element.13.own_ref), channel_id=1, source_target_pairs={{0,4},{4,0},{1,5},{5,1},{2,6},{6,2},{3,7},{7,3},{8,12},{12,8},{9,1... | collective-permute-start | bytes 393224 | tf_op jit(solution)/shard_map/ppermute | solution.py:605
  11.2 1.2 %collective-permute-done.sib_ref = f32[32,8,128]{2,1,0:T(8,128)S(1)} collective-permute-done((f32[32,8,128]{2,1,0:T(8,128)}, f32[32,8,128]{2,1,0:T(8,128)S(1)}, u32[]{:S(2)}, u32[]{:S(2)}) %collective-permute-start) | collective-permute-done | bytes 131104 | tf_op jit(solution)/shard_map/ppermute | solution.py:605
  12.4 0.0 copy-start.2
  12.4 0.9 copy-done.2
  13.3 0.0 copy-start.3
  13.3 1.9 %collective-permute-start.1 = (f32[48,8,128]{2,1,0:T(8,128)S(1)}, f32[48,8,128]{2,1,0:T(8,128)S(1)}, u32[]{:S(2)}, u32[]{:S(2)}) collective-permute-start(f32[48,8,128]{2,1,0:T(8,128)S(1)} %chip.1), channel_id=1, source_target_pairs={{4,8},{12,16},{20,24},{28,32},{36,40},{44,48},{52,56},{60,64},{68,... | collective-permute-start | bytes 589832 | tf_op jit(solution)/shard_map/ppermute | solution.py:606
  15.2 5.1 %collective-permute-done.1.cross_ref = f32[48,8,128]{2,1,0:T(8,128)S(1)} collective-permute-done((f32[48,8,128]{2,1,0:T(8,128)S(1)}, f32[48,8,128]{2,1,0:T(8,128)S(1)}, u32[]{:S(2)}, u32[]{:S(2)}) %collective-permute-start.1) | collective-permute-done | bytes 196640 | tf_op jit(solution)/shard_map/ppermute | solution.py:606
  20.3 1.9 %collective-permute-start.2 = (f32[16,8,128]{2,1,0:T(8,128)S(1)}, f32[16,8,128]{2,1,0:T(8,128)S(1)}, u32[]{:S(2)}, u32[]{:S(2)}) collective-permute-start(f32[16,8,128]{2,1,0:T(8,128)S(1)} %forward.1), channel_id=1, source_target_pairs={{0,4},{4,0},{1,5},{5,1},{2,6},{6,2},{3,7},{7,3},{8,12},{12,8},{9,1... | collective-permute-start | bytes 196616 | tf_op jit(solution)/shard_map/ppermute | solution.py:607
  22.2 1.2 %collective-permute-done.2.forward_ref = f32[16,8,128]{2,1,0:T(8,128)S(1)} collective-permute-done((f32[16,8,128]{2,1,0:T(8,128)S(1)}, f32[16,8,128]{2,1,0:T(8,128)S(1)}, u32[]{:S(2)}, u32[]{:S(2)}) %collective-permute-start.2) | collective-permute-done | bytes 65568 | tf_op jit(solution)/shard_map/ppermute | solution.py:607
  23.5 1.8 %march.1 = (f32[15,8,128]{2,1,0:T(8,128)}, f32[4,17,8,128]{3,2,1,0:T(8,128)}) custom-call(f32[32,8,128]{2,1,0:T(8,128)S(1)} %copy-done.2, f32[32,8,128]{2,1,0:T(8,128)S(1)} %collective-permute-done.sib_ref, f32[48,8,128]{2,1,0:T(8,128)S(1)} %collective-permute-done.1.cross_ref, f32[16,8,128]{2,1,0:T(8,128)S(1)} %collective-permute-done.2.forward_ref), custom_call_target="tpu_custom_call" | custom-call | tf_op jit(solution)/shard_map/march/pallas_call | solution.py:300
  25.3 3.4 %all-to-all-start = ((f32[4,17,8,128]{3,2,1,0:T(8,128)}), f32[4,17,8,128]{3,2,1,0:T(8,128)S(1)}, u32[]{:S(2)}, u32[]{:S(2)}) async-start(f32[4,17,8,128]{3,2,1,0:T(8,128)} %get-tuple-element.15), calls=%async_computation | async-start | bytes 557056 | tf_op jit(solution)/shard_map/all_to_all | solution.py:611
  28.7 0.0 copy-done
  28.7 0.0 copy-done.3
  28.7 1.1 %weights.1 = (bf16[6,256,256]{2,1,0:T(8,128)(2,1)S(1)}, bf16[2,256,256]{2,1,0:T(8,128)(2,1)S(1)}, bf16[2,512,384]{2,1,0:T(8,128)(2,1)S(1)}) custom-call(f32[8,128]{1,0:T(8,128)S(1)} %copy-done.3, f32[1040,256]{1,0:T(8,128)S(1)} %copy-done), custom_call_target="tpu_custom_call" | custom-call | tf_op jit(solution)/shard_map/weights/pallas_call | solution.py:390
  29.8 5.6 %all-to-all-done.nodes_ref = f32[4,17,8,128]{3,2,1,0:T(8,128)S(1)} async-done(((f32[4,17,8,128]{3,2,1,0:T(8,128)}), f32[4,17,8,128]{3,2,1,0:T(8,128)S(1)}, u32[]{:S(2)}, u32[]{:S(2)}) %all-to-all-start) | async-done | bytes 278560 | tf_op jit(solution)/shard_map/all_to_all | solution.py:611
  35.5 2.4 %messages.1 = f32[2368,128]{1,0:T(8,128)} custom-call(f32[4,17,8,128]{3,2,1,0:T(8,128)S(1)} %all-to-all-done.nodes_ref, bf16[6,256,256]{2,1,0:T(8,128)(2,1)S(1)} %get-tuple-element.17.weight_ref, bf16[2,256,256]{2,1,0:T(8,128)(2,1)S(1)} %get-tuple-element.18.point_ref, bf16[2,512,384]{2,1,0:T(8,128)(2,1)S(1)} %get-tuple-element.19.basis_ref), custom_call_target="tpu_custom_call" | custom-call | tf_op jit(solution)/shard_map/messages/pallas_call | solution.py:443
  37.9 0.0 copy-start.1
  37.9 12.1 %all-to-all-start.1 = ((f32[64,37,1,128]{3,2,1,0:T(1,128)}), f32[64,37,1,128]{3,2,1,0:T(1,128)S(1)}, u32[]{:S(2)}, u32[]{:S(2)}) async-start(f32[64,37,1,128]{3,2,1,0:T(1,128)} %bitcast.8), calls=%async_computation.1 | async-start | bytes 2424832 | tf_op jit(solution)/shard_map/all_to_all | solution.py:613
  50.0 0.0 copy-done.1
  50.1 4.0 %collective-permute-start.3 = (f32[9,32,128]{2,1,0:T(8,128)S(1)}, f32[9,32,128]{2,1,0:T(8,128)S(1)}, u32[]{:S(2)}, u32[]{:S(2)}) collective-permute-start(f32[9,32,128]{2,1,0:T(8,128)S(1)} %bitcast.13), channel_id=1, source_target_pairs={{0,4},{4,0},{1,5},{5,1},{2,6},{6,2},{3,7},{7,3},{8,12},{12,8},{9,1... | collective-permute-start | bytes 442376 | tf_op jit(solution)/shard_map/ppermute | solution.py:617
  54.0 1.0 %collective-permute-done.3.sib_ref = f32[9,32,128]{2,1,0:T(8,128)S(1)} collective-permute-done((f32[9,32,128]{2,1,0:T(8,128)S(1)}, f32[9,32,128]{2,1,0:T(8,128)S(1)}, u32[]{:S(2)}, u32[]{:S(2)}) %collective-permute-start.3) | collective-permute-done | bytes 147488 | tf_op jit(solution)/shard_map/ppermute | solution.py:617
  55.0 0.3 rims.1
  55.3 2.2 %collective-permute-start.4 = (f32[2,32,128]{2,1,0:T(8,128)S(1)}, f32[2,32,128]{2,1,0:T(8,128)S(1)}, u32[]{:S(2)}, u32[]{:S(2)}) collective-permute-start(f32[2,32,128]{2,1,0:T(8,128)S(1)} %get-tuple-element.20), channel_id=1, source_target_pairs={{0,1},{1,2},{2,3},{3,0},{4,5},{5,6},{6,7},{7,4},{8,9},{9,10},{10,1... | collective-permute-start | bytes 98312 | tf_op jit(solution)/shard_map/ppermute | solution.py:619
  57.5 4.3 %collective-permute-start.5 = (f32[2,32,128]{2,1,0:T(8,128)S(1)}, f32[2,32,128]{2,1,0:T(8,128)S(1)}, u32[]{:S(2)}, u32[]{:S(2)}) collective-permute-start(f32[2,32,128]{2,1,0:T(8,128)S(1)} %get-tuple-element.21), channel_id=1, source_target_pairs={{1,0},{2,1},{3,2},{0,3},{5,4},{6,5},{7,6},{4,7},{9,8},{10,9},{11,1... | collective-permute-start | bytes 98312 | tf_op jit(solution)/shard_map/ppermute | solution.py:620
  61.8 0.0 collective-permute-done.4.before_ref
  61.8 1.0 %collective-permute-done.5.after_ref = f32[2,32,128]{2,1,0:T(8,128)S(1)} collective-permute-done((f32[2,32,128]{2,1,0:T(8,128)S(1)}, f32[2,32,128]{2,1,0:T(8,128)S(1)}, u32[]{:S(2)}, u32[]{:S(2)}) %collective-permute-start.5) | collective-permute-done | bytes 32800 | tf_op jit(solution)/shard_map/ppermute | solution.py:620
  62.8 16.5 %all-to-all-done.1 = f32[64,37,1,128]{3,2,1,0:T(1,128)S(1)} async-done(((f32[64,37,1,128]{3,2,1,0:T(1,128)}), f32[64,37,1,128]{3,2,1,0:T(1,128)S(1)}, u32[]{:S(2)}, u32[]{:S(2)}) %all-to-all-start.1) | async-done | bytes 1212448 | tf_op jit(solution)/shard_map/all_to_all | solution.py:613
  79.3 0.5 voxels.1.mine_ref
  79.9 7.0 %collective-permute-start.6 = (f32[4,32,128]{2,1,0:T(8,128)S(1)}, f32[4,32,128]{2,1,0:T(8,128)S(1)}, u32[]{:S(2)}, u32[]{:S(2)}) collective-permute-start(f32[4,32,128]{2,1,0:T(8,128)S(1)} %voxels.1.mine_ref), channel_id=1, source_target_pairs={{0,4},{4,0},{1,5},{5,1},{2,6},{6,2},{3,7},{7,3},{8,12},{12,8},{9,1... | collective-permute-start | bytes 196616 | tf_op jit(solution)/shard_map/ppermute | solution.py:622
  86.9 0.9 collective-permute-done.6.theirs_ref
  87.7 0.1 total.1
  87.9 2.9 %collective-permute-start.7 = (f32[8,128]{1,0:T(8,128)S(1)}, f32[8,128]{1,0:T(8,128)S(1)}, u32[]{:S(2)}, u32[]{:S(2)}) collective-permute-start(f32[8,128]{1,0:T(8,128)S(1)} %get-tuple-element.23), channel_id=1, source_target_pairs={{4,8},{12,16},{20,24},{28,32},{36,40},{44,48},{52,56},{60,64},{68,... | collective-permute-start | bytes 12296 | tf_op jit(solution)/shard_map/ppermute | solution.py:623
  90.7 2.1 %collective-permute-done.7.outer_ref = f32[8,128]{1,0:T(8,128)S(1)} collective-permute-done((f32[8,128]{1,0:T(8,128)S(1)}, f32[8,128]{1,0:T(8,128)S(1)}, u32[]{:S(2)}, u32[]{:S(2)}) %collective-permute-start.7) | collective-permute-done | bytes 4128 | tf_op jit(solution)/shard_map/ppermute | solution.py:623
  92.8 0.6 smooth.1
  (2 shorter events, 0.0 us)
Async XLA Ops:
  0.6 28.1 %copy-start = (f32[1040,256]{1,0:T(8,128)S(1)}, f32[1040,256]{1,0:T(8,128)}, u32[]{:S(2)}) copy-start(f32[1040,256]{1,0:T(8,128)} %constant.2.clone.table_ref) | copy-start | bytes 3194884
  2.5 9.9 %collective-permute-start = (f32[32,8,128]{2,1,0:T(8,128)}, f32[32,8,128]{2,1,0:T(8,128)S(1)}, u32[]{:S(2)}, u32[]{:S(2)}) collective-permute-start(f32[32,8,128]{2,1,0:T(8,128)} %get-tuple-element.13.own_ref), channel_id=1, source_target_pairs={{0,4},{4,0},{1,5},{5,1},{2,6},{6,2},{3,7},{7,3},{8,12},{12,8},{9,1... | collective-permute-start | bytes 393224 | tf_op jit(solution)/shard_map/ppermute | solution.py:605
  12.4 0.9 copy-start.2
  13.3 15.5 %copy-start.3 = (f32[8,128]{1,0:T(8,128)S(1)}, f32[8,128]{1,0:T(8,128)}, u32[]{:S(2)}) copy-start(f32[8,128]{1,0:T(8,128)} %get-tuple-element.16.points_ref) | copy-start | bytes 12292
  13.3 7.0 %collective-permute-start.1 = (f32[48,8,128]{2,1,0:T(8,128)S(1)}, f32[48,8,128]{2,1,0:T(8,128)S(1)}, u32[]{:S(2)}, u32[]{:S(2)}) collective-permute-start(f32[48,8,128]{2,1,0:T(8,128)S(1)} %chip.1), channel_id=1, source_target_pairs={{4,8},{12,16},{20,24},{28,32},{36,40},{44,48},{52,56},{60,64},{68,... | collective-permute-start | bytes 589832 | tf_op jit(solution)/shard_map/ppermute | solution.py:606
  20.3 3.1 %collective-permute-start.2 = (f32[16,8,128]{2,1,0:T(8,128)S(1)}, f32[16,8,128]{2,1,0:T(8,128)S(1)}, u32[]{:S(2)}, u32[]{:S(2)}) collective-permute-start(f32[16,8,128]{2,1,0:T(8,128)S(1)} %forward.1), channel_id=1, source_target_pairs={{0,4},{4,0},{1,5},{5,1},{2,6},{6,2},{3,7},{7,3},{8,12},{12,8},{9,1... | collective-permute-start | bytes 196616 | tf_op jit(solution)/shard_map/ppermute | solution.py:607
  25.3 10.2 %all-to-all-start = ((f32[4,17,8,128]{3,2,1,0:T(8,128)}), f32[4,17,8,128]{3,2,1,0:T(8,128)S(1)}, u32[]{:S(2)}, u32[]{:S(2)}) async-start(f32[4,17,8,128]{3,2,1,0:T(8,128)} %get-tuple-element.15), calls=%async_computation | async-start | bytes 557056 | tf_op jit(solution)/shard_map/all_to_all | solution.py:611
  37.9 12.1 %copy-start.1 = (f32[9,8,4,128]{3,2,1,0:T(4,128)S(1)}, f32[9,8,4,128]{3,2,1,0:T(4,128)}, u32[]{:S(2)}) copy-start(f32[9,8,4,128]{3,2,1,0:T(4,128)} %param.26) | copy-start | bytes 442372
  37.9 41.4 %all-to-all-start.1 = ((f32[64,37,1,128]{3,2,1,0:T(1,128)}), f32[64,37,1,128]{3,2,1,0:T(1,128)S(1)}, u32[]{:S(2)}, u32[]{:S(2)}) async-start(f32[64,37,1,128]{3,2,1,0:T(1,128)} %bitcast.8), calls=%async_computation.1 | async-start | bytes 2424832 | tf_op jit(solution)/shard_map/all_to_all | solution.py:613
  50.1 5.0 %collective-permute-start.3 = (f32[9,32,128]{2,1,0:T(8,128)S(1)}, f32[9,32,128]{2,1,0:T(8,128)S(1)}, u32[]{:S(2)}, u32[]{:S(2)}) collective-permute-start(f32[9,32,128]{2,1,0:T(8,128)S(1)} %bitcast.13), channel_id=1, source_target_pairs={{0,4},{4,0},{1,5},{5,1},{2,6},{6,2},{3,7},{7,3},{8,12},{12,8},{9,1... | collective-permute-start | bytes 442376 | tf_op jit(solution)/shard_map/ppermute | solution.py:617
  55.3 6.5 %collective-permute-start.4 = (f32[2,32,128]{2,1,0:T(8,128)S(1)}, f32[2,32,128]{2,1,0:T(8,128)S(1)}, u32[]{:S(2)}, u32[]{:S(2)}) collective-permute-start(f32[2,32,128]{2,1,0:T(8,128)S(1)} %get-tuple-element.20), channel_id=1, source_target_pairs={{0,1},{1,2},{2,3},{3,0},{4,5},{5,6},{6,7},{7,4},{8,9},{9,10},{10,1... | collective-permute-start | bytes 98312 | tf_op jit(solution)/shard_map/ppermute | solution.py:619
  57.5 5.3 %collective-permute-start.5 = (f32[2,32,128]{2,1,0:T(8,128)S(1)}, f32[2,32,128]{2,1,0:T(8,128)S(1)}, u32[]{:S(2)}, u32[]{:S(2)}) collective-permute-start(f32[2,32,128]{2,1,0:T(8,128)S(1)} %get-tuple-element.21), channel_id=1, source_target_pairs={{1,0},{2,1},{3,2},{0,3},{5,4},{6,5},{7,6},{4,7},{9,8},{10,9},{11,1... | collective-permute-start | bytes 98312 | tf_op jit(solution)/shard_map/ppermute | solution.py:620
  79.9 7.9 %collective-permute-start.6 = (f32[4,32,128]{2,1,0:T(8,128)S(1)}, f32[4,32,128]{2,1,0:T(8,128)S(1)}, u32[]{:S(2)}, u32[]{:S(2)}) collective-permute-start(f32[4,32,128]{2,1,0:T(8,128)S(1)} %voxels.1.mine_ref), channel_id=1, source_target_pairs={{0,4},{4,0},{1,5},{5,1},{2,6},{6,2},{3,7},{7,3},{8,12},{12,8},{9,1... | collective-permute-start | bytes 196616 | tf_op jit(solution)/shard_map/ppermute | solution.py:622
  87.9 4.9 %collective-permute-start.7 = (f32[8,128]{1,0:T(8,128)S(1)}, f32[8,128]{1,0:T(8,128)S(1)}, u32[]{:S(2)}, u32[]{:S(2)}) collective-permute-start(f32[8,128]{1,0:T(8,128)S(1)} %get-tuple-element.23), channel_id=1, source_target_pairs={{4,8},{12,16},{20,24},{28,32},{36,40},{44,48},{52,56},{60,64},{68,... | collective-permute-start | bytes 12296 | tf_op jit(solution)/shard_map/ppermute | solution.py:623

commit v4 on v3

--- a/solution.py
+++ b/solution.py
@@ -103,8 +103,8 @@
 
 
 def pack_kernel(*refs):
-    sources, (own_ref, points_ref) = refs[:12], refs[12:14]
-    scratch, arrived = refs[14:26], refs[26]
+    sources, (own_ref, near_ref, points_ref) = refs[:12], refs[12:15]
+    scratch, arrived = refs[15:27], refs[27]
     copies = fetch(list(zip(sources, scratch)), arrived)
     u_ref, v_ref = scratch[:2]
     element_ref, local_ref, scale_ref, owner_ref, cell_ref = scratch[7:]
@@ -120,6 +120,7 @@
         both = ref[...].astype(f32)
         own_ref[30, i:i + 1, :] = jnp.broadcast_to(both[:, 0:1], (1, 128))
         own_ref[31, i:i + 1, :] = jnp.broadcast_to(both[:, 1:2], (1, 128))
+    near_columns(near_ref, own_ref, lax.axis_index("mer_2") == 1)
     points_ref[0:2, 0:64] = local_ref[...]
     points_ref[2:3, 0:64] = (element_ref[1:2, :] % 2).astype(f32)
     points_ref[3:4, 0:64] = scale_ref[...]
@@ -133,32 +134,29 @@
     return pl.pallas_call(
         pack_kernel,
         in_specs=[hbm] * 12,
-        out_specs=(vmem, vmem),
+        out_specs=(vmem, vmem, vmem),
         scratch_shapes=[pltpu.VMEM(a.shape, a.dtype) for a in arrays] + [pltpu.SemaphoreType.DMA((12,))],
         out_shape=(
             jax.ShapeDtypeStruct((32, 8, 128), f32),
+            jax.ShapeDtypeStruct((16, 8, 128), f32),
             jax.ShapeDtypeStruct((8, 128), f32),
         ),
         name="pack",
     )(*arrays)
 
 
-def near_columns(target, first, source, upward):
+def near_columns(target, source, upward):
     row = lax.broadcasted_iota(jnp.int32, (8, 128), 0)
     for i in range(15):
         u, v = source[i], source[15 + i]
         start = jnp.broadcast_to(v[0:1, :], (8, 128))
-        target[first + i] = jnp.where((row == 5) & jnp.logical_not(upward), start, u)
-    target[first + 15] = jnp.where(upward, source[31], source[30])
+        target[i] = jnp.where((row == 5) & jnp.logical_not(upward), start, u)
+    target[15] = jnp.where(upward, source[31], source[30])
 
 
 def chip_kernel(own_ref, sib_ref, out_ref):
     out_ref[0:32] = own_ref[...]
-    near_columns(out_ref, 32, sib_ref, lax.axis_index("mer_2") == 1)
-
-
-def forward_kernel(cross_ref, out_ref):
-    near_columns(out_ref, 0, cross_ref, lax.axis_index("mer_2") == 0)
+    near_columns(out_ref.at[32:48], sib_ref, lax.axis_index("mer_2") == 1)
 
 
 def chip_message(own, sib):
@@ -168,14 +166,7 @@
     )(own, sib)
 
 
-def forward_message(cross):
-    return pl.pallas_call(
-        forward_kernel, out_shape=jax.ShapeDtypeStruct((16, 8, 128), jnp.float32),
-        compiler_params=GRANT, name="forward",
-    )(cross)
-
-
-def step_kernel(own_ref, sib_ref, cross_ref, forward_ref, u_ref, gather_ref,
+def step_kernel(own_ref, sib_ref, cross_ref, diagonal_ref, u_ref, gather_ref,
                 ucol, vcol, coef, state, field):
     core, az = lax.axis_index("mer_2"), lax.axis_index("az")
     is_low = core == 0
@@ -187,10 +178,10 @@
         return jnp.where(is_low, sib_ref[i], cross_ref[i])
 
     def far_left(i):
-        return jnp.where(is_low, cross_ref[32 + i], forward_ref[i])
+        return jnp.where(is_low, cross_ref[32 + i], diagonal_ref[i])
 
     def far_right(i):
-        return jnp.where(is_low, forward_ref[i], cross_ref[32 + i])
+        return jnp.where(is_low, diagonal_ref[i], cross_ref[32 + i])
 
     zero8 = jnp.zeros((8, 128), jnp.float32)
     for i in range(15):
@@ -294,7 +285,7 @@
             gather_ref[q, 15 + i // 8, i % 8:i % 8 + 1, :] = rim
 
 
-def march(own, sib, cross, forward):
+def march(own, sib, cross, diagonal):
     f32 = jnp.float32
     vmem = pl.BlockSpec(memory_space=pltpu.VMEM)
     return pl.pallas_call(
@@ -314,7 +305,7 @@
         ],
         compiler_params=GRANT,
         name="march",
-    )(own, sib, cross, forward)
+    )(own, sib, cross, diagonal)
 
 
 def weight_kernel(points_ref, table_ref, weight_ref, point_ref, basis_ref):
@@ -594,18 +585,19 @@
     az_count = lax.axis_size("az")
     swap = [(0, 1), (1, 0)]
     cross = [(c, c + 1) for c in range(1, count - 1, 2)] + [(c + 1, c) for c in range(1, count - 1, 2)]
+    diagonal = [(c, c - 2) for c in range(2, count, 2)] + [(c, c + 2) for c in range(1, count - 2, 2)]
     ahead = [(i, (i + 1) % az_count) for i in range(az_count)]
 
-    own, points = pack(
+    own, side, points = pack(
         displacement.reshape(15, 8, 128), velocity.reshape(15, 8, 128),
         modulus, hoop_strength, coupling, density, order_count,
         point_element.T, point_local.T, azimuth_scale.reshape(1, 64), point_owner.reshape(1, 64),
         point_cell.reshape(1, 64),
     )
     sib = lax.ppermute(own, "mer_2", swap)
+    same = lax.ppermute(side, MER, diagonal)
     outer = lax.ppermute(chip_message(own, sib), MER, cross)
-    forward = lax.ppermute(forward_message(outer), "mer_2", swap)
-    final, spread = march(own, sib, outer, forward)
+    final, spread = march(own, sib, outer, same)
 
     weights = point_weights(points)
     nodes = lax.all_to_all(spread, "az", 0, 0, tiled=True)

time: 93.9 us -> 92.1 us (0.981)
  waiting for transfers between devices: 34.5 us -> 32.8 us
    ppermute x1, waiting for transfers between devices: 5.06 us -> 1.66 us  [on_device(): outer = lax.ppermute(chip_message(own, sib), MER, cross)]
    all_to_all x1, starting transfers between devices: 12.1 us -> 14.9 us  [on_device(): lax.all_to_all(outgoing.reshape(64, ROWS, 1, 128), SIDES, 0, 0, tiled=True)]
    all_to_all x1, waiting for transfers between devices: 16.5 us -> 18.6 us  [on_device(): lax.all_to_all(outgoing.reshape(64, ROWS, 1, 128), SIDES, 0, 0, tiled=True)]
    ppermute x1, starting transfers between devices: 6.98 us -> 5.42 us  [on_device(): base, edge = total(part, lax.ppermute(part, 'mer_2', swap))]
    all_to_all x1, waiting for transfers between devices: 5.64 us -> 4.48 us  [on_device(): nodes = lax.all_to_all(spread, 'az', 0, 0, tiled=True)]
where the time goes in v4:
time: 92.1 us; the launch traced here: 91.6 us
  starting transfers between devices  48.4 us (53%)
  waiting for transfers between devices  32.8 us (36%)
  Pallas kernels  8.66 us (9%)
    all_to_all x1, waiting for transfers between devices, on_device(): lax.all_to_all(outgoing.reshape(64, ROWS, 1, 128), SIDES, 0, 0, tiled=True)  18.6 us
    all_to_all x1, starting transfers between devices, on_device(): lax.all_to_all(outgoing.reshape(64, ROWS, 1, 128), SIDES, 0, 0, tiled=True)  14.9 us
    ppermute x1, starting transfers between devices, on_device(): sib = lax.ppermute(own, 'mer_2', swap)  8.75 us
    ppermute x1, starting transfers between devices, on_device(): base, edge = total(part, lax.ppermute(part, 'mer_2', swap))  5.42 us
    all_to_all x1, waiting for transfers between devices, on_device(): nodes = lax.all_to_all(spread, 'az', 0, 0, tiled=True)  4.48 us
    ppermute x1, starting transfers between devices, on_device(): after = lax.ppermute(first, 'az', [(b, a) for a, b in ahead])  4.3 us
    all_to_all x1, starting transfers between devices, on_device(): nodes = lax.all_to_all(spread, 'az', 0, 0, tiled=True)  3.45 us
    ppermute x1, starting transfers between devices, on_device(): adjoint_sib = lax.ppermute(adjoint, 'mer_2', swap)  3.18 us
  transfers between devices with their start and end apart: 10, of which 9 were waited for; matrix products, arithmetic and copies ran while one was open for 0% of the time, Pallas kernels for 1%

profile of v4, /device:TPU:1, one launch (start us, length us, event | category | flops | bytes accessed | tf_op | source)
XLA Modules:
  0.0 91.6 jit_solution(11237063499976146495)
XLA Ops:
  0.6 0.0 copy-start
  0.6 1.8 %pack.1 = (f32[32,8,128]{2,1,0:T(8,128)}, f32[16,8,128]{2,1,0:T(8,128)}, f32[8,128]{1,0:T(8,128)}) custom-call(f32[15,8,128]{2,1,0:T(8,128)} %bitcast.16, f32[15,8,128]{2,1,0:T(8,128)} %bitcast.17, f32[1,2]{1,0:T(1,128)} %refs_2_.1, f32[1,2]{1,0:T(1,128)} %refs_3_.1, f32[1,2]{1,0:T(1,128)} %refs_4_.1, f32[1,2]{1,0:T(1,128)} %refs_5_.1, s32[1,2]{1,0:T(1,128)} %refs_6_.1, ...), custom_call_target="tpu_custom_call" | custom-call | tf_op jit(solution)/shard_map/pack/pallas_call | solution.py:134
  2.5 8.7 %collective-permute-start = (f32[32,8,128]{2,1,0:T(8,128)}, f32[32,8,128]{2,1,0:T(8,128)S(1)}, u32[]{:S(2)}, u32[]{:S(2)}) collective-permute-start(f32[32,8,128]{2,1,0:T(8,128)} %get-tuple-element.14.own_ref), channel_id=1, source_target_pairs={{0,4},{4,0},{1,5},{5,1},{2,6},{6,2},{3,7},{7,3},{8,12},{12,8},{9,1... | collective-permute-start | bytes 393224 | tf_op jit(solution)/shard_map/ppermute | solution.py:597
  11.2 1.2 %collective-permute-done.sib_ref = f32[32,8,128]{2,1,0:T(8,128)S(1)} collective-permute-done((f32[32,8,128]{2,1,0:T(8,128)}, f32[32,8,128]{2,1,0:T(8,128)S(1)}, u32[]{:S(2)}, u32[]{:S(2)}) %collective-permute-start) | collective-permute-done | bytes 131104 | tf_op jit(solution)/shard_map/ppermute | solution.py:597
  12.4 0.0 copy-start.2
  12.4 0.9 copy-done.2
  13.3 0.0 copy-start.3
  13.3 1.9 %collective-permute-start.1 = (f32[48,8,128]{2,1,0:T(8,128)S(1)}, f32[48,8,128]{2,1,0:T(8,128)S(1)}, u32[]{:S(2)}, u32[]{:S(2)}) collective-permute-start(f32[48,8,128]{2,1,0:T(8,128)S(1)} %chip.1), channel_id=1, source_target_pairs={{4,8},{12,16},{20,24},{28,32},{36,40},{44,48},{52,56},{60,64},{68,... | collective-permute-start | bytes 589832 | tf_op jit(solution)/shard_map/ppermute | solution.py:599
  15.3 1.3 %collective-permute-start.2 = (f32[16,8,128]{2,1,0:T(8,128)}, f32[16,8,128]{2,1,0:T(8,128)S(1)}, u32[]{:S(2)}, u32[]{:S(2)}) collective-permute-start(f32[16,8,128]{2,1,0:T(8,128)} %get-tuple-element.15), channel_id=1, source_target_pairs={{8,0},{16,8},{24,16},{32,24},{40,32},{48,40},{56,48},{64,56},{72,6... | collective-permute-start | bytes 196616 | tf_op jit(solution)/shard_map/ppermute | solution.py:598
  16.6 2.1 %collective-permute-done.2.diagonal_ref = f32[16,8,128]{2,1,0:T(8,128)S(1)} collective-permute-done((f32[16,8,128]{2,1,0:T(8,128)}, f32[16,8,128]{2,1,0:T(8,128)S(1)}, u32[]{:S(2)}, u32[]{:S(2)}) %collective-permute-start.2) | collective-permute-done | bytes 65568 | tf_op jit(solution)/shard_map/ppermute | solution.py:598
  18.7 1.7 %collective-permute-done.1.cross_ref = f32[48,8,128]{2,1,0:T(8,128)S(1)} collective-permute-done((f32[48,8,128]{2,1,0:T(8,128)S(1)}, f32[48,8,128]{2,1,0:T(8,128)S(1)}, u32[]{:S(2)}, u32[]{:S(2)}) %collective-permute-start.1) | collective-permute-done | bytes 196640 | tf_op jit(solution)/shard_map/ppermute | solution.py:599
  20.3 1.8 %march.1 = (f32[15,8,128]{2,1,0:T(8,128)}, f32[4,17,8,128]{3,2,1,0:T(8,128)}) custom-call(f32[32,8,128]{2,1,0:T(8,128)S(1)} %copy-done.2, f32[32,8,128]{2,1,0:T(8,128)S(1)} %collective-permute-done.sib_ref, f32[48,8,128]{2,1,0:T(8,128)S(1)} %collective-permute-done.1.cross_ref, f32[16,8,128]{2,1,0:T(8,128)S(1)} %collective-permute-done.2.diagonal_ref), custom_call_target="tpu_custom_call" | custom-call | tf_op jit(solution)/shard_map/march/pallas_call | solution.py:291
  22.1 3.4 %all-to-all-start = ((f32[4,17,8,128]{3,2,1,0:T(8,128)}), f32[4,17,8,128]{3,2,1,0:T(8,128)S(1)}, u32[]{:S(2)}, u32[]{:S(2)}) async-start(f32[4,17,8,128]{3,2,1,0:T(8,128)} %get-tuple-element.17), calls=%async_computation | async-start | bytes 557056 | tf_op jit(solution)/shard_map/all_to_all | solution.py:603
  25.6 0.0 copy-done
  25.6 0.0 copy-done.3
  25.6 1.1 %weights.1 = (bf16[6,256,256]{2,1,0:T(8,128)(2,1)S(1)}, bf16[2,256,256]{2,1,0:T(8,128)(2,1)S(1)}, bf16[2,512,384]{2,1,0:T(8,128)(2,1)S(1)}) custom-call(f32[8,128]{1,0:T(8,128)S(1)} %copy-done.3, f32[1040,256]{1,0:T(8,128)S(1)} %copy-done), custom_call_target="tpu_custom_call" | custom-call | tf_op jit(solution)/shard_map/weights/pallas_call | solution.py:381
  26.7 4.5 %all-to-all-done.nodes_ref = f32[4,17,8,128]{3,2,1,0:T(8,128)S(1)} async-done(((f32[4,17,8,128]{3,2,1,0:T(8,128)}), f32[4,17,8,128]{3,2,1,0:T(8,128)S(1)}, u32[]{:S(2)}, u32[]{:S(2)}) %all-to-all-start) | async-done | bytes 278560 | tf_op jit(solution)/shard_map/all_to_all | solution.py:603
  31.2 2.4 %messages.1 = f32[2368,128]{1,0:T(8,128)} custom-call(f32[4,17,8,128]{3,2,1,0:T(8,128)S(1)} %all-to-all-done.nodes_ref, bf16[6,256,256]{2,1,0:T(8,128)(2,1)S(1)} %get-tuple-element.19.weight_ref, bf16[2,256,256]{2,1,0:T(8,128)(2,1)S(1)} %get-tuple-element.20.point_ref, bf16[2,512,384]{2,1,0:T(8,128)(2,1)S(1)} %get-tuple-element.21.basis_ref), custom_call_target="tpu_custom_call" | custom-call | tf_op jit(solution)/shard_map/messages/pallas_call | solution.py:434
  33.6 0.0 copy-start.1
  33.6 14.9 %all-to-all-start.1 = ((f32[64,37,1,128]{3,2,1,0:T(1,128)}), f32[64,37,1,128]{3,2,1,0:T(1,128)S(1)}, u32[]{:S(2)}, u32[]{:S(2)}) async-start(f32[64,37,1,128]{3,2,1,0:T(1,128)} %bitcast.8), calls=%async_computation.1 | async-start | bytes 2424832 | tf_op jit(solution)/shard_map/all_to_all | solution.py:605
  48.5 0.0 copy-done.1
  48.5 3.2 %collective-permute-start.3 = (f32[9,32,128]{2,1,0:T(8,128)S(1)}, f32[9,32,128]{2,1,0:T(8,128)S(1)}, u32[]{:S(2)}, u32[]{:S(2)}) collective-permute-start(f32[9,32,128]{2,1,0:T(8,128)S(1)} %bitcast.13), channel_id=1, source_target_pairs={{0,4},{4,0},{1,5},{5,1},{2,6},{6,2},{3,7},{7,3},{8,12},{12,8},{9,1... | collective-permute-start | bytes 442376 | tf_op jit(solution)/shard_map/ppermute | solution.py:609
  51.7 1.0 %collective-permute-done.3.sib_ref = f32[9,32,128]{2,1,0:T(8,128)S(1)} collective-permute-done((f32[9,32,128]{2,1,0:T(8,128)S(1)}, f32[9,32,128]{2,1,0:T(8,128)S(1)}, u32[]{:S(2)}, u32[]{:S(2)}) %collective-permute-start.3) | collective-permute-done | bytes 147488 | tf_op jit(solution)/shard_map/ppermute | solution.py:609
  52.7 0.3 rims.1
  52.9 2.2 %collective-permute-start.4 = (f32[2,32,128]{2,1,0:T(8,128)S(1)}, f32[2,32,128]{2,1,0:T(8,128)S(1)}, u32[]{:S(2)}, u32[]{:S(2)}) collective-permute-start(f32[2,32,128]{2,1,0:T(8,128)S(1)} %get-tuple-element.22), channel_id=1, source_target_pairs={{0,1},{1,2},{2,3},{3,0},{4,5},{5,6},{6,7},{7,4},{8,9},{9,10},{10,1... | collective-permute-start | bytes 98312 | tf_op jit(solution)/shard_map/ppermute | solution.py:611
  55.1 4.3 %collective-permute-start.5 = (f32[2,32,128]{2,1,0:T(8,128)S(1)}, f32[2,32,128]{2,1,0:T(8,128)S(1)}, u32[]{:S(2)}, u32[]{:S(2)}) collective-permute-start(f32[2,32,128]{2,1,0:T(8,128)S(1)} %get-tuple-element.23), channel_id=1, source_target_pairs={{1,0},{2,1},{3,2},{0,3},{5,4},{6,5},{7,6},{4,7},{9,8},{10,9},{11,1... | collective-permute-start | bytes 98312 | tf_op jit(solution)/shard_map/ppermute | solution.py:612
  59.4 0.0 collective-permute-done.4.before_ref
  59.5 1.0 %collective-permute-done.5.after_ref = f32[2,32,128]{2,1,0:T(8,128)S(1)} collective-permute-done((f32[2,32,128]{2,1,0:T(8,128)S(1)}, f32[2,32,128]{2,1,0:T(8,128)S(1)}, u32[]{:S(2)}, u32[]{:S(2)}) %collective-permute-start.5) | collective-permute-done | bytes 32800 | tf_op jit(solution)/shard_map/ppermute | solution.py:612
  60.4 18.6 %all-to-all-done.1 = f32[64,37,1,128]{3,2,1,0:T(1,128)S(1)} async-done(((f32[64,37,1,128]{3,2,1,0:T(1,128)}), f32[64,37,1,128]{3,2,1,0:T(1,128)S(1)}, u32[]{:S(2)}, u32[]{:S(2)}) %all-to-all-start.1) | async-done | bytes 1212448 | tf_op jit(solution)/shard_map/all_to_all | solution.py:605
  79.1 0.5 voxels.1.mine_ref
  79.6 5.4 %collective-permute-start.6 = (f32[4,32,128]{2,1,0:T(8,128)S(1)}, f32[4,32,128]{2,1,0:T(8,128)S(1)}, u32[]{:S(2)}, u32[]{:S(2)}) collective-permute-start(f32[4,32,128]{2,1,0:T(8,128)S(1)} %voxels.1.mine_ref), channel_id=1, source_target_pairs={{0,4},{4,0},{1,5},{5,1},{2,6},{6,2},{3,7},{7,3},{8,12},{12,8},{9,1... | collective-permute-start | bytes 196616 | tf_op jit(solution)/shard_map/ppermute | solution.py:614
  85.0 0.9 collective-permute-done.6.theirs_ref
  85.9 0.1 total.1
  86.0 3.0 %collective-permute-start.7 = (f32[8,128]{1,0:T(8,128)S(1)}, f32[8,128]{1,0:T(8,128)S(1)}, u32[]{:S(2)}, u32[]{:S(2)}) collective-permute-start(f32[8,128]{1,0:T(8,128)S(1)} %get-tuple-element.25), channel_id=1, source_target_pairs={{4,8},{12,16},{20,24},{28,32},{36,40},{44,48},{52,56},{60,64},{68,... | collective-permute-start | bytes 12296 | tf_op jit(solution)/shard_map/ppermute | solution.py:615
  89.0 1.9 %collective-permute-done.7.outer_ref = f32[8,128]{1,0:T(8,128)S(1)} collective-permute-done((f32[8,128]{1,0:T(8,128)S(1)}, f32[8,128]{1,0:T(8,128)S(1)}, u32[]{:S(2)}, u32[]{:S(2)}) %collective-permute-start.7) | collective-permute-done | bytes 4128 | tf_op jit(solution)/shard_map/ppermute | solution.py:615
  90.9 0.6 smooth.1
  (1 shorter events, 0.0 us)
Async XLA Ops:
  0.6 24.9 %copy-start = (f32[1040,256]{1,0:T(8,128)S(1)}, f32[1040,256]{1,0:T(8,128)}, u32[]{:S(2)}) copy-start(f32[1040,256]{1,0:T(8,128)} %constant.2.clone.table_ref) | copy-start | bytes 3194884
  2.5 9.9 %collective-permute-start = (f32[32,8,128]{2,1,0:T(8,128)}, f32[32,8,128]{2,1,0:T(8,128)S(1)}, u32[]{:S(2)}, u32[]{:S(2)}) collective-permute-start(f32[32,8,128]{2,1,0:T(8,128)} %get-tuple-element.14.own_ref), channel_id=1, source_target_pairs={{0,4},{4,0},{1,5},{5,1},{2,6},{6,2},{3,7},{7,3},{8,12},{12,8},{9,1... | collective-permute-start | bytes 393224 | tf_op jit(solution)/shard_map/ppermute | solution.py:597
  12.4 0.9 copy-start.2
  13.3 12.3 %copy-start.3 = (f32[8,128]{1,0:T(8,128)S(1)}, f32[8,128]{1,0:T(8,128)}, u32[]{:S(2)}) copy-start(f32[8,128]{1,0:T(8,128)} %get-tuple-element.18.points_ref) | copy-start | bytes 12292
  13.3 7.0 %collective-permute-start.1 = (f32[48,8,128]{2,1,0:T(8,128)S(1)}, f32[48,8,128]{2,1,0:T(8,128)S(1)}, u32[]{:S(2)}, u32[]{:S(2)}) collective-permute-start(f32[48,8,128]{2,1,0:T(8,128)S(1)} %chip.1), channel_id=1, source_target_pairs={{4,8},{12,16},{20,24},{28,32},{36,40},{44,48},{52,56},{60,64},{68,... | collective-permute-start | bytes 589832 | tf_op jit(solution)/shard_map/ppermute | solution.py:599
  15.3 3.4 %collective-permute-start.2 = (f32[16,8,128]{2,1,0:T(8,128)}, f32[16,8,128]{2,1,0:T(8,128)S(1)}, u32[]{:S(2)}, u32[]{:S(2)}) collective-permute-start(f32[16,8,128]{2,1,0:T(8,128)} %get-tuple-element.15), channel_id=1, source_target_pairs={{8,0},{16,8},{24,16},{32,24},{40,32},{48,40},{56,48},{64,56},{72,6... | collective-permute-start | bytes 196616 | tf_op jit(solution)/shard_map/ppermute | solution.py:598
  22.1 9.0 %all-to-all-start = ((f32[4,17,8,128]{3,2,1,0:T(8,128)}), f32[4,17,8,128]{3,2,1,0:T(8,128)S(1)}, u32[]{:S(2)}, u32[]{:S(2)}) async-start(f32[4,17,8,128]{3,2,1,0:T(8,128)} %get-tuple-element.17), calls=%async_computation | async-start | bytes 557056 | tf_op jit(solution)/shard_map/all_to_all | solution.py:603
  33.6 14.9 %copy-start.1 = (f32[9,8,4,128]{3,2,1,0:T(4,128)S(1)}, f32[9,8,4,128]{3,2,1,0:T(4,128)}, u32[]{:S(2)}) copy-start(f32[9,8,4,128]{3,2,1,0:T(4,128)} %param.26) | copy-start | bytes 442372
  33.6 45.5 %all-to-all-start.1 = ((f32[64,37,1,128]{3,2,1,0:T(1,128)}), f32[64,37,1,128]{3,2,1,0:T(1,128)S(1)}, u32[]{:S(2)}, u32[]{:S(2)}) async-start(f32[64,37,1,128]{3,2,1,0:T(1,128)} %bitcast.8), calls=%async_computation.1 | async-start | bytes 2424832 | tf_op jit(solution)/shard_map/all_to_all | solution.py:605
  48.5 4.2 %collective-permute-start.3 = (f32[9,32,128]{2,1,0:T(8,128)S(1)}, f32[9,32,128]{2,1,0:T(8,128)S(1)}, u32[]{:S(2)}, u32[]{:S(2)}) collective-permute-start(f32[9,32,128]{2,1,0:T(8,128)S(1)} %bitcast.13), channel_id=1, source_target_pairs={{0,4},{4,0},{1,5},{5,1},{2,6},{6,2},{3,7},{7,3},{8,12},{12,8},{9,1... | collective-permute-start | bytes 442376 | tf_op jit(solution)/shard_map/ppermute | solution.py:609
  52.9 6.5 %collective-permute-start.4 = (f32[2,32,128]{2,1,0:T(8,128)S(1)}, f32[2,32,128]{2,1,0:T(8,128)S(1)}, u32[]{:S(2)}, u32[]{:S(2)}) collective-permute-start(f32[2,32,128]{2,1,0:T(8,128)S(1)} %get-tuple-element.22), channel_id=1, source_target_pairs={{0,1},{1,2},{2,3},{3,0},{4,5},{5,6},{6,7},{7,4},{8,9},{9,10},{10,1... | collective-permute-start | bytes 98312 | tf_op jit(solution)/shard_map/ppermute | solution.py:611
  55.1 5.3 %collective-permute-start.5 = (f32[2,32,128]{2,1,0:T(8,128)S(1)}, f32[2,32,128]{2,1,0:T(8,128)S(1)}, u32[]{:S(2)}, u32[]{:S(2)}) collective-permute-start(f32[2,32,128]{2,1,0:T(8,128)S(1)} %get-tuple-element.23), channel_id=1, source_target_pairs={{1,0},{2,1},{3,2},{0,3},{5,4},{6,5},{7,6},{4,7},{9,8},{10,9},{11,1... | collective-permute-start | bytes 98312 | tf_op jit(solution)/shard_map/ppermute | solution.py:612
  79.6 6.3 %collective-permute-start.6 = (f32[4,32,128]{2,1,0:T(8,128)S(1)}, f32[4,32,128]{2,1,0:T(8,128)S(1)}, u32[]{:S(2)}, u32[]{:S(2)}) collective-permute-start(f32[4,32,128]{2,1,0:T(8,128)S(1)} %voxels.1.mine_ref), channel_id=1, source_target_pairs={{0,4},{4,0},{1,5},{5,1},{2,6},{6,2},{3,7},{7,3},{8,12},{12,8},{9,1... | collective-permute-start | bytes 196616 | tf_op jit(solution)/shard_map/ppermute | solution.py:614
  86.0 4.9 %collective-permute-start.7 = (f32[8,128]{1,0:T(8,128)S(1)}, f32[8,128]{1,0:T(8,128)S(1)}, u32[]{:S(2)}, u32[]{:S(2)}) collective-permute-start(f32[8,128]{1,0:T(8,128)S(1)} %get-tuple-element.25), channel_id=1, source_target_pairs={{4,8},{12,16},{20,24},{28,32},{36,40},{44,48},{52,56},{60,64},{68,... | collective-permute-start | bytes 12296 | tf_op jit(solution)/shard_map/ppermute | solution.py:615

commit v5 on v4

--- a/solution.py
+++ b/solution.py
@@ -154,16 +154,27 @@
     target[15] = jnp.where(upward, source[31], source[30])
 
 
-def chip_kernel(own_ref, sib_ref, out_ref):
+def stage_kernel(own_ref, out_ref):
     out_ref[0:32] = own_ref[...]
+    out_ref[32:48] = jnp.zeros((16, 8, 128), jnp.float32)
+
+
+def stage(own):
+    return pl.pallas_call(
+        stage_kernel, out_shape=jax.ShapeDtypeStruct((48, 8, 128), jnp.float32), compiler_params=GRANT,
+        cost_estimate=pl.CostEstimate(flops=0, bytes_accessed=1 << 20, transcendentals=0), name="stage",
+    )(own)
+
+
+def chip_kernel(staged_ref, sib_ref, out_ref):
     near_columns(out_ref.at[32:48], sib_ref, lax.axis_index("mer_2") == 1)
 
 
-def chip_message(own, sib):
+def chip_message(staged, sib):
     return pl.pallas_call(
         chip_kernel, out_shape=jax.ShapeDtypeStruct((48, 8, 128), jnp.float32),
-        compiler_params=GRANT, name="chip",
-    )(own, sib)
+        input_output_aliases={0: 0}, compiler_params=GRANT, name="chip",
+    )(staged, sib)
 
 
 def step_kernel(own_ref, sib_ref, cross_ref, diagonal_ref, u_ref, gather_ref,
@@ -596,8 +607,9 @@
     )
     sib = lax.ppermute(own, "mer_2", swap)
     same = lax.ppermute(side, MER, diagonal)
-    outer = lax.ppermute(chip_message(own, sib), MER, cross)
-    final, spread = march(own, sib, outer, same)
+    message = chip_message(stage(own), sib)
+    outer = lax.ppermute(message, MER, cross)
+    final, spread = march(message, sib, outer, same)
 
     weights = point_weights(points)
     nodes = lax.all_to_all(spread, "az", 0, 0, tiled=True)

time: 92.1 us -> 91.2 us (level)
    ppermute x1, waiting for transfers between devices: 1.17 us -> 0.25 us  [on_device(): sib = lax.ppermute(own, 'mer_2', swap)]
where the time goes in v5:
time: 91.2 us; the launch traced here: 90.6 us
  starting transfers between devices  48.3 us (53%)
  waiting for transfers between devices  31.9 us (35%)
  Pallas kernels  8.66 us (9%)
    all_to_all x1, waiting for transfers between devices, on_device(): lax.all_to_all(outgoing.reshape(64, ROWS, 1, 128), SIDES, 0, 0, tiled=True)  18.6 us
    all_to_all x1, starting transfers between devices, on_device(): lax.all_to_all(outgoing.reshape(64, ROWS, 1, 128), SIDES, 0, 0, tiled=True)  14.9 us
    ppermute x1, starting transfers between devices, on_device(): sib = lax.ppermute(own, 'mer_2', swap)  8.75 us
    ppermute x1, starting transfers between devices, on_device(): base, edge = total(part, lax.ppermute(part, 'mer_2', swap))  5.42 us
    all_to_all x1, waiting for transfers between devices, on_device(): nodes = lax.all_to_all(spread, 'az', 0, 0, tiled=True)  4.49 us
    ppermute x1, starting transfers between devices, on_device(): after = lax.ppermute(first, 'az', [(b, a) for a, b in ahead])  4.3 us
    all_to_all x1, starting transfers between devices, on_device(): nodes = lax.all_to_all(spread, 'az', 0, 0, tiled=True)  3.45 us
    ppermute x1, starting transfers between devices, on_device(): adjoint_sib = lax.ppermute(adjoint, 'mer_2', swap)  3.18 us
  transfers between devices with their start and end apart: 10, of which 9 were waited for; matrix products, arithmetic and copies ran while one was open for 0% of the time, Pallas kernels for 1%

profile of v5, /device:TPU:1, one launch (start us, length us, event | category | flops | bytes accessed | tf_op | source)
XLA Modules:
  0.0 90.6 jit_solution(17886261708752385233)
XLA Ops:
  0.6 0.0 copy-start
  0.6 1.8 %pack.1 = (f32[32,8,128]{2,1,0:T(8,128)}, f32[16,8,128]{2,1,0:T(8,128)}, f32[8,128]{1,0:T(8,128)}) custom-call(f32[15,8,128]{2,1,0:T(8,128)} %bitcast.16, f32[15,8,128]{2,1,0:T(8,128)} %bitcast.17, f32[1,2]{1,0:T(1,128)} %refs_2_.1, f32[1,2]{1,0:T(1,128)} %refs_3_.1, f32[1,2]{1,0:T(1,128)} %refs_4_.1, f32[1,2]{1,0:T(1,128)} %refs_5_.1, s32[1,2]{1,0:T(1,128)} %refs_6_.1, ...), custom_call_target="tpu_custom_call" | custom-call | tf_op jit(solution)/shard_map/pack/pallas_call | solution.py:134
  2.5 8.7 %collective-permute-start = (f32[32,8,128]{2,1,0:T(8,128)}, f32[32,8,128]{2,1,0:T(8,128)S(1)}, u32[]{:S(2)}, u32[]{:S(2)}) collective-permute-start(f32[32,8,128]{2,1,0:T(8,128)} %get-tuple-element.14.own_ref), channel_id=1, source_target_pairs={{0,4},{4,0},{1,5},{5,1},{2,6},{6,2},{3,7},{7,3},{8,12},{12,8},{9,1... | collective-permute-start | bytes 393224 | tf_op jit(solution)/shard_map/ppermute | solution.py:608
  11.2 0.0 copy-start.2
  11.2 0.9 copy-done.2
  12.1 0.0 copy-start.3
  12.1 0.2 collective-permute-done.sib_ref
  12.4 1.9 %collective-permute-start.1 = (f32[48,8,128]{2,1,0:T(8,128)S(1)}, f32[48,8,128]{2,1,0:T(8,128)S(1)}, u32[]{:S(2)}, u32[]{:S(2)}) collective-permute-start(f32[48,8,128]{2,1,0:T(8,128)S(1)} %chip.1.own_ref), channel_id=1, source_target_pairs={{4,8},{12,16},{20,24},{28,32},{36,40},{44,48},{52,56},{60,64},{68,... | collective-permute-start | bytes 589832 | tf_op jit(solution)/shard_map/ppermute | solution.py:611
  14.3 1.3 %collective-permute-start.2 = (f32[16,8,128]{2,1,0:T(8,128)}, f32[16,8,128]{2,1,0:T(8,128)S(1)}, u32[]{:S(2)}, u32[]{:S(2)}) collective-permute-start(f32[16,8,128]{2,1,0:T(8,128)} %get-tuple-element.15), channel_id=1, source_target_pairs={{8,0},{16,8},{24,16},{32,24},{40,32},{48,40},{56,48},{64,56},{72,6... | collective-permute-start | bytes 196616 | tf_op jit(solution)/shard_map/ppermute | solution.py:609
  15.6 2.1 %collective-permute-done.2.diagonal_ref = f32[16,8,128]{2,1,0:T(8,128)S(1)} collective-permute-done((f32[16,8,128]{2,1,0:T(8,128)}, f32[16,8,128]{2,1,0:T(8,128)S(1)}, u32[]{:S(2)}, u32[]{:S(2)}) %collective-permute-start.2) | collective-permute-done | bytes 65568 | tf_op jit(solution)/shard_map/ppermute | solution.py:609
  17.7 1.7 %collective-permute-done.1.cross_ref = f32[48,8,128]{2,1,0:T(8,128)S(1)} collective-permute-done((f32[48,8,128]{2,1,0:T(8,128)S(1)}, f32[48,8,128]{2,1,0:T(8,128)S(1)}, u32[]{:S(2)}, u32[]{:S(2)}) %collective-permute-start.1) | collective-permute-done | bytes 196640 | tf_op jit(solution)/shard_map/ppermute | solution.py:611
  19.4 1.8 %march.1 = (f32[15,8,128]{2,1,0:T(8,128)}, f32[4,17,8,128]{3,2,1,0:T(8,128)}) custom-call(f32[48,8,128]{2,1,0:T(8,128)S(1)} %chip.1.own_ref, f32[32,8,128]{2,1,0:T(8,128)S(1)} %collective-permute-done.sib_ref, f32[48,8,128]{2,1,0:T(8,128)S(1)} %collective-permute-done.1.cross_ref, f32[16,8,128]{2,1,0:T(8,128)S(1)} %collective-permute-done.2.diagonal_ref), custom_call_target="tpu_custom_call" | custom-call | tf_op jit(solution)/shard_map/march/pallas_call | solution.py:302
  21.2 3.4 %all-to-all-start = ((f32[4,17,8,128]{3,2,1,0:T(8,128)}), f32[4,17,8,128]{3,2,1,0:T(8,128)S(1)}, u32[]{:S(2)}, u32[]{:S(2)}) async-start(f32[4,17,8,128]{3,2,1,0:T(8,128)} %get-tuple-element.17), calls=%async_computation | async-start | bytes 557056 | tf_op jit(solution)/shard_map/all_to_all | solution.py:615
  24.7 0.0 copy-done
  24.7 0.0 copy-done.3
  24.7 1.1 %weights.1 = (bf16[6,256,256]{2,1,0:T(8,128)(2,1)S(1)}, bf16[2,256,256]{2,1,0:T(8,128)(2,1)S(1)}, bf16[2,512,384]{2,1,0:T(8,128)(2,1)S(1)}) custom-call(f32[8,128]{1,0:T(8,128)S(1)} %copy-done.3, f32[1040,256]{1,0:T(8,128)S(1)} %copy-done), custom_call_target="tpu_custom_call" | custom-call | tf_op jit(solution)/shard_map/weights/pallas_call | solution.py:392
  25.8 4.5 %all-to-all-done.nodes_ref = f32[4,17,8,128]{3,2,1,0:T(8,128)S(1)} async-done(((f32[4,17,8,128]{3,2,1,0:T(8,128)}), f32[4,17,8,128]{3,2,1,0:T(8,128)S(1)}, u32[]{:S(2)}, u32[]{:S(2)}) %all-to-all-start) | async-done | bytes 278560 | tf_op jit(solution)/shard_map/all_to_all | solution.py:615
  30.2 2.4 %messages.1 = f32[2368,128]{1,0:T(8,128)} custom-call(f32[4,17,8,128]{3,2,1,0:T(8,128)S(1)} %all-to-all-done.nodes_ref, bf16[6,256,256]{2,1,0:T(8,128)(2,1)S(1)} %get-tuple-element.19.weight_ref, bf16[2,256,256]{2,1,0:T(8,128)(2,1)S(1)} %get-tuple-element.20.point_ref, bf16[2,512,384]{2,1,0:T(8,128)(2,1)S(1)} %get-tuple-element.21.basis_ref), custom_call_target="tpu_custom_call" | custom-call | tf_op jit(solution)/shard_map/messages/pallas_call | solution.py:445
  32.7 0.0 copy-start.1
  32.7 14.9 %all-to-all-start.1 = ((f32[64,37,1,128]{3,2,1,0:T(1,128)}), f32[64,37,1,128]{3,2,1,0:T(1,128)S(1)}, u32[]{:S(2)}, u32[]{:S(2)}) async-start(f32[64,37,1,128]{3,2,1,0:T(1,128)} %bitcast.8), calls=%async_computation.1 | async-start | bytes 2424832 | tf_op jit(solution)/shard_map/all_to_all | solution.py:617
  47.6 0.0 copy-done.1
  47.6 3.2 %collective-permute-start.3 = (f32[9,32,128]{2,1,0:T(8,128)S(1)}, f32[9,32,128]{2,1,0:T(8,128)S(1)}, u32[]{:S(2)}, u32[]{:S(2)}) collective-permute-start(f32[9,32,128]{2,1,0:T(8,128)S(1)} %bitcast.13), channel_id=1, source_target_pairs={{0,4},{4,0},{1,5},{5,1},{2,6},{6,2},{3,7},{7,3},{8,12},{12,8},{9,1... | collective-permute-start | bytes 442376 | tf_op jit(solution)/shard_map/ppermute | solution.py:621
  50.8 1.0 %collective-permute-done.3.sib_ref = f32[9,32,128]{2,1,0:T(8,128)S(1)} collective-permute-done((f32[9,32,128]{2,1,0:T(8,128)S(1)}, f32[9,32,128]{2,1,0:T(8,128)S(1)}, u32[]{:S(2)}, u32[]{:S(2)}) %collective-permute-start.3) | collective-permute-done | bytes 147488 | tf_op jit(solution)/shard_map/ppermute | solution.py:621
  51.7 0.3 rims.1
  52.0 2.2 %collective-permute-start.4 = (f32[2,32,128]{2,1,0:T(8,128)S(1)}, f32[2,32,128]{2,1,0:T(8,128)S(1)}, u32[]{:S(2)}, u32[]{:S(2)}) collective-permute-start(f32[2,32,128]{2,1,0:T(8,128)S(1)} %get-tuple-element.22), channel_id=1, source_target_pairs={{0,1},{1,2},{2,3},{3,0},{4,5},{5,6},{6,7},{7,4},{8,9},{9,10},{10,1... | collective-permute-start | bytes 98312 | tf_op jit(solution)/shard_map/ppermute | solution.py:623
  54.2 4.3 %collective-permute-start.5 = (f32[2,32,128]{2,1,0:T(8,128)S(1)}, f32[2,32,128]{2,1,0:T(8,128)S(1)}, u32[]{:S(2)}, u32[]{:S(2)}) collective-permute-start(f32[2,32,128]{2,1,0:T(8,128)S(1)} %get-tuple-element.23), channel_id=1, source_target_pairs={{1,0},{2,1},{3,2},{0,3},{5,4},{6,5},{7,6},{4,7},{9,8},{10,9},{11,1... | collective-permute-start | bytes 98312 | tf_op jit(solution)/shard_map/ppermute | solution.py:624
  58.5 0.0 collective-permute-done.4.before_ref
  58.5 1.0 %collective-permute-done.5.after_ref = f32[2,32,128]{2,1,0:T(8,128)S(1)} collective-permute-done((f32[2,32,128]{2,1,0:T(8,128)S(1)}, f32[2,32,128]{2,1,0:T(8,128)S(1)}, u32[]{:S(2)}, u32[]{:S(2)}) %collective-permute-start.5) | collective-permute-done | bytes 32800 | tf_op jit(solution)/shard_map/ppermute | solution.py:624
  59.5 18.6 %all-to-all-done.1 = f32[64,37,1,128]{3,2,1,0:T(1,128)S(1)} async-done(((f32[64,37,1,128]{3,2,1,0:T(1,128)}), f32[64,37,1,128]{3,2,1,0:T(1,128)S(1)}, u32[]{:S(2)}, u32[]{:S(2)}) %all-to-all-start.1) | async-done | bytes 1212448 | tf_op jit(solution)/shard_map/all_to_all | solution.py:617
  78.2 0.5 voxels.1.mine_ref
  78.7 5.4 %collective-permute-start.6 = (f32[4,32,128]{2,1,0:T(8,128)S(1)}, f32[4,32,128]{2,1,0:T(8,128)S(1)}, u32[]{:S(2)}, u32[]{:S(2)}) collective-permute-start(f32[4,32,128]{2,1,0:T(8,128)S(1)} %voxels.1.mine_ref), channel_id=1, source_target_pairs={{0,4},{4,0},{1,5},{5,1},{2,6},{6,2},{3,7},{7,3},{8,12},{12,8},{9,1... | collective-permute-start | bytes 196616 | tf_op jit(solution)/shard_map/ppermute | solution.py:626
  84.1 0.9 collective-permute-done.6.theirs_ref
  85.0 0.1 total.1
  85.1 3.0 %collective-permute-start.7 = (f32[8,128]{1,0:T(8,128)S(1)}, f32[8,128]{1,0:T(8,128)S(1)}, u32[]{:S(2)}, u32[]{:S(2)}) collective-permute-start(f32[8,128]{1,0:T(8,128)S(1)} %get-tuple-element.25), channel_id=1, source_target_pairs={{4,8},{12,16},{20,24},{28,32},{36,40},{44,48},{52,56},{60,64},{68,... | collective-permute-start | bytes 12296 | tf_op jit(solution)/shard_map/ppermute | solution.py:627
  88.1 1.9 %collective-permute-done.7.outer_ref = f32[8,128]{1,0:T(8,128)S(1)} collective-permute-done((f32[8,128]{1,0:T(8,128)S(1)}, f32[8,128]{1,0:T(8,128)S(1)}, u32[]{:S(2)}, u32[]{:S(2)}) %collective-permute-start.7) | collective-permute-done | bytes 4128 | tf_op jit(solution)/shard_map/ppermute | solution.py:627
  90.0 0.6 smooth.1
  (2 shorter events, 0.0 us)
Async XLA Ops:
  0.6 24.0 %copy-start = (f32[1040,256]{1,0:T(8,128)S(1)}, f32[1040,256]{1,0:T(8,128)}, u32[]{:S(2)}) copy-start(f32[1040,256]{1,0:T(8,128)} %constant.2.clone.table_ref) | copy-start | bytes 3194884
  2.5 9.9 %collective-permute-start = (f32[32,8,128]{2,1,0:T(8,128)}, f32[32,8,128]{2,1,0:T(8,128)S(1)}, u32[]{:S(2)}, u32[]{:S(2)}) collective-permute-start(f32[32,8,128]{2,1,0:T(8,128)} %get-tuple-element.14.own_ref), channel_id=1, source_target_pairs={{0,4},{4,0},{1,5},{5,1},{2,6},{6,2},{3,7},{7,3},{8,12},{12,8},{9,1... | collective-permute-start | bytes 393224 | tf_op jit(solution)/shard_map/ppermute | solution.py:608
  11.2 0.9 copy-start.2
  12.1 12.5 %copy-start.3 = (f32[8,128]{1,0:T(8,128)S(1)}, f32[8,128]{1,0:T(8,128)}, u32[]{:S(2)}) copy-start(f32[8,128]{1,0:T(8,128)} %get-tuple-element.18.points_ref) | copy-start | bytes 12292
  12.4 7.0 %collective-permute-start.1 = (f32[48,8,128]{2,1,0:T(8,128)S(1)}, f32[48,8,128]{2,1,0:T(8,128)S(1)}, u32[]{:S(2)}, u32[]{:S(2)}) collective-permute-start(f32[48,8,128]{2,1,0:T(8,128)S(1)} %chip.1.own_ref), channel_id=1, source_target_pairs={{4,8},{12,16},{20,24},{28,32},{36,40},{44,48},{52,56},{60,64},{68,... | collective-permute-start | bytes 589832 | tf_op jit(solution)/shard_map/ppermute | solution.py:611
  14.3 3.4 %collective-permute-start.2 = (f32[16,8,128]{2,1,0:T(8,128)}, f32[16,8,128]{2,1,0:T(8,128)S(1)}, u32[]{:S(2)}, u32[]{:S(2)}) collective-permute-start(f32[16,8,128]{2,1,0:T(8,128)} %get-tuple-element.15), channel_id=1, source_target_pairs={{8,0},{16,8},{24,16},{32,24},{40,32},{48,40},{56,48},{64,56},{72,6... | collective-permute-start | bytes 196616 | tf_op jit(solution)/shard_map/ppermute | solution.py:609
  21.2 9.0 %all-to-all-start = ((f32[4,17,8,128]{3,2,1,0:T(8,128)}), f32[4,17,8,128]{3,2,1,0:T(8,128)S(1)}, u32[]{:S(2)}, u32[]{:S(2)}) async-start(f32[4,17,8,128]{3,2,1,0:T(8,128)} %get-tuple-element.17), calls=%async_computation | async-start | bytes 557056 | tf_op jit(solution)/shard_map/all_to_all | solution.py:615
  32.7 14.9 %copy-start.1 = (f32[9,8,4,128]{3,2,1,0:T(4,128)S(1)}, f32[9,8,4,128]{3,2,1,0:T(4,128)}, u32[]{:S(2)}) copy-start(f32[9,8,4,128]{3,2,1,0:T(4,128)} %param.26) | copy-start | bytes 442372
  32.7 45.5 %all-to-all-start.1 = ((f32[64,37,1,128]{3,2,1,0:T(1,128)}), f32[64,37,1,128]{3,2,1,0:T(1,128)S(1)}, u32[]{:S(2)}, u32[]{:S(2)}) async-start(f32[64,37,1,128]{3,2,1,0:T(1,128)} %bitcast.8), calls=%async_computation.1 | async-start | bytes 2424832 | tf_op jit(solution)/shard_map/all_to_all | solution.py:617
  47.6 4.2 %collective-permute-start.3 = (f32[9,32,128]{2,1,0:T(8,128)S(1)}, f32[9,32,128]{2,1,0:T(8,128)S(1)}, u32[]{:S(2)}, u32[]{:S(2)}) collective-permute-start(f32[9,32,128]{2,1,0:T(8,128)S(1)} %bitcast.13), channel_id=1, source_target_pairs={{0,4},{4,0},{1,5},{5,1},{2,6},{6,2},{3,7},{7,3},{8,12},{12,8},{9,1... | collective-permute-start | bytes 442376 | tf_op jit(solution)/shard_map/ppermute | solution.py:621
  52.0 6.5 %collective-permute-start.4 = (f32[2,32,128]{2,1,0:T(8,128)S(1)}, f32[2,32,128]{2,1,0:T(8,128)S(1)}, u32[]{:S(2)}, u32[]{:S(2)}) collective-permute-start(f32[2,32,128]{2,1,0:T(8,128)S(1)} %get-tuple-element.22), channel_id=1, source_target_pairs={{0,1},{1,2},{2,3},{3,0},{4,5},{5,6},{6,7},{7,4},{8,9},{9,10},{10,1... | collective-permute-start | bytes 98312 | tf_op jit(solution)/shard_map/ppermute | solution.py:623
  54.2 5.3 %collective-permute-start.5 = (f32[2,32,128]{2,1,0:T(8,128)S(1)}, f32[2,32,128]{2,1,0:T(8,128)S(1)}, u32[]{:S(2)}, u32[]{:S(2)}) collective-permute-start(f32[2,32,128]{2,1,0:T(8,128)S(1)} %get-tuple-element.23), channel_id=1, source_target_pairs={{1,0},{2,1},{3,2},{0,3},{5,4},{6,5},{7,6},{4,7},{9,8},{10,9},{11,1... | collective-permute-start | bytes 98312 | tf_op jit(solution)/shard_map/ppermute | solution.py:624
  78.7 6.3 %collective-permute-start.6 = (f32[4,32,128]{2,1,0:T(8,128)S(1)}, f32[4,32,128]{2,1,0:T(8,128)S(1)}, u32[]{:S(2)}, u32[]{:S(2)}) collective-permute-start(f32[4,32,128]{2,1,0:T(8,128)S(1)} %voxels.1.mine_ref), channel_id=1, source_target_pairs={{0,4},{4,0},{1,5},{5,1},{2,6},{6,2},{3,7},{7,3},{8,12},{12,8},{9,1... | collective-permute-start | bytes 196616 | tf_op jit(solution)/shard_map/ppermute | solution.py:626
  85.1 4.9 %collective-permute-start.7 = (f32[8,128]{1,0:T(8,128)S(1)}, f32[8,128]{1,0:T(8,128)S(1)}, u32[]{:S(2)}, u32[]{:S(2)}) collective-permute-start(f32[8,128]{1,0:T(8,128)S(1)} %get-tuple-element.25), channel_id=1, source_target_pairs={{4,8},{12,16},{20,24},{28,32},{36,40},{44,48},{52,56},{60,64},{68,... | collective-permute-start | bytes 12296 | tf_op jit(solution)/shard_map/ppermute | solution.py:627

commit v6 on v5

--- a/solution.py
+++ b/solution.py
@@ -103,8 +103,8 @@
 
 
 def pack_kernel(*refs):
-    sources, (own_ref, near_ref, points_ref) = refs[:12], refs[12:15]
-    scratch, arrived = refs[15:27], refs[27]
+    sources, (own_ref, points_ref) = refs[:12], refs[12:14]
+    scratch, arrived = refs[14:26], refs[26]
     copies = fetch(list(zip(sources, scratch)), arrived)
     u_ref, v_ref = scratch[:2]
     element_ref, local_ref, scale_ref, owner_ref, cell_ref = scratch[7:]
@@ -120,7 +120,6 @@
         both = ref[...].astype(f32)
         own_ref[30, i:i + 1, :] = jnp.broadcast_to(both[:, 0:1], (1, 128))
         own_ref[31, i:i + 1, :] = jnp.broadcast_to(both[:, 1:2], (1, 128))
-    near_columns(near_ref, own_ref, lax.axis_index("mer_2") == 1)
     points_ref[0:2, 0:64] = local_ref[...]
     points_ref[2:3, 0:64] = (element_ref[1:2, :] % 2).astype(f32)
     points_ref[3:4, 0:64] = scale_ref[...]
@@ -134,11 +133,10 @@
     return pl.pallas_call(
         pack_kernel,
         in_specs=[hbm] * 12,
-        out_specs=(vmem, vmem, vmem),
+        out_specs=(vmem, vmem),
         scratch_shapes=[pltpu.VMEM(a.shape, a.dtype) for a in arrays] + [pltpu.SemaphoreType.DMA((12,))],
         out_shape=(
             jax.ShapeDtypeStruct((32, 8, 128), f32),
-            jax.ShapeDtypeStruct((16, 8, 128), f32),
             jax.ShapeDtypeStruct((8, 128), f32),
         ),
         name="pack",
@@ -154,14 +152,17 @@
     target[15] = jnp.where(upward, source[31], source[30])
 
 
-def stage_kernel(own_ref, out_ref):
+def stage_kernel(own_ref, out_ref, side_ref):
+    near_columns(side_ref, own_ref, lax.axis_index("mer_2") == 1)
     out_ref[0:32] = own_ref[...]
     out_ref[32:48] = jnp.zeros((16, 8, 128), jnp.float32)
 
 
 def stage(own):
     return pl.pallas_call(
-        stage_kernel, out_shape=jax.ShapeDtypeStruct((48, 8, 128), jnp.float32), compiler_params=GRANT,
+        stage_kernel, compiler_params=GRANT,
+        out_shape=(
+            jax.ShapeDtypeStruct((48, 8, 128), jnp.float32), jax.ShapeDtypeStruct((16, 8, 128), jnp.float32)),
         cost_estimate=pl.CostEstimate(flops=0, bytes_accessed=1 << 20, transcendentals=0), name="stage",
     )(own)
 
@@ -599,15 +600,16 @@
     diagonal = [(c, c - 2) for c in range(2, count, 2)] + [(c, c + 2) for c in range(1, count - 2, 2)]
     ahead = [(i, (i + 1) % az_count) for i in range(az_count)]
 
-    own, side, points = pack(
+    own, points = pack(
         displacement.reshape(15, 8, 128), velocity.reshape(15, 8, 128),
         modulus, hoop_strength, coupling, density, order_count,
         point_element.T, point_local.T, azimuth_scale.reshape(1, 64), point_owner.reshape(1, 64),
         point_cell.reshape(1, 64),
     )
     sib = lax.ppermute(own, "mer_2", swap)
+    staged, side = stage(own)
     same = lax.ppermute(side, MER, diagonal)
-    message = chip_message(stage(own), sib)
+    message = chip_message(staged, sib)
     outer = lax.ppermute(message, MER, cross)
     final, spread = march(message, sib, outer, same)
 

time: 91.2 us -> 90.9 us (level)
  no operation moved by 1% of the time
where the time goes in v6:
time: 90.9 us; the launch traced here: 90.4 us
  starting transfers between devices  48.1 us (53%)
  waiting for transfers between devices  31.9 us (35%)
  Pallas kernels  8.64 us (10%)
  local copies, waits for them, and re-layouts  0.91 us (1%)
    all_to_all x1, waiting for transfers between devices, on_device(): lax.all_to_all(outgoing.reshape(64, ROWS, 1, 128), SIDES, 0, 0, tiled=True)  18.6 us
    all_to_all x1, starting transfers between devices, on_device(): lax.all_to_all(outgoing.reshape(64, ROWS, 1, 128), SIDES, 0, 0, tiled=True)  14.7 us
    ppermute x1, starting transfers between devices, on_device(): sib = lax.ppermute(own, 'mer_2', swap)  8.75 us
    ppermute x1, starting transfers between devices, on_device(): base, edge = total(part, lax.ppermute(part, 'mer_2', swap))  5.42 us
    all_to_all x1, waiting for transfers between devices, on_device(): nodes = lax.all_to_all(spread, 'az', 0, 0, tiled=True)  4.48 us
    ppermute x1, starting transfers between devices, on_device(): after = lax.ppermute(first, 'az', [(b, a) for a, b in ahead])  4.3 us
    all_to_all x1, starting transfers between devices, on_device(): nodes = lax.all_to_all(spread, 'az', 0, 0, tiled=True)  3.45 us
    ppermute x1, starting transfers between devices, on_device(): adjoint_sib = lax.ppermute(adjoint, 'mer_2', swap)  3.19 us
  transfers between devices with their start and end apart: 10, of which 9 were waited for; matrix products, arithmetic and copies ran while one was open for 0% of the time, Pallas kernels for 1%

profile of v6, /device:TPU:1, one launch (start us, length us, event | category | flops | bytes accessed | tf_op | source)
XLA Modules:
  0.0 90.4 jit_solution(4288812964289123829)
XLA Ops:
  0.6 0.0 copy-start
  0.6 1.8 %pack.1 = (f32[32,8,128]{2,1,0:T(8,128)}, f32[8,128]{1,0:T(8,128)}) custom-call(f32[15,8,128]{2,1,0:T(8,128)} %bitcast.16, f32[15,8,128]{2,1,0:T(8,128)} %bitcast.17, f32[1,2]{1,0:T(1,128)} %refs_2_.1, f32[1,2]{1,0:T(1,128)} %refs_3_.1, f32[1,2]{1,0:T(1,128)} %refs_4_.1, f32[1,2]{1,0:T(1,128)} %refs_5_.1, s32[1,2]{1,0:T(1,128)} %refs_6_.1, ...), custom_call_target="tpu_custom_call" | custom-call | tf_op jit(solution)/shard_map/pack/pallas_call | solution.py:133
  2.4 8.7 %collective-permute-start = (f32[32,8,128]{2,1,0:T(8,128)}, f32[32,8,128]{2,1,0:T(8,128)S(1)}, u32[]{:S(2)}, u32[]{:S(2)}) collective-permute-start(f32[32,8,128]{2,1,0:T(8,128)} %get-tuple-element.15.own_ref), channel_id=1, source_target_pairs={{0,4},{4,0},{1,5},{5,1},{2,6},{6,2},{3,7},{7,3},{8,12},{12,8},{9,1... | collective-permute-start | bytes 393224 | tf_op jit(solution)/shard_map/ppermute | solution.py:609
  11.2 0.0 copy-start.2
  11.2 0.9 copy-done.2
  12.1 0.0 copy-start.3
  12.1 0.2 collective-permute-done.sib_ref
  12.4 1.9 %collective-permute-start.1 = (f32[48,8,128]{2,1,0:T(8,128)S(1)}, f32[48,8,128]{2,1,0:T(8,128)S(1)}, u32[]{:S(2)}, u32[]{:S(2)}) collective-permute-start(f32[48,8,128]{2,1,0:T(8,128)S(1)} %chip.1.own_ref), channel_id=1, source_target_pairs={{4,8},{12,16},{20,24},{28,32},{36,40},{44,48},{52,56},{60,64},{68,... | collective-permute-start | bytes 589832 | tf_op jit(solution)/shard_map/ppermute | solution.py:613
  14.3 1.3 %collective-permute-start.2 = (f32[16,8,128]{2,1,0:T(8,128)S(1)}, f32[16,8,128]{2,1,0:T(8,128)S(1)}, u32[]{:S(2)}, u32[]{:S(2)}) collective-permute-start(f32[16,8,128]{2,1,0:T(8,128)S(1)} %get-tuple-element.17), channel_id=1, source_target_pairs={{8,0},{16,8},{24,16},{32,24},{40,32},{48,40},{56,48},{64,56},{72,6... | collective-permute-start | bytes 196616 | tf_op jit(solution)/shard_map/ppermute | solution.py:611
  15.6 2.0 %collective-permute-done.2.diagonal_ref = f32[16,8,128]{2,1,0:T(8,128)S(1)} collective-permute-done((f32[16,8,128]{2,1,0:T(8,128)S(1)}, f32[16,8,128]{2,1,0:T(8,128)S(1)}, u32[]{:S(2)}, u32[]{:S(2)}) %collective-permute-start.2) | collective-permute-done | bytes 65568 | tf_op jit(solution)/shard_map/ppermute | solution.py:611
  17.6 1.8 %collective-permute-done.1.cross_ref = f32[48,8,128]{2,1,0:T(8,128)S(1)} collective-permute-done((f32[48,8,128]{2,1,0:T(8,128)S(1)}, f32[48,8,128]{2,1,0:T(8,128)S(1)}, u32[]{:S(2)}, u32[]{:S(2)}) %collective-permute-start.1) | collective-permute-done | bytes 196640 | tf_op jit(solution)/shard_map/ppermute | solution.py:613
  19.4 1.8 %march.1 = (f32[15,8,128]{2,1,0:T(8,128)}, f32[4,17,8,128]{3,2,1,0:T(8,128)}) custom-call(f32[48,8,128]{2,1,0:T(8,128)S(1)} %chip.1.own_ref, f32[32,8,128]{2,1,0:T(8,128)S(1)} %collective-permute-done.sib_ref, f32[48,8,128]{2,1,0:T(8,128)S(1)} %collective-permute-done.1.cross_ref, f32[16,8,128]{2,1,0:T(8,128)S(1)} %collective-permute-done.2.diagonal_ref), custom_call_target="tpu_custom_call" | custom-call | tf_op jit(solution)/shard_map/march/pallas_call | solution.py:303
  21.2 3.4 %all-to-all-start = ((f32[4,17,8,128]{3,2,1,0:T(8,128)}), f32[4,17,8,128]{3,2,1,0:T(8,128)S(1)}, u32[]{:S(2)}, u32[]{:S(2)}) async-start(f32[4,17,8,128]{3,2,1,0:T(8,128)} %get-tuple-element.19), calls=%async_computation | async-start | bytes 557056 | tf_op jit(solution)/shard_map/all_to_all | solution.py:617
  24.6 0.0 copy-done
  24.7 0.0 copy-done.3
  24.7 1.1 %weights.1 = (bf16[6,256,256]{2,1,0:T(8,128)(2,1)S(1)}, bf16[2,256,256]{2,1,0:T(8,128)(2,1)S(1)}, bf16[2,512,384]{2,1,0:T(8,128)(2,1)S(1)}) custom-call(f32[8,128]{1,0:T(8,128)S(1)} %copy-done.3, f32[1040,256]{1,0:T(8,128)S(1)} %copy-done), custom_call_target="tpu_custom_call" | custom-call | tf_op jit(solution)/shard_map/weights/pallas_call | solution.py:393
  25.7 4.5 %all-to-all-done.nodes_ref = f32[4,17,8,128]{3,2,1,0:T(8,128)S(1)} async-done(((f32[4,17,8,128]{3,2,1,0:T(8,128)}), f32[4,17,8,128]{3,2,1,0:T(8,128)S(1)}, u32[]{:S(2)}, u32[]{:S(2)}) %all-to-all-start) | async-done | bytes 278560 | tf_op jit(solution)/shard_map/all_to_all | solution.py:617
  30.2 2.4 %messages.1 = f32[2368,128]{1,0:T(8,128)} custom-call(f32[4,17,8,128]{3,2,1,0:T(8,128)S(1)} %all-to-all-done.nodes_ref, bf16[6,256,256]{2,1,0:T(8,128)(2,1)S(1)} %get-tuple-element.21.weight_ref, bf16[2,256,256]{2,1,0:T(8,128)(2,1)S(1)} %get-tuple-element.22.point_ref, bf16[2,512,384]{2,1,0:T(8,128)(2,1)S(1)} %get-tuple-element.23.basis_ref), custom_call_target="tpu_custom_call" | custom-call | tf_op jit(solution)/shard_map/messages/pallas_call | solution.py:446
  32.6 0.0 copy-start.1
  32.7 14.7 %all-to-all-start.1 = ((f32[64,37,1,128]{3,2,1,0:T(1,128)}), f32[64,37,1,128]{3,2,1,0:T(1,128)S(1)}, u32[]{:S(2)}, u32[]{:S(2)}) async-start(f32[64,37,1,128]{3,2,1,0:T(1,128)} %bitcast.8), calls=%async_computation.1 | async-start | bytes 2424832 | tf_op jit(solution)/shard_map/all_to_all | solution.py:619
  47.3 0.0 copy-done.1
  47.3 3.2 %collective-permute-start.3 = (f32[9,32,128]{2,1,0:T(8,128)S(1)}, f32[9,32,128]{2,1,0:T(8,128)S(1)}, u32[]{:S(2)}, u32[]{:S(2)}) collective-permute-start(f32[9,32,128]{2,1,0:T(8,128)S(1)} %bitcast.13), channel_id=1, source_target_pairs={{0,4},{4,0},{1,5},{5,1},{2,6},{6,2},{3,7},{7,3},{8,12},{12,8},{9,1... | collective-permute-start | bytes 442376 | tf_op jit(solution)/shard_map/ppermute | solution.py:623
  50.5 1.0 %collective-permute-done.3.sib_ref = f32[9,32,128]{2,1,0:T(8,128)S(1)} collective-permute-done((f32[9,32,128]{2,1,0:T(8,128)S(1)}, f32[9,32,128]{2,1,0:T(8,128)S(1)}, u32[]{:S(2)}, u32[]{:S(2)}) %collective-permute-start.3) | collective-permute-done | bytes 147488 | tf_op jit(solution)/shard_map/ppermute | solution.py:623
  51.5 0.3 rims.1
  51.8 2.2 %collective-permute-start.4 = (f32[2,32,128]{2,1,0:T(8,128)S(1)}, f32[2,32,128]{2,1,0:T(8,128)S(1)}, u32[]{:S(2)}, u32[]{:S(2)}) collective-permute-start(f32[2,32,128]{2,1,0:T(8,128)S(1)} %get-tuple-element.24), channel_id=1, source_target_pairs={{0,1},{1,2},{2,3},{3,0},{4,5},{5,6},{6,7},{7,4},{8,9},{9,10},{10,1... | collective-permute-start | bytes 98312 | tf_op jit(solution)/shard_map/ppermute | solution.py:625
  54.0 4.3 %collective-permute-start.5 = (f32[2,32,128]{2,1,0:T(8,128)S(1)}, f32[2,32,128]{2,1,0:T(8,128)S(1)}, u32[]{:S(2)}, u32[]{:S(2)}) collective-permute-start(f32[2,32,128]{2,1,0:T(8,128)S(1)} %get-tuple-element.25), channel_id=1, source_target_pairs={{1,0},{2,1},{3,2},{0,3},{5,4},{6,5},{7,6},{4,7},{9,8},{10,9},{11,1... | collective-permute-start | bytes 98312 | tf_op jit(solution)/shard_map/ppermute | solution.py:626
  58.3 0.0 collective-permute-done.4.before_ref
  58.3 1.0 %collective-permute-done.5.after_ref = f32[2,32,128]{2,1,0:T(8,128)S(1)} collective-permute-done((f32[2,32,128]{2,1,0:T(8,128)S(1)}, f32[2,32,128]{2,1,0:T(8,128)S(1)}, u32[]{:S(2)}, u32[]{:S(2)}) %collective-permute-start.5) | collective-permute-done | bytes 32800 | tf_op jit(solution)/shard_map/ppermute | solution.py:626
  59.3 18.6 %all-to-all-done.1 = f32[64,37,1,128]{3,2,1,0:T(1,128)S(1)} async-done(((f32[64,37,1,128]{3,2,1,0:T(1,128)}), f32[64,37,1,128]{3,2,1,0:T(1,128)S(1)}, u32[]{:S(2)}, u32[]{:S(2)}) %all-to-all-start.1) | async-done | bytes 1212448 | tf_op jit(solution)/shard_map/all_to_all | solution.py:619
  77.9 0.5 voxels.1.mine_ref
  78.5 5.4 %collective-permute-start.6 = (f32[4,32,128]{2,1,0:T(8,128)S(1)}, f32[4,32,128]{2,1,0:T(8,128)S(1)}, u32[]{:S(2)}, u32[]{:S(2)}) collective-permute-start(f32[4,32,128]{2,1,0:T(8,128)S(1)} %voxels.1.mine_ref), channel_id=1, source_target_pairs={{0,4},{4,0},{1,5},{5,1},{2,6},{6,2},{3,7},{7,3},{8,12},{12,8},{9,1... | collective-permute-start | bytes 196616 | tf_op jit(solution)/shard_map/ppermute | solution.py:628
  83.9 0.9 collective-permute-done.6.theirs_ref
  84.8 0.1 total.1
  84.9 3.0 %collective-permute-start.7 = (f32[8,128]{1,0:T(8,128)S(1)}, f32[8,128]{1,0:T(8,128)S(1)}, u32[]{:S(2)}, u32[]{:S(2)}) collective-permute-start(f32[8,128]{1,0:T(8,128)S(1)} %get-tuple-element.27), channel_id=1, source_target_pairs={{4,8},{12,16},{20,24},{28,32},{36,40},{44,48},{52,56},{60,64},{68,... | collective-permute-start | bytes 12296 | tf_op jit(solution)/shard_map/ppermute | solution.py:629
  87.8 2.0 %collective-permute-done.7.outer_ref = f32[8,128]{1,0:T(8,128)S(1)} collective-permute-done((f32[8,128]{1,0:T(8,128)S(1)}, f32[8,128]{1,0:T(8,128)S(1)}, u32[]{:S(2)}, u32[]{:S(2)}) %collective-permute-start.7) | collective-permute-done | bytes 4128 | tf_op jit(solution)/shard_map/ppermute | solution.py:629
  89.8 0.6 smooth.1
  (2 shorter events, 0.0 us)
Async XLA Ops:
  0.6 24.0 %copy-start = (f32[1040,256]{1,0:T(8,128)S(1)}, f32[1040,256]{1,0:T(8,128)}, u32[]{:S(2)}) copy-start(f32[1040,256]{1,0:T(8,128)} %constant.2.clone.table_ref) | copy-start | bytes 3194884
  2.4 9.9 %collective-permute-start = (f32[32,8,128]{2,1,0:T(8,128)}, f32[32,8,128]{2,1,0:T(8,128)S(1)}, u32[]{:S(2)}, u32[]{:S(2)}) collective-permute-start(f32[32,8,128]{2,1,0:T(8,128)} %get-tuple-element.15.own_ref), channel_id=1, source_target_pairs={{0,4},{4,0},{1,5},{5,1},{2,6},{6,2},{3,7},{7,3},{8,12},{12,8},{9,1... | collective-permute-start | bytes 393224 | tf_op jit(solution)/shard_map/ppermute | solution.py:609
  11.2 0.9 %copy-start.2 = (f32[32,8,128]{2,1,0:T(8,128)S(1)}, f32[32,8,128]{2,1,0:T(8,128)}, u32[]{:S(2)}) copy-start(f32[32,8,128]{2,1,0:T(8,128)} %get-tuple-element.15.own_ref) | copy-start | bytes 393220
  12.1 12.5 %copy-start.3 = (f32[8,128]{1,0:T(8,128)S(1)}, f32[8,128]{1,0:T(8,128)}, u32[]{:S(2)}) copy-start(f32[8,128]{1,0:T(8,128)} %get-tuple-element.20.points_ref) | copy-start | bytes 12292
  12.4 7.0 %collective-permute-start.1 = (f32[48,8,128]{2,1,0:T(8,128)S(1)}, f32[48,8,128]{2,1,0:T(8,128)S(1)}, u32[]{:S(2)}, u32[]{:S(2)}) collective-permute-start(f32[48,8,128]{2,1,0:T(8,128)S(1)} %chip.1.own_ref), channel_id=1, source_target_pairs={{4,8},{12,16},{20,24},{28,32},{36,40},{44,48},{52,56},{60,64},{68,... | collective-permute-start | bytes 589832 | tf_op jit(solution)/shard_map/ppermute | solution.py:613
  14.3 3.3 %collective-permute-start.2 = (f32[16,8,128]{2,1,0:T(8,128)S(1)}, f32[16,8,128]{2,1,0:T(8,128)S(1)}, u32[]{:S(2)}, u32[]{:S(2)}) collective-permute-start(f32[16,8,128]{2,1,0:T(8,128)S(1)} %get-tuple-element.17), channel_id=1, source_target_pairs={{8,0},{16,8},{24,16},{32,24},{40,32},{48,40},{56,48},{64,56},{72,6... | collective-permute-start | bytes 196616 | tf_op jit(solution)/shard_map/ppermute | solution.py:611
  21.2 9.0 %all-to-all-start = ((f32[4,17,8,128]{3,2,1,0:T(8,128)}), f32[4,17,8,128]{3,2,1,0:T(8,128)S(1)}, u32[]{:S(2)}, u32[]{:S(2)}) async-start(f32[4,17,8,128]{3,2,1,0:T(8,128)} %get-tuple-element.19), calls=%async_computation | async-start | bytes 557056 | tf_op jit(solution)/shard_map/all_to_all | solution.py:617
  32.6 14.7 %copy-start.1 = (f32[9,8,4,128]{3,2,1,0:T(4,128)S(1)}, f32[9,8,4,128]{3,2,1,0:T(4,128)}, u32[]{:S(2)}) copy-start(f32[9,8,4,128]{3,2,1,0:T(4,128)} %param.26) | copy-start | bytes 442372
  32.7 45.3 %all-to-all-start.1 = ((f32[64,37,1,128]{3,2,1,0:T(1,128)}), f32[64,37,1,128]{3,2,1,0:T(1,128)S(1)}, u32[]{:S(2)}, u32[]{:S(2)}) async-start(f32[64,37,1,128]{3,2,1,0:T(1,128)} %bitcast.8), calls=%async_computation.1 | async-start | bytes 2424832 | tf_op jit(solution)/shard_map/all_to_all | solution.py:619
  47.3 4.2 %collective-permute-start.3 = (f32[9,32,128]{2,1,0:T(8,128)S(1)}, f32[9,32,128]{2,1,0:T(8,128)S(1)}, u32[]{:S(2)}, u32[]{:S(2)}) collective-permute-start(f32[9,32,128]{2,1,0:T(8,128)S(1)} %bitcast.13), channel_id=1, source_target_pairs={{0,4},{4,0},{1,5},{5,1},{2,6},{6,2},{3,7},{7,3},{8,12},{12,8},{9,1... | collective-permute-start | bytes 442376 | tf_op jit(solution)/shard_map/ppermute | solution.py:623
  51.8 6.5 %collective-permute-start.4 = (f32[2,32,128]{2,1,0:T(8,128)S(1)}, f32[2,32,128]{2,1,0:T(8,128)S(1)}, u32[]{:S(2)}, u32[]{:S(2)}) collective-permute-start(f32[2,32,128]{2,1,0:T(8,128)S(1)} %get-tuple-element.24), channel_id=1, source_target_pairs={{0,1},{1,2},{2,3},{3,0},{4,5},{5,6},{6,7},{7,4},{8,9},{9,10},{10,1... | collective-permute-start | bytes 98312 | tf_op jit(solution)/shard_map/ppermute | solution.py:625
  54.0 5.3 %collective-permute-start.5 = (f32[2,32,128]{2,1,0:T(8,128)S(1)}, f32[2,32,128]{2,1,0:T(8,128)S(1)}, u32[]{:S(2)}, u32[]{:S(2)}) collective-permute-start(f32[2,32,128]{2,1,0:T(8,128)S(1)} %get-tuple-element.25), channel_id=1, source_target_pairs={{1,0},{2,1},{3,2},{0,3},{5,4},{6,5},{7,6},{4,7},{9,8},{10,9},{11,1... | collective-permute-start | bytes 98312 | tf_op jit(solution)/shard_map/ppermute | solution.py:626
  78.5 6.3 %collective-permute-start.6 = (f32[4,32,128]{2,1,0:T(8,128)S(1)}, f32[4,32,128]{2,1,0:T(8,128)S(1)}, u32[]{:S(2)}, u32[]{:S(2)}) collective-permute-start(f32[4,32,128]{2,1,0:T(8,128)S(1)} %voxels.1.mine_ref), channel_id=1, source_target_pairs={{0,4},{4,0},{1,5},{5,1},{2,6},{6,2},{3,7},{7,3},{8,12},{12,8},{9,1... | collective-permute-start | bytes 196616 | tf_op jit(solution)/shard_map/ppermute | solution.py:628
  84.9 4.9 %collective-permute-start.7 = (f32[8,128]{1,0:T(8,128)S(1)}, f32[8,128]{1,0:T(8,128)S(1)}, u32[]{:S(2)}, u32[]{:S(2)}) collective-permute-start(f32[8,128]{1,0:T(8,128)S(1)} %get-tuple-element.27), channel_id=1, source_target_pairs={{4,8},{12,16},{20,24},{28,32},{36,40},{44,48},{52,56},{60,64},{68,... | collective-permute-start | bytes 12296 | tf_op jit(solution)/shard_map/ppermute | solution.py:629
